TPU v7x, 128 devices: a whole 4x4x4 slice. The times are simulated.
128 devices in a mesh: row: 32 (over x, y, core), col: 4 (over z).
Axes of the slice: x: 4, y: 4, z: 4, core: 2. Of those that a mesh axis runs over, the one named last changes fastest.
Arguments:
- start_vectors: float32 [512, 32, 128], P(('row', 'col')), may hold values from -6 to 6
- blocks: bfloat16 [81920, 128, 128], P(('row', 'col')), may hold values from -0.078125 to 0.078125
- block_rows: int32 [81920], P(('row', 'col')), may hold values from 0 to 15
- block_cols: int32 [81920], P(('row', 'col')), may hold values from 0 to 127
- live_counts: int32 [128], P(('row', 'col')), may hold values from 1 to 640, as said below
- center: float32 [], replicated, may hold values from -0.5 to 0.5
- half_width: float32 [], replicated, may hold values from 1.5 to 2.5
Outputs:
- filtered: float32 [512, 32, 128], P(('row', 'col'))
Inputs may be any that keep to these rules, and one draw needn't show every extreme that they name: `live_counts`: some device has all 640 slots live.
All inputs are finite; a program needn't handle non-finite values.
Results may differ from a plain program's by a relative error of at most 0.0031.
Values may be sent and summed in bfloat16 or wider, within the bound.
No kernel may reach another device: no remote copies, remote signals or barrier semaphores. Data moves between devices by JAX's collectives and lax.ppermute only.
A program may use at most 64 MiB of HBM per device.

v0:
```python
import functools

import jax
import jax.numpy as jnp
from jax import lax
from jax.experimental import pallas as pl
from jax.experimental.pallas import tpu as pltpu
from jax.sharding import PartitionSpec as P


SIDE = 4
CORES = 2
CHUNK = 64
UNROLL = 16
GROUP = 8
BATCH = 4
MIB = 1 << 20


VMEM = pl.BlockSpec(memory_space=pltpu.VMEM)
SMEM = pl.BlockSpec(memory_space=pltpu.SMEM)


def small_call(kernel, outs, in_specs, flops=1000):
    cost = pl.CostEstimate(flops=flops, bytes_accessed=1000, transcendentals=0)
    return pl.pallas_call(
        kernel,
        out_shape=outs,
        in_specs=in_specs,
        out_specs=jax.tree.map(lambda _: VMEM, outs),
        compiler_params=pltpu.CompilerParams(vmem_limit_bytes=4 * MIB),
        cost_estimate=cost,
    )


def join_kernel(count, *refs):
    parts, out = refs[:count], refs[-1]
    size = parts[0].shape[0]
    for place, part in enumerate(parts):
        out[place * size : (place + 1) * size] = part[...]


def joined(parts, after=()):
    shape = (len(parts) * parts[0].shape[0], *parts[0].shape[1:])
    kernel = functools.partial(join_kernel, len(parts))
    specs = [VMEM] * (len(parts) + len(after))
    return small_call(kernel, jax.ShapeDtypeStruct(shape, parts[0].dtype), specs)(*parts, *after)


def round_kernel(value, out):
    out[...] = value[...].astype(out.dtype)


def rounded(value):
    return small_call(round_kernel, jax.ShapeDtypeStruct(value.shape, jnp.bfloat16), [VMEM])(value)


def chip_shifts(dx, dy, dcore=0):
    pairs = []
    for x in range(SIDE):
        for y in range(SIDE):
            for core in range(CORES):
                to = ((x + dx) % SIDE * SIDE + (y + dy) % SIDE) * CORES + (core + dcore) % CORES
                pairs.append(((x * SIDE + y) * CORES + core, to))
    return pairs


def line_gathered(owned, after=()):
    return joined([owned] + [lax.ppermute(owned, "row", chip_shifts(0, dy)) for dy in range(1, SIDE)], after)


def all_gathered(line, after=()):
    mine = joined([line] + [lax.ppermute(line, "row", chip_shifts(dx, 0)) for dx in range(1, SIDE)], after)
    theirs = lax.ppermute(mine, "row", chip_shifts(0, 0, 1))
    return joined([mine, theirs])


def padded_room(slots, span):
    step = GROUP * BATCH
    return (slots + span * (GROUP - 1) + step - 1) // step * step


def iota(shape, dim):
    return lax.broadcasted_iota(jnp.int32, shape, dim)


def plan_kernel(parts, owned, live_ref, rows_ref, cols_ref, _after, place_ref, order_ref, groups_ref, sizes_ref):
    live = live_ref[0]
    me, here = lax.axis_index("row"), lax.axis_index("col")
    rows, cols = rows_ref[...], cols_ref[...]
    slots = rows.shape[1]
    span = parts * owned
    room = order_ref.shape[1] - CHUNK
    lanes = groups_ref.shape[1]

    turned = lax.rem(lax.div(rows, owned) + (parts - here), parts) * owned + lax.rem(rows, owned)
    ids = iota((1, slots), 1)
    alive = ids < live
    hot = jnp.where((turned == iota((span, slots), 0)) & alive, 1.0, 0.0)
    earlier = jnp.where(iota((slots, slots), 0) < iota((slots, slots), 1), 1.0, 0.0).astype(jnp.bfloat16)
    rank = jnp.dot(hot.astype(jnp.bfloat16), earlier, preferred_element_type=jnp.float32)
    counts = jnp.sum(hot, axis=1, keepdims=True).astype(jnp.int32)
    padded = lax.div(counts + (GROUP - 1), GROUP) * GROUP
    row_of, lane_of = iota((span, lanes), 0), iota((span, lanes), 1)
    across = jnp.sum(jnp.where(row_of == lane_of, padded, 0).astype(jnp.float32), axis=0, keepdims=True)
    starts = jnp.sum(jnp.where(lane_of < row_of, across, 0.0), axis=1, keepdims=True)
    ends = starts.astype(jnp.int32) + padded
    place = jnp.sum(hot * (rank + starts), axis=0, keepdims=True).astype(jnp.int32)
    place = jnp.where(alive, place, room + lax.rem(ids, CHUNK))
    place_ref[...] = place

    owner = lax.div(cols, owned)
    chip, my_chip = lax.div(owner, CORES), lax.div(me, CORES)
    dx = lax.rem(lax.div(my_chip, SIDE) + SIDE - lax.div(chip, SIDE), SIDE)
    dy = lax.rem(lax.rem(my_chip, SIDE) + SIDE - lax.rem(chip, SIDE), SIDE)
    dcore = lax.rem(me + owner, CORES)
    source = ((dcore * SIDE + dx) * SIDE + dy) * owned + lax.rem(cols, owned)
    weights = jnp.broadcast_to(jnp.where(alive, source, 0).astype(jnp.float32), (8, slots)).astype(jnp.bfloat16)
    for block in range((room + CHUNK) // CHUNK):
        match = jnp.where(place == iota((CHUNK, slots), 0) + block * CHUNK, 1.0, 0.0).astype(jnp.bfloat16)
        found = lax.dot_general(weights, match, (((1,), (1,)), ((), ())), preferred_element_type=jnp.float32)
        order_ref[:, block * CHUNK : (block + 1) * CHUNK] = found[:1].astype(jnp.int32)

    ended = jnp.where(ends <= lane_of * GROUP, 1.0, 0.0)
    groups_ref[...] = jnp.sum(ended, axis=0, keepdims=True).astype(jnp.int32)
    total = jnp.sum(padded.astype(jnp.float32), axis=0, keepdims=True).astype(jnp.int32)
    at_ends = jnp.sum(jnp.where(row_of == lane_of, ends, 0).astype(jnp.float32), axis=0, keepdims=True).astype(jnp.int32)
    lane = iota((1, lanes), 1)
    batches = lax.div(total + (GROUP * BATCH - 1), GROUP * BATCH)
    sizes = jnp.where(lane == span, lax.div(live + (CHUNK - 1), CHUNK), at_ends)
    sizes = jnp.where(lane == span + 1, batches, sizes)
    sizes_ref[...] = jnp.where(lane == span + 2, total, sizes)


def sort_plan(rows, cols, live, after, parts, owned):
    slots = rows.shape[0]
    room = padded_room(slots, parts * owned)
    widths = (slots, room + CHUNK, 128, 128)
    return pl.pallas_call(
        functools.partial(plan_kernel, parts, owned),
        out_shape=[jax.ShapeDtypeStruct((1, width), jnp.int32) for width in widths],
        in_specs=[SMEM, VMEM, VMEM, VMEM],
        out_specs=[VMEM] * len(widths),
        compiler_params=pltpu.CompilerParams(vmem_limit_bytes=8 * MIB),
        cost_estimate=pl.CostEstimate(flops=1000, bytes_accessed=1000, transcendentals=0),
    )(live, rows.reshape(1, slots), cols.reshape(1, slots), after)


def prepare_kernel(span, place, sizes, _center, _half, _after, blocks_hbm, store, raw, sems):
    chunks = sizes[0, span]
    total = sizes[0, span + 2]
    room = store.shape[0] - CHUNK
    size = raw.shape[1]

    def copy_of(c):
        part = pl.ds(c * CHUNK, CHUNK)
        return pltpu.make_async_copy(blocks_hbm.at[part], raw.at[part], sems.at[c])

    @pl.loop(0, chunks)
    def _(c):
        copy_of(c).start()

    nothing = jnp.zeros((GROUP, size, size), store.dtype)

    @pl.loop(0, span)
    def _(row):
        store[pl.ds(jnp.maximum(sizes[0, row] - GROUP, 0), GROUP)] = nothing

    @pl.loop(0, BATCH)
    def _(k):
        @pl.when(total + k * GROUP < room)
        def _():
            store[pl.ds(total + k * GROUP, GROUP)] = nothing

    @pl.loop(0, chunks)
    def _(c):
        copy_of(c).wait()

        @pl.loop(0, CHUNK // UNROLL)
        def _(g):
            for u in range(UNROLL):
                slot = c * CHUNK + g * UNROLL + u
                store[place[0, slot]] = raw[slot].T


def prepared(place, sizes, blocks, scalars, after, span):
    slots, size, _ = blocks.shape
    return pl.pallas_call(
        functools.partial(prepare_kernel, span),
        out_shape=pltpu.VMEM((padded_room(slots, span) + CHUNK, size, size), blocks.dtype),
        in_specs=[SMEM] * 4 + [VMEM, pl.BlockSpec(memory_space=pl.ANY)],
        out_specs=VMEM,
        scratch_shapes=[
            pltpu.VMEM((slots, size, size), blocks.dtype),
            pltpu.SemaphoreType.DMA((slots // CHUNK,)),
        ],
        compiler_params=pltpu.CompilerParams(vmem_limit_bytes=24 * MIB),
        cost_estimate=pl.CostEstimate(flops=1000, bytes_accessed=2 * slots * size * size, transcendentals=0),
    )(place, sizes, *scalars, after, blocks)


def products_kernel(first_row, order, groups, sizes, vec, store, *refs):
    out, sums = refs[-2:]
    owned = out.shape[0]
    size = store.shape[1]
    start = lax.div(sizes[0, first_row - 1], GROUP) if first_row else 0
    count = lax.div(sizes[0, first_row + owned - 1], GROUP) - start
    sums[...] = jnp.zeros_like(sums)

    @pl.loop(0, lax.div(count + (BATCH - 1), BATCH))
    def _(batch):
        for k in range(BATCH):
            group = start + batch * BATCH + k
            left = jnp.concatenate([vec[order[0, group * GROUP + i]] for i in range(GROUP)], axis=1)
            right = store[pl.ds(group * GROUP, GROUP)].reshape(GROUP * size, size)
            sums[groups[0, group]] += jnp.dot(left, right, preferred_element_type=jnp.float32)

    out[...] = sums[first_row : first_row + owned]


def local_products(part, vec, prep, after, owned, parts):
    order, groups, sizes, store = prep
    _, vecs, size = vec.shape
    return pl.pallas_call(
        functools.partial(products_kernel, part * owned),
        out_shape=jax.ShapeDtypeStruct((owned, vecs, size), jnp.float32),
        in_specs=[SMEM] * 3 + [VMEM] * (2 + len(after)),
        out_specs=VMEM,
        scratch_shapes=[pltpu.VMEM((owned * parts + 1, vecs, size), jnp.float32)],
        compiler_params=pltpu.CompilerParams(vmem_limit_bytes=4 * MIB),
        cost_estimate=pl.CostEstimate(flops=640 // 2 * vecs * size * size, bytes_accessed=MIB, transcendentals=0),
    )(order, groups, sizes, vec, kept(store), *after)


def kept(store):
    return pltpu.with_memory_space_constraint(store, pltpu.VMEM)


def first_kernel(center, half_width, current, *refs):
    pieces, (out, out_bf) = refs[:-2], refs[-2:]
    image = pieces[0][...]
    for piece in pieces[1:]:
        image += piece[...]
    value = (image - center[0] * current[...]) / half_width[0]
    out[...] = value
    out_bf[...] = value.astype(out_bf.dtype)


def next_kernel(center, half_width, current, previous, *refs):
    pieces, (out, out_bf) = refs[:-2], refs[-2:]
    image = pieces[0][...]
    for piece in pieces[1:]:
        image += piece[...]
    value = 2.0 * (image - center[0] * current[...]) / half_width[0] - previous[...]
    out[...] = value
    out_bf[...] = value.astype(out_bf.dtype)


def on_device(start_vectors, blocks, block_rows, block_cols, live_counts, center, half_width):
    parts = lax.axis_size("col")
    owned = start_vectors.shape[0]
    shape = start_vectors.shape
    scalars = (center.reshape(1), half_width.reshape(1))
    outs = (jax.ShapeDtypeStruct(shape, jnp.float32), jax.ShapeDtypeStruct(shape, jnp.bfloat16))

    def image_pieces(vec):
        pieces, last = [], ()
        for part in (*range(1, parts), 0):
            piece = local_products(part, vec, prep, last, owned, parts)
            last = (piece,)
            if part:
                piece = lax.ppermute(piece, "col", [(i, (i + part) % parts) for i in range(parts)])
            pieces.append(piece)
        return pieces

    start_bf = rounded(start_vectors)
    place, order, groups, sizes = sort_plan(block_rows, block_cols, live_counts, start_bf, parts, owned)
    line = line_gathered(start_bf, (sizes,))
    store = prepared(place, sizes, blocks, scalars, line, parts * owned)
    prep = (order, groups, sizes, store)
    pieces = image_pieces(all_gathered(line, (kept(store),)))
    first = small_call(first_kernel, outs, [SMEM, SMEM] + [VMEM] * (1 + parts))
    current, current_bf = first(*scalars, start_vectors, *pieces)
    previous = start_vectors
    for _ in range(2):
        pieces = image_pieces(all_gathered(line_gathered(current_bf)))
        step = small_call(next_kernel, outs, [SMEM, SMEM] + [VMEM] * (2 + parts))
        following, current_bf = step(*scalars, current, previous, *pieces)
        previous, current = current, following
    return current


def solution(mesh):
    return jax.shard_map(
        on_device,
        mesh=mesh,
        in_specs=(
            P(("row", "col"), None, None),
            P(("row", "col"), None, None),
            P(("row", "col")),
            P(("row", "col")),
            P(("row", "col")),
            P(),
            P(),
        ),
        out_specs=P(("row", "col"), None, None),
        check_vma=False,
    )
```

profile of v0, /device:TPU:1, one launch (start us, length us, event | category | flops | bytes accessed | tf_op | source)
XLA Modules:
  0.0 107.4 jit_solution(17359714273393522792)
XLA Ops:
  0.8 3.6 %collective-permute-start.2 = (bf16[4,32,128]{2,1,0:T(8,128)(2,1)S(1)}, bf16[4,32,128]{2,1,0:T(8,128)(2,1)S(1)}, u32[]{:S(2)}, u32[]{:S(2)}) collective-permute-start(bf16[4,32,128]{2,1,0:T(8,128)(2,1)S(1)} %shard_map.73._after.refs_0_), channel_id=1, source_target_pairs={{0,24},{4,28},{8,0},{12,4},{16,8},{20,12},{24,16},{28,20},{32,56},... | collective-permute-start | bytes 98312 | tf_op jit(solution)/shard_map/ppermute | solution.py:69
  9.0 2.5 %collective-permute-start.5 = (bf16[16,32,128]{2,1,0:T(8,128)(2,1)S(1)}, bf16[16,32,128]{2,1,0:T(8,128)(2,1)S(1)}, u32[]{:S(2)}, u32[]{:S(2)}) collective-permute-start(bf16[16,32,128]{2,1,0:T(8,128)(2,1)S(1)} %shard_map.75._after.refs_0_), channel_id=1, source_target_pairs={{0,96},{4,100},{8,104},{12,108},{16,112},{20,116},{24,120},{28,124... | collective-permute-start | bytes 393224 | tf_op jit(solution)/shard_map/ppermute | solution.py:73
  14.0 6.1 %shard_map.76.refs_4_.store = bf16[832,128,128]{2,1,0:T(8,128)(2,1)S(1)} custom-call(s32[1,640]{1,0:T(1,128)S(1)} %get-tuple-element.17.place, s32[1,128]{1,0:T(1,128)S(1)} %get-tuple-element.16.refs_4_.sizes, f32[1]{0:T(128)} %bitcast.2._center, f32[1]{0:T(128)} %bitcast.6._half, bf16[16,32,128]{2,1,0:T(8,128)(2,1)S(1)} %shard_map.75._after.refs_0_, ...), custom_call_target="tpu_custom_call" | custom-call | flops 1000 | bytes 20971520 | tf_op jit(solution)/shard_map/pallas_call | solution.py:188
  20.2 1.7 %collective-permute-start.6 = (bf16[64,32,128]{2,1,0:T(8,128)(2,1)S(1)}, bf16[64,32,128]{2,1,0:T(8,128)(2,1)S(1)}, u32[]{:S(2)}, u32[]{:S(2)}) collective-permute-start(bf16[64,32,128]{2,1,0:T(8,128)(2,1)S(1)} %shard_map.77.refs_0_), channel_id=1, source_target_pairs={{0,4},{4,0},{8,12},{12,8},{16,20},{20,16},{24,28},{28,24},{32,36},... | collective-permute-start | bytes 1572872 | tf_op jit(solution)/shard_map/ppermute | solution.py:74
  22.0 1.5 %collective-permute-done.6.refs_1_ = bf16[64,32,128]{2,1,0:T(8,128)(2,1)S(1)} collective-permute-done((bf16[64,32,128]{2,1,0:T(8,128)(2,1)S(1)}, bf16[64,32,128]{2,1,0:T(8,128)(2,1)S(1)}, u32[]{:S(2)}, u32[]{:S(2)}) %collective-permute-start.6) | collective-permute-done | bytes 524320 | tf_op jit(solution)/shard_map/ppermute | solution.py:74
  23.6 1.5 %shard_map.79.refs_0_ = f32[4,32,128]{2,1,0:T(8,128)S(1)} custom-call(s32[1,832]{1,0:T(1,128)S(1)} %get-tuple-element.14.order, s32[1,128]{1,0:T(1,128)S(1)} %get-tuple-element.15.groups, s32[1,128]{1,0:T(1,128)S(1)} %get-tuple-element.16.refs_4_.sizes, bf16[128,32,128]{2,1,0:T(8,128)(2,1)S(1)} %shard_map.78.vec, ...), custom_call_target="tpu_custom_call" | custom-call | flops 167772160 | bytes 1048576 | tf_op jit(solution)/shard_map/pallas_call | solution.py:224
  25.1 1.5 %shard_map.80.refs_0_ = f32[4,32,128]{2,1,0:T(8,128)S(1)} custom-call(s32[1,832]{1,0:T(1,128)S(1)} %get-tuple-element.14.order, s32[1,128]{1,0:T(1,128)S(1)} %get-tuple-element.15.groups, s32[1,128]{1,0:T(1,128)S(1)} %get-tuple-element.16.refs_4_.sizes, bf16[128,32,128]{2,1,0:T(8,128)(2,1)S(1)} %shard_map.78.vec, ...), custom_call_target="tpu_custom_call" | custom-call | flops 167772160 | bytes 1048576 | tf_op jit(solution)/shard_map/pallas_call | solution.py:224
  26.6 1.5 %shard_map.81.refs_0_ = f32[4,32,128]{2,1,0:T(8,128)S(1)} custom-call(s32[1,832]{1,0:T(1,128)S(1)} %get-tuple-element.14.order, s32[1,128]{1,0:T(1,128)S(1)} %get-tuple-element.15.groups, s32[1,128]{1,0:T(1,128)S(1)} %get-tuple-element.16.refs_4_.sizes, bf16[128,32,128]{2,1,0:T(8,128)(2,1)S(1)} %shard_map.78.vec, ...), custom_call_target="tpu_custom_call" | custom-call | flops 167772160 | bytes 1048576 | tf_op jit(solution)/shard_map/pallas_call | solution.py:224
  28.2 2.0 %collective-permute-start.9 = (f32[4,32,128]{2,1,0:T(8,128)S(1)}, f32[4,32,128]{2,1,0:T(8,128)S(1)}, u32[]{:S(2)}, u32[]{:S(2)}) collective-permute-start(f32[4,32,128]{2,1,0:T(8,128)S(1)} %shard_map.81.refs_0_), channel_id=1, source_target_pairs={{0,3},{1,0},{2,1},{3,2},{4,7},{5,4},{6,5},{7,6},{8,11},{9,8},{10,9... | collective-permute-start | bytes 196616 | tf_op jit(solution)/shard_map/ppermute | solution.py:272
  30.2 4.0 %collective-permute-start.8 = (f32[4,32,128]{2,1,0:T(8,128)S(1)}, f32[4,32,128]{2,1,0:T(8,128)S(1)}, u32[]{:S(2)}, u32[]{:S(2)}) collective-permute-start(f32[4,32,128]{2,1,0:T(8,128)S(1)} %shard_map.80.refs_0_), channel_id=1, source_target_pairs={{0,2},{1,3},{2,0},{3,1},{4,6},{5,7},{6,4},{7,5},{8,10},{9,11},{10,... | collective-permute-start | bytes 196616 | tf_op jit(solution)/shard_map/ppermute | solution.py:272
  36.5 2.0 %collective-permute-done.7.refs_0_ = f32[4,32,128]{2,1,0:T(8,128)S(1)} collective-permute-done((f32[4,32,128]{2,1,0:T(8,128)S(1)}, f32[4,32,128]{2,1,0:T(8,128)S(1)}, u32[]{:S(2)}, u32[]{:S(2)}) %collective-permute-start.7) | collective-permute-done | bytes 65568 | tf_op jit(solution)/shard_map/ppermute | solution.py:272
  38.6 2.2 %collective-permute-start.12 = (bf16[4,32,128]{2,1,0:T(8,128)(2,1)S(1)}, bf16[4,32,128]{2,1,0:T(8,128)(2,1)S(1)}, u32[]{:S(2)}, u32[]{:S(2)}) collective-permute-start(bf16[4,32,128]{2,1,0:T(8,128)(2,1)S(1)} %get-tuple-element.19.refs_0_), channel_id=1, source_target_pairs={{0,24},{4,28},{8,0},{12,4},{16,8},{20,12},{24,16},{28,20},{32,56},... | collective-permute-start | bytes 98312 | tf_op jit(solution)/shard_map/ppermute | solution.py:69
  41.8 3.3 %collective-permute-done.11.refs_2_ = bf16[4,32,128]{2,1,0:T(8,128)(2,1)S(1)} collective-permute-done((bf16[4,32,128]{2,1,0:T(8,128)(2,1)S(1)}, bf16[4,32,128]{2,1,0:T(8,128)(2,1)S(1)}, u32[]{:S(2)}, u32[]{:S(2)}) %collective-permute-start.11) | collective-permute-done | bytes 32800 | tf_op jit(solution)/shard_map/ppermute | solution.py:69
  45.1 3.3 %collective-permute-start.15 = (bf16[16,32,128]{2,1,0:T(8,128)(2,1)S(1)}, bf16[16,32,128]{2,1,0:T(8,128)(2,1)S(1)}, u32[]{:S(2)}, u32[]{:S(2)}) collective-permute-start(bf16[16,32,128]{2,1,0:T(8,128)(2,1)S(1)} %shard_map.84.refs_0_), channel_id=1, source_target_pairs={{0,96},{4,100},{8,104},{12,108},{16,112},{20,116},{24,120},{28,124... | collective-permute-start | bytes 393224 | tf_op jit(solution)/shard_map/ppermute | solution.py:73
  49.3 2.4 %collective-permute-done.15.refs_3_ = bf16[16,32,128]{2,1,0:T(8,128)(2,1)S(1)} collective-permute-done((bf16[16,32,128]{2,1,0:T(8,128)(2,1)S(1)}, bf16[16,32,128]{2,1,0:T(8,128)(2,1)S(1)}, u32[]{:S(2)}, u32[]{:S(2)}) %collective-permute-start.15) | collective-permute-done | bytes 131104 | tf_op jit(solution)/shard_map/ppermute | solution.py:73
  51.8 2.1 %collective-permute-done.14.refs_2_ = bf16[16,32,128]{2,1,0:T(8,128)(2,1)S(1)} collective-permute-done((bf16[16,32,128]{2,1,0:T(8,128)(2,1)S(1)}, bf16[16,32,128]{2,1,0:T(8,128)(2,1)S(1)}, u32[]{:S(2)}, u32[]{:S(2)}) %collective-permute-start.14) | collective-permute-done | bytes 131104 | tf_op jit(solution)/shard_map/ppermute | solution.py:73
  55.2 7.0 %collective-permute-start.16 = (bf16[64,32,128]{2,1,0:T(8,128)(2,1)S(1)}, bf16[64,32,128]{2,1,0:T(8,128)(2,1)S(1)}, u32[]{:S(2)}, u32[]{:S(2)}) collective-permute-start(bf16[64,32,128]{2,1,0:T(8,128)(2,1)S(1)} %shard_map.85.refs_0_), channel_id=1, source_target_pairs={{0,4},{4,0},{8,12},{12,8},{16,20},{20,16},{24,28},{28,24},{32,36},... | collective-permute-start | bytes 1572872 | tf_op jit(solution)/shard_map/ppermute | solution.py:74
  62.2 1.5 %collective-permute-done.16.refs_1_ = bf16[64,32,128]{2,1,0:T(8,128)(2,1)S(1)} collective-permute-done((bf16[64,32,128]{2,1,0:T(8,128)(2,1)S(1)}, bf16[64,32,128]{2,1,0:T(8,128)(2,1)S(1)}, u32[]{:S(2)}, u32[]{:S(2)}) %collective-permute-start.16) | collective-permute-done | bytes 524320 | tf_op jit(solution)/shard_map/ppermute | solution.py:74
  63.8 1.5 %shard_map.87.refs_0_ = f32[4,32,128]{2,1,0:T(8,128)S(1)} custom-call(s32[1,832]{1,0:T(1,128)S(1)} %get-tuple-element.14.order, s32[1,128]{1,0:T(1,128)S(1)} %get-tuple-element.15.groups, s32[1,128]{1,0:T(1,128)S(1)} %get-tuple-element.16.refs_4_.sizes, bf16[128,32,128]{2,1,0:T(8,128)(2,1)S(1)} %shard_map.86.vec, ...), custom_call_target="tpu_custom_call" | custom-call | flops 167772160 | bytes 1048576 | tf_op jit(solution)/shard_map/pallas_call | solution.py:224
  65.4 1.5 %shard_map.88.refs_0_ = f32[4,32,128]{2,1,0:T(8,128)S(1)} custom-call(s32[1,832]{1,0:T(1,128)S(1)} %get-tuple-element.14.order, s32[1,128]{1,0:T(1,128)S(1)} %get-tuple-element.15.groups, s32[1,128]{1,0:T(1,128)S(1)} %get-tuple-element.16.refs_4_.sizes, bf16[128,32,128]{2,1,0:T(8,128)(2,1)S(1)} %shard_map.86.vec, ...), custom_call_target="tpu_custom_call" | custom-call | flops 167772160 | bytes 1048576 | tf_op jit(solution)/shard_map/pallas_call | solution.py:224
  66.9 1.5 %shard_map.89.refs_0_ = f32[4,32,128]{2,1,0:T(8,128)S(1)} custom-call(s32[1,832]{1,0:T(1,128)S(1)} %get-tuple-element.14.order, s32[1,128]{1,0:T(1,128)S(1)} %get-tuple-element.15.groups, s32[1,128]{1,0:T(1,128)S(1)} %get-tuple-element.16.refs_4_.sizes, bf16[128,32,128]{2,1,0:T(8,128)(2,1)S(1)} %shard_map.86.vec, ...), custom_call_target="tpu_custom_call" | custom-call | flops 167772160 | bytes 1048576 | tf_op jit(solution)/shard_map/pallas_call | solution.py:224
  68.5 2.5 %collective-permute-start.18 = (f32[4,32,128]{2,1,0:T(8,128)S(1)}, f32[4,32,128]{2,1,0:T(8,128)S(1)}, u32[]{:S(2)}, u32[]{:S(2)}) collective-permute-start(f32[4,32,128]{2,1,0:T(8,128)S(1)} %shard_map.88.refs_0_), channel_id=1, source_target_pairs={{0,2},{1,3},{2,0},{3,1},{4,6},{5,7},{6,4},{7,5},{8,10},{9,11},{10,... | collective-permute-start | bytes 196616 | tf_op jit(solution)/shard_map/ppermute | solution.py:272
  73.2 2.1 %collective-permute-done.17.refs_0_ = f32[4,32,128]{2,1,0:T(8,128)S(1)} collective-permute-done((f32[4,32,128]{2,1,0:T(8,128)S(1)}, f32[4,32,128]{2,1,0:T(8,128)S(1)}, u32[]{:S(2)}, u32[]{:S(2)}) %collective-permute-start.17) | collective-permute-done | bytes 65568 | tf_op jit(solution)/shard_map/ppermute | solution.py:272
  80.6 1.7 %collective-permute-start.25 = (bf16[16,32,128]{2,1,0:T(8,128)(2,1)S(1)}, bf16[16,32,128]{2,1,0:T(8,128)(2,1)S(1)}, u32[]{:S(2)}, u32[]{:S(2)}) collective-permute-start(bf16[16,32,128]{2,1,0:T(8,128)(2,1)S(1)} %shard_map.92.refs_0_), channel_id=1, source_target_pairs={{0,96},{4,100},{8,104},{12,108},{16,112},{20,116},{24,120},{28,124... | collective-permute-start | bytes 393224 | tf_op jit(solution)/shard_map/ppermute | solution.py:73
  83.7 1.9 %collective-permute-done.25.refs_3_ = bf16[16,32,128]{2,1,0:T(8,128)(2,1)S(1)} collective-permute-done((bf16[16,32,128]{2,1,0:T(8,128)(2,1)S(1)}, bf16[16,32,128]{2,1,0:T(8,128)(2,1)S(1)}, u32[]{:S(2)}, u32[]{:S(2)}) %collective-permute-start.25) | collective-permute-done | bytes 131104 | tf_op jit(solution)/shard_map/ppermute | solution.py:73
  85.6 2.0 %collective-permute-done.24.refs_2_ = bf16[16,32,128]{2,1,0:T(8,128)(2,1)S(1)} collective-permute-done((bf16[16,32,128]{2,1,0:T(8,128)(2,1)S(1)}, bf16[16,32,128]{2,1,0:T(8,128)(2,1)S(1)}, u32[]{:S(2)}, u32[]{:S(2)}) %collective-permute-start.24) | collective-permute-done | bytes 131104 | tf_op jit(solution)/shard_map/ppermute | solution.py:73
  89.1 4.4 %collective-permute-start.26 = (bf16[64,32,128]{2,1,0:T(8,128)(2,1)S(1)}, bf16[64,32,128]{2,1,0:T(8,128)(2,1)S(1)}, u32[]{:S(2)}, u32[]{:S(2)}) collective-permute-start(bf16[64,32,128]{2,1,0:T(8,128)(2,1)S(1)} %shard_map.93.refs_0_), channel_id=1, source_target_pairs={{0,4},{4,0},{8,12},{12,8},{16,20},{20,16},{24,28},{28,24},{32,36},... | collective-permute-start | bytes 1572872 | tf_op jit(solution)/shard_map/ppermute | solution.py:74
  93.5 1.5 %collective-permute-done.26.refs_1_ = bf16[64,32,128]{2,1,0:T(8,128)(2,1)S(1)} collective-permute-done((bf16[64,32,128]{2,1,0:T(8,128)(2,1)S(1)}, bf16[64,32,128]{2,1,0:T(8,128)(2,1)S(1)}, u32[]{:S(2)}, u32[]{:S(2)}) %collective-permute-start.26) | collective-permute-done | bytes 524320 | tf_op jit(solution)/shard_map/ppermute | solution.py:74
  95.1 1.5 %shard_map.95.refs_0_ = f32[4,32,128]{2,1,0:T(8,128)S(1)} custom-call(s32[1,832]{1,0:T(1,128)S(1)} %get-tuple-element.14.order, s32[1,128]{1,0:T(1,128)S(1)} %get-tuple-element.15.groups, s32[1,128]{1,0:T(1,128)S(1)} %get-tuple-element.16.refs_4_.sizes, bf16[128,32,128]{2,1,0:T(8,128)(2,1)S(1)} %shard_map.94.vec, ...), custom_call_target="tpu_custom_call" | custom-call | flops 167772160 | bytes 1048576 | tf_op jit(solution)/shard_map/pallas_call | solution.py:224
  98.1 1.5 %shard_map.97.refs_0_ = f32[4,32,128]{2,1,0:T(8,128)S(1)} custom-call(s32[1,832]{1,0:T(1,128)S(1)} %get-tuple-element.14.order, s32[1,128]{1,0:T(1,128)S(1)} %get-tuple-element.15.groups, s32[1,128]{1,0:T(1,128)S(1)} %get-tuple-element.16.refs_4_.sizes, bf16[128,32,128]{2,1,0:T(8,128)(2,1)S(1)} %shard_map.94.vec, ...), custom_call_target="tpu_custom_call" | custom-call | flops 167772160 | bytes 1048576 | tf_op jit(solution)/shard_map/pallas_call | solution.py:224
  99.8 2.7 %collective-permute-start.28 = (f32[4,32,128]{2,1,0:T(8,128)S(1)}, f32[4,32,128]{2,1,0:T(8,128)S(1)}, u32[]{:S(2)}, u32[]{:S(2)}) collective-permute-start(f32[4,32,128]{2,1,0:T(8,128)S(1)} %shard_map.96.refs_0_), channel_id=1, source_target_pairs={{0,2},{1,3},{2,0},{3,1},{4,6},{5,7},{6,4},{7,5},{8,10},{9,11},{10,... | collective-permute-start | bytes 196616 | tf_op jit(solution)/shard_map/ppermute | solution.py:272
  104.5 2.3 %collective-permute-done.27.refs_0_ = f32[4,32,128]{2,1,0:T(8,128)S(1)} collective-permute-done((f32[4,32,128]{2,1,0:T(8,128)S(1)}, f32[4,32,128]{2,1,0:T(8,128)S(1)}, u32[]{:S(2)}, u32[]{:S(2)}) %collective-permute-start.27) | collective-permute-done | bytes 65568 | tf_op jit(solution)/shard_map/ppermute | solution.py:272
  (61 shorter events, 26.4 us)
Async XLA Ops:
  0.0 0.8 copy-start
  0.8 7.3 %collective-permute-start.2 = (bf16[4,32,128]{2,1,0:T(8,128)(2,1)S(1)}, bf16[4,32,128]{2,1,0:T(8,128)(2,1)S(1)}, u32[]{:S(2)}, u32[]{:S(2)}) collective-permute-start(bf16[4,32,128]{2,1,0:T(8,128)(2,1)S(1)} %shard_map.73._after.refs_0_), channel_id=1, source_target_pairs={{0,24},{4,28},{8,0},{12,4},{16,8},{20,12},{24,16},{28,20},{32,56},... | collective-permute-start | bytes 98312 | tf_op jit(solution)/shard_map/ppermute | solution.py:69
  4.4 4.3 %collective-permute-start.1 = (bf16[4,32,128]{2,1,0:T(8,128)(2,1)S(1)}, bf16[4,32,128]{2,1,0:T(8,128)(2,1)S(1)}, u32[]{:S(2)}, u32[]{:S(2)}) collective-permute-start(bf16[4,32,128]{2,1,0:T(8,128)(2,1)S(1)} %shard_map.73._after.refs_0_), channel_id=1, source_target_pairs={{0,16},{4,20},{8,24},{12,28},{16,0},{20,4},{24,8},{28,12},{32,48},... | collective-permute-start | bytes 98312 | tf_op jit(solution)/shard_map/ppermute | solution.py:69
  4.7 4.3 %collective-permute-start = (bf16[4,32,128]{2,1,0:T(8,128)(2,1)S(1)}, bf16[4,32,128]{2,1,0:T(8,128)(2,1)S(1)}, u32[]{:S(2)}, u32[]{:S(2)}) collective-permute-start(bf16[4,32,128]{2,1,0:T(8,128)(2,1)S(1)} %shard_map.73._after.refs_0_), channel_id=1, source_target_pairs={{0,8},{4,12},{8,16},{12,20},{16,24},{20,28},{24,0},{28,4},{32,40},... | collective-permute-start | bytes 98312 | tf_op jit(solution)/shard_map/ppermute | solution.py:69
  9.0 11.1 %collective-permute-start.5 = (bf16[16,32,128]{2,1,0:T(8,128)(2,1)S(1)}, bf16[16,32,128]{2,1,0:T(8,128)(2,1)S(1)}, u32[]{:S(2)}, u32[]{:S(2)}) collective-permute-start(bf16[16,32,128]{2,1,0:T(8,128)(2,1)S(1)} %shard_map.75._after.refs_0_), channel_id=1, source_target_pairs={{0,96},{4,100},{8,104},{12,108},{16,112},{20,116},{24,120},{28,124... | collective-permute-start | bytes 393224 | tf_op jit(solution)/shard_map/ppermute | solution.py:73
  11.6 8.6 %collective-permute-start.4 = (bf16[16,32,128]{2,1,0:T(8,128)(2,1)S(1)}, bf16[16,32,128]{2,1,0:T(8,128)(2,1)S(1)}, u32[]{:S(2)}, u32[]{:S(2)}) collective-permute-start(bf16[16,32,128]{2,1,0:T(8,128)(2,1)S(1)} %shard_map.75._after.refs_0_), channel_id=1, source_target_pairs={{0,64},{4,68},{8,72},{12,76},{16,80},{20,84},{24,88},{28,92},{32,9... | collective-permute-start | bytes 393224 | tf_op jit(solution)/shard_map/ppermute | solution.py:73
  12.1 8.1 %collective-permute-start.3 = (bf16[16,32,128]{2,1,0:T(8,128)(2,1)S(1)}, bf16[16,32,128]{2,1,0:T(8,128)(2,1)S(1)}, u32[]{:S(2)}, u32[]{:S(2)}) collective-permute-start(bf16[16,32,128]{2,1,0:T(8,128)(2,1)S(1)} %shard_map.75._after.refs_0_), channel_id=1, source_target_pairs={{0,32},{4,36},{8,40},{12,44},{16,48},{20,52},{24,56},{28,60},{32,6... | collective-permute-start | bytes 393224 | tf_op jit(solution)/shard_map/ppermute | solution.py:73
  20.2 3.3 %collective-permute-start.6 = (bf16[64,32,128]{2,1,0:T(8,128)(2,1)S(1)}, bf16[64,32,128]{2,1,0:T(8,128)(2,1)S(1)}, u32[]{:S(2)}, u32[]{:S(2)}) collective-permute-start(bf16[64,32,128]{2,1,0:T(8,128)(2,1)S(1)} %shard_map.77.refs_0_), channel_id=1, source_target_pairs={{0,4},{4,0},{8,12},{12,8},{16,20},{20,16},{24,28},{28,24},{32,36},... | collective-permute-start | bytes 1572872 | tf_op jit(solution)/shard_map/ppermute | solution.py:74
  26.6 11.9 %copy-start.1 = (f32[4,32,128]{2,1,0:T(8,128)S(1)}, f32[4,32,128]{2,1,0:T(8,128)}, u32[]{:S(2)}) copy-start(f32[4,32,128]{2,1,0:T(8,128)} %previous.1) | copy-start | bytes 196612
  28.2 8.1 %collective-permute-start.9 = (f32[4,32,128]{2,1,0:T(8,128)S(1)}, f32[4,32,128]{2,1,0:T(8,128)S(1)}, u32[]{:S(2)}, u32[]{:S(2)}) collective-permute-start(f32[4,32,128]{2,1,0:T(8,128)S(1)} %shard_map.81.refs_0_), channel_id=1, source_target_pairs={{0,3},{1,0},{2,1},{3,2},{4,7},{5,4},{6,5},{7,6},{8,11},{9,8},{10,9... | collective-permute-start | bytes 196616 | tf_op jit(solution)/shard_map/ppermute | solution.py:272
  30.2 6.3 %collective-permute-start.8 = (f32[4,32,128]{2,1,0:T(8,128)S(1)}, f32[4,32,128]{2,1,0:T(8,128)S(1)}, u32[]{:S(2)}, u32[]{:S(2)}) collective-permute-start(f32[4,32,128]{2,1,0:T(8,128)S(1)} %shard_map.80.refs_0_), channel_id=1, source_target_pairs={{0,2},{1,3},{2,0},{3,1},{4,6},{5,7},{6,4},{7,5},{8,10},{9,11},{10,... | collective-permute-start | bytes 196616 | tf_op jit(solution)/shard_map/ppermute | solution.py:272
  34.2 4.3 %collective-permute-start.7 = (f32[4,32,128]{2,1,0:T(8,128)S(1)}, f32[4,32,128]{2,1,0:T(8,128)S(1)}, u32[]{:S(2)}, u32[]{:S(2)}) collective-permute-start(f32[4,32,128]{2,1,0:T(8,128)S(1)} %shard_map.79.refs_0_), channel_id=1, source_target_pairs={{0,1},{1,2},{2,3},{3,0},{4,5},{5,6},{6,7},{7,4},{8,9},{9,10},{10,1... | collective-permute-start | bytes 196616 | tf_op jit(solution)/shard_map/ppermute | solution.py:272
  38.6 3.2 %collective-permute-start.12 = (bf16[4,32,128]{2,1,0:T(8,128)(2,1)S(1)}, bf16[4,32,128]{2,1,0:T(8,128)(2,1)S(1)}, u32[]{:S(2)}, u32[]{:S(2)}) collective-permute-start(bf16[4,32,128]{2,1,0:T(8,128)(2,1)S(1)} %get-tuple-element.19.refs_0_), channel_id=1, source_target_pairs={{0,24},{4,28},{8,0},{12,4},{16,8},{20,12},{24,16},{28,20},{32,56},... | collective-permute-start | bytes 98312 | tf_op jit(solution)/shard_map/ppermute | solution.py:69
  40.8 4.3 %collective-permute-start.11 = (bf16[4,32,128]{2,1,0:T(8,128)(2,1)S(1)}, bf16[4,32,128]{2,1,0:T(8,128)(2,1)S(1)}, u32[]{:S(2)}, u32[]{:S(2)}) collective-permute-start(bf16[4,32,128]{2,1,0:T(8,128)(2,1)S(1)} %get-tuple-element.19.refs_0_), channel_id=1, source_target_pairs={{0,16},{4,20},{8,24},{12,28},{16,0},{20,4},{24,8},{28,12},{32,48},... | collective-permute-start | bytes 98312 | tf_op jit(solution)/shard_map/ppermute | solution.py:69
  40.8 4.3 %collective-permute-start.10 = (bf16[4,32,128]{2,1,0:T(8,128)(2,1)S(1)}, bf16[4,32,128]{2,1,0:T(8,128)(2,1)S(1)}, u32[]{:S(2)}, u32[]{:S(2)}) collective-permute-start(bf16[4,32,128]{2,1,0:T(8,128)(2,1)S(1)} %get-tuple-element.19.refs_0_), channel_id=1, source_target_pairs={{0,8},{4,12},{8,16},{12,20},{16,24},{20,28},{24,0},{28,4},{32,40},... | collective-permute-start | bytes 98312 | tf_op jit(solution)/shard_map/ppermute | solution.py:69
  45.1 6.6 %collective-permute-start.15 = (bf16[16,32,128]{2,1,0:T(8,128)(2,1)S(1)}, bf16[16,32,128]{2,1,0:T(8,128)(2,1)S(1)}, u32[]{:S(2)}, u32[]{:S(2)}) collective-permute-start(bf16[16,32,128]{2,1,0:T(8,128)(2,1)S(1)} %shard_map.84.refs_0_), channel_id=1, source_target_pairs={{0,96},{4,100},{8,104},{12,108},{16,112},{20,116},{24,120},{28,124... | collective-permute-start | bytes 393224 | tf_op jit(solution)/shard_map/ppermute | solution.py:73
  48.4 5.4 %collective-permute-start.14 = (bf16[16,32,128]{2,1,0:T(8,128)(2,1)S(1)}, bf16[16,32,128]{2,1,0:T(8,128)(2,1)S(1)}, u32[]{:S(2)}, u32[]{:S(2)}) collective-permute-start(bf16[16,32,128]{2,1,0:T(8,128)(2,1)S(1)} %shard_map.84.refs_0_), channel_id=1, source_target_pairs={{0,64},{4,68},{8,72},{12,76},{16,80},{20,84},{24,88},{28,92},{32,9... | collective-permute-start | bytes 393224 | tf_op jit(solution)/shard_map/ppermute | solution.py:73
  49.3 5.8 %collective-permute-start.13 = (bf16[16,32,128]{2,1,0:T(8,128)(2,1)S(1)}, bf16[16,32,128]{2,1,0:T(8,128)(2,1)S(1)}, u32[]{:S(2)}, u32[]{:S(2)}) collective-permute-start(bf16[16,32,128]{2,1,0:T(8,128)(2,1)S(1)} %shard_map.84.refs_0_), channel_id=1, source_target_pairs={{0,32},{4,36},{8,40},{12,44},{16,48},{20,52},{24,56},{28,60},{32,6... | collective-permute-start | bytes 393224 | tf_op jit(solution)/shard_map/ppermute | solution.py:73
  55.2 8.6 %collective-permute-start.16 = (bf16[64,32,128]{2,1,0:T(8,128)(2,1)S(1)}, bf16[64,32,128]{2,1,0:T(8,128)(2,1)S(1)}, u32[]{:S(2)}, u32[]{:S(2)}) collective-permute-start(bf16[64,32,128]{2,1,0:T(8,128)(2,1)S(1)} %shard_map.85.refs_0_), channel_id=1, source_target_pairs={{0,4},{4,0},{8,12},{12,8},{16,20},{20,16},{24,28},{28,24},{32,36},... | collective-permute-start | bytes 1572872 | tf_op jit(solution)/shard_map/ppermute | solution.py:74
  68.5 4.1 %collective-permute-start.19 = (f32[4,32,128]{2,1,0:T(8,128)S(1)}, f32[4,32,128]{2,1,0:T(8,128)S(1)}, u32[]{:S(2)}, u32[]{:S(2)}) collective-permute-start(f32[4,32,128]{2,1,0:T(8,128)S(1)} %shard_map.89.refs_0_), channel_id=1, source_target_pairs={{0,3},{1,0},{2,1},{3,2},{4,7},{5,4},{6,5},{7,6},{8,11},{9,8},{10,9... | collective-permute-start | bytes 196616 | tf_op jit(solution)/shard_map/ppermute | solution.py:272
  68.5 4.7 %collective-permute-start.18 = (f32[4,32,128]{2,1,0:T(8,128)S(1)}, f32[4,32,128]{2,1,0:T(8,128)S(1)}, u32[]{:S(2)}, u32[]{:S(2)}) collective-permute-start(f32[4,32,128]{2,1,0:T(8,128)S(1)} %shard_map.88.refs_0_), channel_id=1, source_target_pairs={{0,2},{1,3},{2,0},{3,1},{4,6},{5,7},{6,4},{7,5},{8,10},{9,11},{10,... | collective-permute-start | bytes 196616 | tf_op jit(solution)/shard_map/ppermute | solution.py:272
  71.0 4.3 %collective-permute-start.17 = (f32[4,32,128]{2,1,0:T(8,128)S(1)}, f32[4,32,128]{2,1,0:T(8,128)S(1)}, u32[]{:S(2)}, u32[]{:S(2)}) collective-permute-start(f32[4,32,128]{2,1,0:T(8,128)S(1)} %shard_map.87.refs_0_), channel_id=1, source_target_pairs={{0,1},{1,2},{2,3},{3,0},{4,5},{5,6},{6,7},{7,4},{8,9},{9,10},{10,1... | collective-permute-start | bytes 196616 | tf_op jit(solution)/shard_map/ppermute | solution.py:272
  75.4 3.3 %collective-permute-start.22 = (bf16[4,32,128]{2,1,0:T(8,128)(2,1)S(1)}, bf16[4,32,128]{2,1,0:T(8,128)(2,1)S(1)}, u32[]{:S(2)}, u32[]{:S(2)}) collective-permute-start(bf16[4,32,128]{2,1,0:T(8,128)(2,1)S(1)} %get-tuple-element.21.refs_0_), channel_id=1, source_target_pairs={{0,24},{4,28},{8,0},{12,4},{16,8},{20,12},{24,16},{28,20},{32,56},... | collective-permute-start | bytes 98312 | tf_op jit(solution)/shard_map/ppermute | solution.py:69
  75.4 4.3 %collective-permute-start.21 = (bf16[4,32,128]{2,1,0:T(8,128)(2,1)S(1)}, bf16[4,32,128]{2,1,0:T(8,128)(2,1)S(1)}, u32[]{:S(2)}, u32[]{:S(2)}) collective-permute-start(bf16[4,32,128]{2,1,0:T(8,128)(2,1)S(1)} %get-tuple-element.21.refs_0_), channel_id=1, source_target_pairs={{0,16},{4,20},{8,24},{12,28},{16,0},{20,4},{24,8},{28,12},{32,48},... | collective-permute-start | bytes 98312 | tf_op jit(solution)/shard_map/ppermute | solution.py:69
  76.4 4.2 %collective-permute-start.20 = (bf16[4,32,128]{2,1,0:T(8,128)(2,1)S(1)}, bf16[4,32,128]{2,1,0:T(8,128)(2,1)S(1)}, u32[]{:S(2)}, u32[]{:S(2)}) collective-permute-start(bf16[4,32,128]{2,1,0:T(8,128)(2,1)S(1)} %get-tuple-element.21.refs_0_), channel_id=1, source_target_pairs={{0,8},{4,12},{8,16},{12,20},{16,24},{20,28},{24,0},{28,4},{32,40},... | collective-permute-start | bytes 98312 | tf_op jit(solution)/shard_map/ppermute | solution.py:69
  80.6 5.0 %collective-permute-start.25 = (bf16[16,32,128]{2,1,0:T(8,128)(2,1)S(1)}, bf16[16,32,128]{2,1,0:T(8,128)(2,1)S(1)}, u32[]{:S(2)}, u32[]{:S(2)}) collective-permute-start(bf16[16,32,128]{2,1,0:T(8,128)(2,1)S(1)} %shard_map.92.refs_0_), channel_id=1, source_target_pairs={{0,96},{4,100},{8,104},{12,108},{16,112},{20,116},{24,120},{28,124... | collective-permute-start | bytes 393224 | tf_op jit(solution)/shard_map/ppermute | solution.py:73
  82.3 5.4 %collective-permute-start.24 = (bf16[16,32,128]{2,1,0:T(8,128)(2,1)S(1)}, bf16[16,32,128]{2,1,0:T(8,128)(2,1)S(1)}, u32[]{:S(2)}, u32[]{:S(2)}) collective-permute-start(bf16[16,32,128]{2,1,0:T(8,128)(2,1)S(1)} %shard_map.92.refs_0_), channel_id=1, source_target_pairs={{0,64},{4,68},{8,72},{12,76},{16,80},{20,84},{24,88},{28,92},{32,9... | collective-permute-start | bytes 393224 | tf_op jit(solution)/shard_map/ppermute | solution.py:73
  83.7 5.3 %collective-permute-start.23 = (bf16[16,32,128]{2,1,0:T(8,128)(2,1)S(1)}, bf16[16,32,128]{2,1,0:T(8,128)(2,1)S(1)}, u32[]{:S(2)}, u32[]{:S(2)}) collective-permute-start(bf16[16,32,128]{2,1,0:T(8,128)(2,1)S(1)} %shard_map.92.refs_0_), channel_id=1, source_target_pairs={{0,32},{4,36},{8,40},{12,44},{16,48},{20,52},{24,56},{28,60},{32,6... | collective-permute-start | bytes 393224 | tf_op jit(solution)/shard_map/ppermute | solution.py:73
  89.1 5.9 %collective-permute-start.26 = (bf16[64,32,128]{2,1,0:T(8,128)(2,1)S(1)}, bf16[64,32,128]{2,1,0:T(8,128)(2,1)S(1)}, u32[]{:S(2)}, u32[]{:S(2)}) collective-permute-start(bf16[64,32,128]{2,1,0:T(8,128)(2,1)S(1)} %shard_map.93.refs_0_), channel_id=1, source_target_pairs={{0,4},{4,0},{8,12},{12,8},{16,20},{20,16},{24,28},{28,24},{32,36},... | collective-permute-start | bytes 1572872 | tf_op jit(solution)/shard_map/ppermute | solution.py:74
  99.7 4.3 %collective-permute-start.29 = (f32[4,32,128]{2,1,0:T(8,128)S(1)}, f32[4,32,128]{2,1,0:T(8,128)S(1)}, u32[]{:S(2)}, u32[]{:S(2)}) collective-permute-start(f32[4,32,128]{2,1,0:T(8,128)S(1)} %shard_map.97.refs_0_), channel_id=1, source_target_pairs={{0,3},{1,0},{2,1},{3,2},{4,7},{5,4},{6,5},{7,6},{8,11},{9,8},{10,9... | collective-permute-start | bytes 196616 | tf_op jit(solution)/shard_map/ppermute | solution.py:272
  99.8 4.7 %collective-permute-start.28 = (f32[4,32,128]{2,1,0:T(8,128)S(1)}, f32[4,32,128]{2,1,0:T(8,128)S(1)}, u32[]{:S(2)}, u32[]{:S(2)}) collective-permute-start(f32[4,32,128]{2,1,0:T(8,128)S(1)} %shard_map.96.refs_0_), channel_id=1, source_target_pairs={{0,2},{1,3},{2,0},{3,1},{4,6},{5,7},{6,4},{7,5},{8,10},{9,11},{10,... | collective-permute-start | bytes 196616 | tf_op jit(solution)/shard_map/ppermute | solution.py:272
  102.4 4.3 %collective-permute-start.27 = (f32[4,32,128]{2,1,0:T(8,128)S(1)}, f32[4,32,128]{2,1,0:T(8,128)S(1)}, u32[]{:S(2)}, u32[]{:S(2)}) collective-permute-start(f32[4,32,128]{2,1,0:T(8,128)S(1)} %shard_map.95.refs_0_), channel_id=1, source_target_pairs={{0,1},{1,2},{2,3},{3,0},{4,5},{5,6},{6,7},{7,4},{8,9},{9,10},{10,1... | collective-permute-start | bytes 196616 | tf_op jit(solution)/shard_map/ppermute | solution.py:272
where the time goes:
time: 108 us; the launch traced here: 107 us
  starting transfers between devices  45.3 us (42%)
  waiting for transfers between devices  31.5 us (29%)
  Pallas kernels  26.2 us (24%)
  local copies, waits for them, and re-layouts  2.23 us (2%)
  between operations  2.2 us (2%)
    pallas_call x12, Pallas kernels, local_products(): pl.pallas_call(functools.partial(products_kernel, part * owned), out_shap...  18.3 us
    ppermute x3, starting transfers between devices, all_gathered(): theirs = lax.ppermute(mine, 'row', chip_shifts(0, 0, 1))  13.1 us
    ppermute x9, starting transfers between devices, image_pieces(): lax.ppermute(piece, 'col', [(i, (i + part) % parts) for i in range(parts)])  11.9 us
    ppermute x9, waiting for transfers between devices, all_gathered(): lax.ppermute(line, 'row', chip_shifts(dx, 0))  11.2 us
    ppermute x9, starting transfers between devices, all_gathered(): lax.ppermute(line, 'row', chip_shifts(dx, 0))  11 us
    ppermute x9, starting transfers between devices, line_gathered(): lax.ppermute(owned, 'row', chip_shifts(0, dy))  9.29 us
    ppermute x9, waiting for transfers between devices, line_gathered(): lax.ppermute(owned, 'row', chip_shifts(0, dy))  7.92 us
    ppermute x9, waiting for transfers between devices, image_pieces(): lax.ppermute(piece, 'col', [(i, (i + part) % parts) for i in range(parts)])  7.83 us
  transfers between devices with their start and end apart: 30, of which 22 were waited for; matrix products, arithmetic and copies ran while one was open for 1% of the time, Pallas kernels for 11%

commit v1 on v0

--- a/solution.py
+++ b/solution.py
@@ -10,10 +10,12 @@
 
 SIDE = 4
 CORES = 2
-CHUNK = 64
-UNROLL = 16
-GROUP = 8
-BATCH = 4
+CHUNK = 32
+SPARE = 64
+GROUP = 4
+BATCH = 24
+LANES = 256
+HEAD = 2 * LANES
 MIB = 1 << 20
 
 
@@ -40,10 +42,10 @@
         out[place * size : (place + 1) * size] = part[...]
 
 
-def joined(parts, after=()):
+def joined(parts, after=(), after_specs=()):
     shape = (len(parts) * parts[0].shape[0], *parts[0].shape[1:])
     kernel = functools.partial(join_kernel, len(parts))
-    specs = [VMEM] * (len(parts) + len(after))
+    specs = [VMEM] * len(parts) + list(after_specs or [VMEM] * len(after))
     return small_call(kernel, jax.ShapeDtypeStruct(shape, parts[0].dtype), specs)(*parts, *after)
 
 
@@ -65,8 +67,8 @@
     return pairs
 
 
-def line_gathered(owned, after=()):
-    return joined([owned] + [lax.ppermute(owned, "row", chip_shifts(0, dy)) for dy in range(1, SIDE)], after)
+def line_gathered(owned, after=(), specs=()):
+    return joined([owned] + [lax.ppermute(owned, "row", chip_shifts(0, dy)) for dy in range(1, SIDE)], after, specs)
 
 
 def all_gathered(line, after=()):
@@ -84,14 +86,15 @@
     return lax.broadcasted_iota(jnp.int32, shape, dim)
 
 
-def plan_kernel(parts, owned, live_ref, rows_ref, cols_ref, _after, place_ref, order_ref, groups_ref, sizes_ref):
+def plan_kernel(parts, owned, live_ref, rows_ref, cols_ref, _center, _half, _after, place_out, table_out, place_ref, table_ref, sems):
     live = live_ref[0]
     me, here = lax.axis_index("row"), lax.axis_index("col")
     rows, cols = rows_ref[...], cols_ref[...]
     slots = rows.shape[1]
     span = parts * owned
-    room = order_ref.shape[1] - CHUNK
-    lanes = groups_ref.shape[1]
+    lanes = LANES
+    head = HEAD
+    room = table_ref.shape[1] - head - SPARE
 
     turned = lax.rem(lax.div(rows, owned) + (parts - here), parts) * owned + lax.rem(rows, owned)
     ids = iota((1, slots), 1)
@@ -116,40 +119,43 @@
     dcore = lax.rem(me + owner, CORES)
     source = ((dcore * SIDE + dx) * SIDE + dy) * owned + lax.rem(cols, owned)
     weights = jnp.broadcast_to(jnp.where(alive, source, 0).astype(jnp.float32), (8, slots)).astype(jnp.bfloat16)
-    for block in range((room + CHUNK) // CHUNK):
-        match = jnp.where(place == iota((CHUNK, slots), 0) + block * CHUNK, 1.0, 0.0).astype(jnp.bfloat16)
+    for block in range((room + SPARE) // SPARE):
+        match = jnp.where(place == iota((SPARE, slots), 0) + block * SPARE, 1.0, 0.0).astype(jnp.bfloat16)
         found = lax.dot_general(weights, match, (((1,), (1,)), ((), ())), preferred_element_type=jnp.float32)
-        order_ref[:, block * CHUNK : (block + 1) * CHUNK] = found[:1].astype(jnp.int32)
+        table_ref[:, head + block * SPARE : head + (block + 1) * SPARE] = found[:1].astype(jnp.int32)
 
     ended = jnp.where(ends <= lane_of * GROUP, 1.0, 0.0)
-    groups_ref[...] = jnp.sum(ended, axis=0, keepdims=True).astype(jnp.int32)
-    total = jnp.sum(padded.astype(jnp.float32), axis=0, keepdims=True).astype(jnp.int32)
+    table_ref[:, lanes:head] = jnp.sum(ended, axis=0, keepdims=True).astype(jnp.int32)
     at_ends = jnp.sum(jnp.where(row_of == lane_of, ends, 0).astype(jnp.float32), axis=0, keepdims=True).astype(jnp.int32)
     lane = iota((1, lanes), 1)
-    batches = lax.div(total + (GROUP * BATCH - 1), GROUP * BATCH)
-    sizes = jnp.where(lane == span, lax.div(live + (CHUNK - 1), CHUNK), at_ends)
-    sizes = jnp.where(lane == span + 1, batches, sizes)
-    sizes_ref[...] = jnp.where(lane == span + 2, total, sizes)
-
-
-def sort_plan(rows, cols, live, after, parts, owned):
+    table_ref[:, :lanes] = jnp.where(lane == span, lax.div(live + (CHUNK - 1), CHUNK), at_ends)
+    copies = [
+        pltpu.make_async_copy(place_ref, place_out, sems.at[0]),
+        pltpu.make_async_copy(table_ref, table_out, sems.at[1]),
+    ]
+    for copy in copies:
+        copy.start()
+    for copy in copies:
+        copy.wait()
+
+
+def sort_plan(rows, cols, live, scalars, after, parts, owned):
     slots = rows.shape[0]
     room = padded_room(slots, parts * owned)
-    widths = (slots, room + CHUNK, 128, 128)
+    widths = (slots, HEAD + room + SPARE)
     return pl.pallas_call(
         functools.partial(plan_kernel, parts, owned),
-        out_shape=[jax.ShapeDtypeStruct((1, width), jnp.int32) for width in widths],
-        in_specs=[SMEM, VMEM, VMEM, VMEM],
-        out_specs=[VMEM] * len(widths),
+        out_shape=[pltpu.SMEM((1, width), jnp.int32) for width in widths],
+        in_specs=[SMEM, VMEM, VMEM, SMEM, SMEM, VMEM],
+        out_specs=[SMEM] * len(widths),
+        scratch_shapes=[pltpu.VMEM((1, width), jnp.int32) for width in widths] + [pltpu.SemaphoreType.DMA((2,))],
         compiler_params=pltpu.CompilerParams(vmem_limit_bytes=8 * MIB),
         cost_estimate=pl.CostEstimate(flops=1000, bytes_accessed=1000, transcendentals=0),
-    )(live, rows.reshape(1, slots), cols.reshape(1, slots), after)
-
-
-def prepare_kernel(span, place, sizes, _center, _half, _after, blocks_hbm, store, raw, sems):
+    )(live, rows.reshape(1, slots), cols.reshape(1, slots), *scalars, after)
+
+
+def prepare_kernel(span, place, sizes, _after, blocks_hbm, store, raw, sems):
     chunks = sizes[0, span]
-    total = sizes[0, span + 2]
-    room = store.shape[0] - CHUNK
     size = raw.shape[1]
 
     def copy_of(c):
@@ -166,29 +172,21 @@
     def _(row):
         store[pl.ds(jnp.maximum(sizes[0, row] - GROUP, 0), GROUP)] = nothing
 
-    @pl.loop(0, BATCH)
-    def _(k):
-        @pl.when(total + k * GROUP < room)
-        def _():
-            store[pl.ds(total + k * GROUP, GROUP)] = nothing
-
     @pl.loop(0, chunks)
     def _(c):
         copy_of(c).wait()
 
-        @pl.loop(0, CHUNK // UNROLL)
-        def _(g):
-            for u in range(UNROLL):
-                slot = c * CHUNK + g * UNROLL + u
-                store[place[0, slot]] = raw[slot].T
-
-
-def prepared(place, sizes, blocks, scalars, after, span):
+        for u in range(CHUNK):
+            slot = c * CHUNK + u
+            store[place[0, slot]] = raw[slot].T
+
+
+def prepared(place, sizes, blocks, after, span):
     slots, size, _ = blocks.shape
     return pl.pallas_call(
         functools.partial(prepare_kernel, span),
-        out_shape=pltpu.VMEM((padded_room(slots, span) + CHUNK, size, size), blocks.dtype),
-        in_specs=[SMEM] * 4 + [VMEM, pl.BlockSpec(memory_space=pl.ANY)],
+        out_shape=pltpu.VMEM((padded_room(slots, span) + SPARE, size, size), blocks.dtype),
+        in_specs=[SMEM] * 2 + [VMEM, pl.BlockSpec(memory_space=pl.ANY)],
         out_specs=VMEM,
         scratch_shapes=[
             pltpu.VMEM((slots, size, size), blocks.dtype),
@@ -196,40 +194,40 @@
         ],
         compiler_params=pltpu.CompilerParams(vmem_limit_bytes=24 * MIB),
         cost_estimate=pl.CostEstimate(flops=1000, bytes_accessed=2 * slots * size * size, transcendentals=0),
-    )(place, sizes, *scalars, after, blocks)
-
-
-def products_kernel(first_row, order, groups, sizes, vec, store, *refs):
+    )(place, sizes, after, blocks)
+
+
+def products_kernel(first_row, table, vec, store, *refs):
     out, sums = refs[-2:]
     owned = out.shape[0]
     size = store.shape[1]
-    start = lax.div(sizes[0, first_row - 1], GROUP) if first_row else 0
-    count = lax.div(sizes[0, first_row + owned - 1], GROUP) - start
+    start = lax.div(table[0, first_row - 1], GROUP) if first_row else 0
+    count = lax.div(table[0, first_row + owned - 1], GROUP) - start
     sums[...] = jnp.zeros_like(sums)
 
     @pl.loop(0, lax.div(count + (BATCH - 1), BATCH))
     def _(batch):
         for k in range(BATCH):
             group = start + batch * BATCH + k
-            left = jnp.concatenate([vec[order[0, group * GROUP + i]] for i in range(GROUP)], axis=1)
+            left = jnp.concatenate([vec[table[0, HEAD + group * GROUP + i]] for i in range(GROUP)], axis=1)
             right = store[pl.ds(group * GROUP, GROUP)].reshape(GROUP * size, size)
-            sums[groups[0, group]] += jnp.dot(left, right, preferred_element_type=jnp.float32)
+            sums[table[0, LANES + group]] += jnp.dot(left, right, preferred_element_type=jnp.float32)
 
     out[...] = sums[first_row : first_row + owned]
 
 
 def local_products(part, vec, prep, after, owned, parts):
-    order, groups, sizes, store = prep
+    table, store = prep
     _, vecs, size = vec.shape
     return pl.pallas_call(
         functools.partial(products_kernel, part * owned),
         out_shape=jax.ShapeDtypeStruct((owned, vecs, size), jnp.float32),
-        in_specs=[SMEM] * 3 + [VMEM] * (2 + len(after)),
+        in_specs=[SMEM] + [VMEM] * (2 + len(after)),
         out_specs=VMEM,
         scratch_shapes=[pltpu.VMEM((owned * parts + 1, vecs, size), jnp.float32)],
         compiler_params=pltpu.CompilerParams(vmem_limit_bytes=4 * MIB),
         cost_estimate=pl.CostEstimate(flops=640 // 2 * vecs * size * size, bytes_accessed=MIB, transcendentals=0),
-    )(order, groups, sizes, vec, kept(store), *after)
+    )(table, vec, kept(store), *after)
 
 
 def kept(store):
@@ -246,14 +244,14 @@
     out_bf[...] = value.astype(out_bf.dtype)
 
 
-def next_kernel(center, half_width, current, previous, *refs):
-    pieces, (out, out_bf) = refs[:-2], refs[-2:]
+def next_kernel(count, center, half_width, current, previous, *refs):
+    pieces, outs = refs[:count], refs[count:]
     image = pieces[0][...]
     for piece in pieces[1:]:
         image += piece[...]
     value = 2.0 * (image - center[0] * current[...]) / half_width[0] - previous[...]
-    out[...] = value
-    out_bf[...] = value.astype(out_bf.dtype)
+    for out in outs:
+        out[...] = value.astype(out.dtype)
 
 
 def on_device(start_vectors, blocks, block_rows, block_cols, live_counts, center, half_width):
@@ -274,19 +272,20 @@
         return pieces
 
     start_bf = rounded(start_vectors)
-    place, order, groups, sizes = sort_plan(block_rows, block_cols, live_counts, start_bf, parts, owned)
-    line = line_gathered(start_bf, (sizes,))
-    store = prepared(place, sizes, blocks, scalars, line, parts * owned)
-    prep = (order, groups, sizes, store)
+    place, table = sort_plan(block_rows, block_cols, live_counts, scalars, start_bf, parts, owned)
+    line = line_gathered(start_bf, (table,), (SMEM,))
+    store = prepared(place, table, blocks, line, parts * owned)
+    prep = (table, store)
     pieces = image_pieces(all_gathered(line, (kept(store),)))
     first = small_call(first_kernel, outs, [SMEM, SMEM] + [VMEM] * (1 + parts))
     current, current_bf = first(*scalars, start_vectors, *pieces)
     previous = start_vectors
-    for _ in range(2):
+    for turn in range(2):
         pieces = image_pieces(all_gathered(line_gathered(current_bf)))
-        step = small_call(next_kernel, outs, [SMEM, SMEM] + [VMEM] * (2 + parts))
-        following, current_bf = step(*scalars, current, previous, *pieces)
-        previous, current = current, following
+        wanted = outs[:1] if turn else outs
+        step = small_call(functools.partial(next_kernel, parts), wanted, [SMEM, SMEM] + [VMEM] * (2 + parts))
+        following, *rest = step(*scalars, current, previous, *pieces)
+        previous, current, current_bf = current, following, rest[0] if rest else None
     return current
 
 

time: 108 us -> 98.1 us (0.908)
  the two profiles are of different devices: /device:TPU:1 before, /device:TPU:0 now
where the time goes in v1:
time: 98.1 us; the launch traced here: 96.7 us
  waiting for transfers between devices  47 us (48%)
  starting transfers between devices  37.2 us (38%)
  Pallas kernels  8.13 us (8%)
  local copies, waits for them, and re-layouts  2.23 us (2%)
  between operations  2.19 us (2%)
    ppermute x9, waiting for transfers between devices, all_gathered(): lax.ppermute(line, 'row', chip_shifts(dx, 0))  17.9 us
    ppermute x9, waiting for transfers between devices, image_pieces(): lax.ppermute(piece, 'col', [(i, (i + part) % parts) for i in range(parts)])  13.8 us
    ppermute x9, starting transfers between devices, image_pieces(): lax.ppermute(piece, 'col', [(i, (i + part) % parts) for i in range(parts)])  13.5 us
    ppermute x9, starting transfers between devices, line_gathered(): lax.ppermute(owned, 'row', chip_shifts(0, dy))  12 us
    ppermute x9, starting transfers between devices, all_gathered(): lax.ppermute(line, 'row', chip_shifts(dx, 0))  11.4 us
    ppermute x9, waiting for transfers between devices, line_gathered(): lax.ppermute(owned, 'row', chip_shifts(0, dy))  9.59 us
    ppermute x3, waiting for transfers between devices, all_gathered(): theirs = lax.ppermute(mine, 'row', chip_shifts(0, 0, 1))  5.69 us
    pallas_call x12, Pallas kernels, local_products(): pl.pallas_call(functools.partial(products_kernel, part * owned), out_shap...  4.01 us
  transfers between devices with their start and end apart: 30, of which 26 were waited for; matrix products, arithmetic and copies ran while one was open for 1% of the time, Pallas kernels for 5%

profile of v1, /device:TPU:0, one launch (start us, length us, event | category | flops | bytes accessed | tf_op | source)
XLA Modules:
  0.0 96.7 jit_solution(10048572196393922096)
XLA Ops:
  0.8 3.1 %collective-permute-start.2 = (bf16[4,32,128]{2,1,0:T(8,128)(2,1)S(1)}, bf16[4,32,128]{2,1,0:T(8,128)(2,1)S(1)}, u32[]{:S(2)}, u32[]{:S(2)}) collective-permute-start(bf16[4,32,128]{2,1,0:T(8,128)(2,1)S(1)} %shard_map.73._after.refs_0_), channel_id=1, source_target_pairs={{0,24},{4,28},{8,0},{12,4},{16,8},{20,12},{24,16},{28,20},{32,56},... | collective-permute-start | bytes 98312 | tf_op jit(solution)/shard_map/ppermute | solution.py:71
  8.9 1.4 %shard_map.74 = (s32[1,640]{1,0:T(1,128)S(4)}, s32[1,1344]{1,0:T(1,128)S(4)}) custom-call(s32[1]{0:T(128)S(6)} %copy.8.live_ref, s32[1,640]{1,0:T(1,128)S(1)} %reshape.14.rows_ref, s32[1,640]{1,0:T(1,128)S(1)} %reshape.15.cols_ref, f32[1]{0:T(128)} %bitcast.2._center, f32[1]{0:T(128)} %bitcast.6._half, bf16[4,32,128]{2,1,0:T(8,128)(2,1)S(1)} %shard_map.73._after.refs_0_), custom_call_target="tpu_custom_call" | custom-call | flops 1000 | bytes 1000 | tf_op jit(solution)/shard_map/pallas_call | solution.py:146
  10.3 2.8 %collective-permute-start.5 = (bf16[16,32,128]{2,1,0:T(8,128)(2,1)S(1)}, bf16[16,32,128]{2,1,0:T(8,128)(2,1)S(1)}, u32[]{:S(2)}, u32[]{:S(2)}) collective-permute-start(bf16[16,32,128]{2,1,0:T(8,128)(2,1)S(1)} %shard_map.75._after.refs_0_), channel_id=1, source_target_pairs={{0,96},{4,100},{8,104},{12,108},{16,112},{20,116},{24,120},{28,124... | collective-permute-start | bytes 393224 | tf_op jit(solution)/shard_map/ppermute | solution.py:75
  14.8 1.7 %shard_map.76.refs_4_.store = bf16[832,128,128]{2,1,0:T(8,128)(2,1)S(1)} custom-call(s32[1,640]{1,0:T(1,128)S(4)} %get-tuple-element.12.place, s32[1,1344]{1,0:T(1,128)S(4)} %get-tuple-element.11.refs_4_.sizes.table, bf16[16,32,128]{2,1,0:T(8,128)(2,1)S(1)} %shard_map.75._after.refs_0_, bf16[640,128,128]{2,1,0:T(8,128)(2,1)} %blocks_hbm.1), custom_call_target="tpu_custom_call" | custom-call | flops 1000 | bytes 20971520 | tf_op jit(solution)/shard_map/pallas_call | solution.py:186
  16.6 1.3 %collective-permute-done.5.refs_3_ = bf16[16,32,128]{2,1,0:T(8,128)(2,1)S(1)} collective-permute-done((bf16[16,32,128]{2,1,0:T(8,128)(2,1)S(1)}, bf16[16,32,128]{2,1,0:T(8,128)(2,1)S(1)}, u32[]{:S(2)}, u32[]{:S(2)}) %collective-permute-start.5) | collective-permute-done | bytes 131104 | tf_op jit(solution)/shard_map/ppermute | solution.py:75
  17.9 2.3 %collective-permute-done.4.refs_2_ = bf16[16,32,128]{2,1,0:T(8,128)(2,1)S(1)} collective-permute-done((bf16[16,32,128]{2,1,0:T(8,128)(2,1)S(1)}, bf16[16,32,128]{2,1,0:T(8,128)(2,1)S(1)}, u32[]{:S(2)}, u32[]{:S(2)}) %collective-permute-start.4) | collective-permute-done | bytes 131104 | tf_op jit(solution)/shard_map/ppermute | solution.py:75
  20.2 1.4 %collective-permute-done.3.refs_1_ = bf16[16,32,128]{2,1,0:T(8,128)(2,1)S(1)} collective-permute-done((bf16[16,32,128]{2,1,0:T(8,128)(2,1)S(1)}, bf16[16,32,128]{2,1,0:T(8,128)(2,1)S(1)}, u32[]{:S(2)}, u32[]{:S(2)}) %collective-permute-start.3) | collective-permute-done | bytes 131104 | tf_op jit(solution)/shard_map/ppermute | solution.py:75
  21.7 1.9 %collective-permute-done.6.refs_1_ = bf16[64,32,128]{2,1,0:T(8,128)(2,1)S(1)} collective-permute-done((bf16[64,32,128]{2,1,0:T(8,128)(2,1)S(1)}, bf16[64,32,128]{2,1,0:T(8,128)(2,1)S(1)}, u32[]{:S(2)}, u32[]{:S(2)}) %collective-permute-start.6) | collective-permute-done | bytes 524320 | tf_op jit(solution)/shard_map/ppermute | solution.py:76
  24.4 4.7 %collective-permute-start.9 = (f32[4,32,128]{2,1,0:T(8,128)S(1)}, f32[4,32,128]{2,1,0:T(8,128)S(1)}, u32[]{:S(2)}, u32[]{:S(2)}) collective-permute-start(f32[4,32,128]{2,1,0:T(8,128)S(1)} %shard_map.81.refs_0_), channel_id=1, source_target_pairs={{0,3},{1,0},{2,1},{3,2},{4,7},{5,4},{6,5},{7,6},{8,11},{9,8},{10,9... | collective-permute-start | bytes 196616 | tf_op jit(solution)/shard_map/ppermute | solution.py:270
  29.6 1.3 %collective-permute-start.7 = (f32[4,32,128]{2,1,0:T(8,128)S(1)}, f32[4,32,128]{2,1,0:T(8,128)S(1)}, u32[]{:S(2)}, u32[]{:S(2)}) collective-permute-start(f32[4,32,128]{2,1,0:T(8,128)S(1)} %shard_map.79.refs_0_), channel_id=1, source_target_pairs={{0,1},{1,2},{2,3},{3,0},{4,5},{5,6},{6,7},{7,4},{8,9},{9,10},{10,1... | collective-permute-start | bytes 196616 | tf_op jit(solution)/shard_map/ppermute | solution.py:270
  32.8 2.8 %collective-permute-done.8.refs_1_ = f32[4,32,128]{2,1,0:T(8,128)S(1)} collective-permute-done((f32[4,32,128]{2,1,0:T(8,128)S(1)}, f32[4,32,128]{2,1,0:T(8,128)S(1)}, u32[]{:S(2)}, u32[]{:S(2)}) %collective-permute-start.8) | collective-permute-done | bytes 65568 | tf_op jit(solution)/shard_map/ppermute | solution.py:270
  36.3 2.9 %collective-permute-start.12 = (bf16[4,32,128]{2,1,0:T(8,128)(2,1)S(1)}, bf16[4,32,128]{2,1,0:T(8,128)(2,1)S(1)}, u32[]{:S(2)}, u32[]{:S(2)}) collective-permute-start(bf16[4,32,128]{2,1,0:T(8,128)(2,1)S(1)} %get-tuple-element.14.refs_0_), channel_id=1, source_target_pairs={{0,24},{4,28},{8,0},{12,4},{16,8},{20,12},{24,16},{28,20},{32,56},... | collective-permute-start | bytes 98312 | tf_op jit(solution)/shard_map/ppermute | solution.py:71
  40.8 3.8 %collective-permute-done.11.refs_2_ = bf16[4,32,128]{2,1,0:T(8,128)(2,1)S(1)} collective-permute-done((bf16[4,32,128]{2,1,0:T(8,128)(2,1)S(1)}, bf16[4,32,128]{2,1,0:T(8,128)(2,1)S(1)}, u32[]{:S(2)}, u32[]{:S(2)}) %collective-permute-start.11) | collective-permute-done | bytes 32800 | tf_op jit(solution)/shard_map/ppermute | solution.py:71
  45.3 3.1 %collective-permute-start.15 = (bf16[16,32,128]{2,1,0:T(8,128)(2,1)S(1)}, bf16[16,32,128]{2,1,0:T(8,128)(2,1)S(1)}, u32[]{:S(2)}, u32[]{:S(2)}) collective-permute-start(bf16[16,32,128]{2,1,0:T(8,128)(2,1)S(1)} %shard_map.84.refs_0_), channel_id=1, source_target_pairs={{0,96},{4,100},{8,104},{12,108},{16,112},{20,116},{24,120},{28,124... | collective-permute-start | bytes 393224 | tf_op jit(solution)/shard_map/ppermute | solution.py:75
  49.4 3.0 %collective-permute-done.15.refs_3_ = bf16[16,32,128]{2,1,0:T(8,128)(2,1)S(1)} collective-permute-done((bf16[16,32,128]{2,1,0:T(8,128)(2,1)S(1)}, bf16[16,32,128]{2,1,0:T(8,128)(2,1)S(1)}, u32[]{:S(2)}, u32[]{:S(2)}) %collective-permute-start.15) | collective-permute-done | bytes 131104 | tf_op jit(solution)/shard_map/ppermute | solution.py:75
  52.4 2.6 %collective-permute-done.14.refs_2_ = bf16[16,32,128]{2,1,0:T(8,128)(2,1)S(1)} collective-permute-done((bf16[16,32,128]{2,1,0:T(8,128)(2,1)S(1)}, bf16[16,32,128]{2,1,0:T(8,128)(2,1)S(1)}, u32[]{:S(2)}, u32[]{:S(2)}) %collective-permute-start.14) | collective-permute-done | bytes 131104 | tf_op jit(solution)/shard_map/ppermute | solution.py:75
  56.2 1.9 %collective-permute-done.16.refs_1_ = bf16[64,32,128]{2,1,0:T(8,128)(2,1)S(1)} collective-permute-done((bf16[64,32,128]{2,1,0:T(8,128)(2,1)S(1)}, bf16[64,32,128]{2,1,0:T(8,128)(2,1)S(1)}, u32[]{:S(2)}, u32[]{:S(2)}) %collective-permute-start.16) | collective-permute-done | bytes 524320 | tf_op jit(solution)/shard_map/ppermute | solution.py:76
  59.4 2.2 %collective-permute-start.18 = (f32[4,32,128]{2,1,0:T(8,128)S(1)}, f32[4,32,128]{2,1,0:T(8,128)S(1)}, u32[]{:S(2)}, u32[]{:S(2)}) collective-permute-start(f32[4,32,128]{2,1,0:T(8,128)S(1)} %shard_map.88.refs_0_), channel_id=1, source_target_pairs={{0,2},{1,3},{2,0},{3,1},{4,6},{5,7},{6,4},{7,5},{8,10},{9,11},{10,... | collective-permute-start | bytes 196616 | tf_op jit(solution)/shard_map/ppermute | solution.py:270
  63.5 2.3 %collective-permute-done.18.refs_1_ = f32[4,32,128]{2,1,0:T(8,128)S(1)} collective-permute-done((f32[4,32,128]{2,1,0:T(8,128)S(1)}, f32[4,32,128]{2,1,0:T(8,128)S(1)}, u32[]{:S(2)}, u32[]{:S(2)}) %collective-permute-start.18) | collective-permute-done | bytes 65568 | tf_op jit(solution)/shard_map/ppermute | solution.py:270
  65.8 1.6 %collective-permute-done.17.refs_0_ = f32[4,32,128]{2,1,0:T(8,128)S(1)} collective-permute-done((f32[4,32,128]{2,1,0:T(8,128)S(1)}, f32[4,32,128]{2,1,0:T(8,128)S(1)}, u32[]{:S(2)}, u32[]{:S(2)}) %collective-permute-start.17) | collective-permute-done | bytes 65568 | tf_op jit(solution)/shard_map/ppermute | solution.py:270
  67.4 2.4 %collective-permute-start.22 = (bf16[4,32,128]{2,1,0:T(8,128)(2,1)S(1)}, bf16[4,32,128]{2,1,0:T(8,128)(2,1)S(1)}, u32[]{:S(2)}, u32[]{:S(2)}) collective-permute-start(bf16[4,32,128]{2,1,0:T(8,128)(2,1)S(1)} %get-tuple-element.16.refs_0_), channel_id=1, source_target_pairs={{0,24},{4,28},{8,0},{12,4},{16,8},{20,12},{24,16},{28,20},{32,56},... | collective-permute-start | bytes 98312 | tf_op jit(solution)/shard_map/ppermute | solution.py:71
  71.4 3.9 %collective-permute-done.21.refs_2_ = bf16[4,32,128]{2,1,0:T(8,128)(2,1)S(1)} collective-permute-done((bf16[4,32,128]{2,1,0:T(8,128)(2,1)S(1)}, bf16[4,32,128]{2,1,0:T(8,128)(2,1)S(1)}, u32[]{:S(2)}, u32[]{:S(2)}) %collective-permute-start.21) | collective-permute-done | bytes 32800 | tf_op jit(solution)/shard_map/ppermute | solution.py:71
  75.3 1.3 %collective-permute-start.25 = (bf16[16,32,128]{2,1,0:T(8,128)(2,1)S(1)}, bf16[16,32,128]{2,1,0:T(8,128)(2,1)S(1)}, u32[]{:S(2)}, u32[]{:S(2)}) collective-permute-start(bf16[16,32,128]{2,1,0:T(8,128)(2,1)S(1)} %shard_map.92.refs_0_), channel_id=1, source_target_pairs={{0,96},{4,100},{8,104},{12,108},{16,112},{20,116},{24,120},{28,124... | collective-permute-start | bytes 393224 | tf_op jit(solution)/shard_map/ppermute | solution.py:75
  76.8 1.3 %collective-permute-start.23 = (bf16[16,32,128]{2,1,0:T(8,128)(2,1)S(1)}, bf16[16,32,128]{2,1,0:T(8,128)(2,1)S(1)}, u32[]{:S(2)}, u32[]{:S(2)}) collective-permute-start(bf16[16,32,128]{2,1,0:T(8,128)(2,1)S(1)} %shard_map.92.refs_0_), channel_id=1, source_target_pairs={{0,32},{4,36},{8,40},{12,44},{16,48},{20,52},{24,56},{28,60},{32,6... | collective-permute-start | bytes 393224 | tf_op jit(solution)/shard_map/ppermute | solution.py:75
  78.1 2.2 %collective-permute-done.25.refs_3_ = bf16[16,32,128]{2,1,0:T(8,128)(2,1)S(1)} collective-permute-done((bf16[16,32,128]{2,1,0:T(8,128)(2,1)S(1)}, bf16[16,32,128]{2,1,0:T(8,128)(2,1)S(1)}, u32[]{:S(2)}, u32[]{:S(2)}) %collective-permute-start.25) | collective-permute-done | bytes 131104 | tf_op jit(solution)/shard_map/ppermute | solution.py:75
  80.3 2.9 %collective-permute-done.24.refs_2_ = bf16[16,32,128]{2,1,0:T(8,128)(2,1)S(1)} collective-permute-done((bf16[16,32,128]{2,1,0:T(8,128)(2,1)S(1)}, bf16[16,32,128]{2,1,0:T(8,128)(2,1)S(1)}, u32[]{:S(2)}, u32[]{:S(2)}) %collective-permute-start.24) | collective-permute-done | bytes 131104 | tf_op jit(solution)/shard_map/ppermute | solution.py:75
  83.2 1.2 %collective-permute-done.23.refs_1_ = bf16[16,32,128]{2,1,0:T(8,128)(2,1)S(1)} collective-permute-done((bf16[16,32,128]{2,1,0:T(8,128)(2,1)S(1)}, bf16[16,32,128]{2,1,0:T(8,128)(2,1)S(1)}, u32[]{:S(2)}, u32[]{:S(2)}) %collective-permute-start.23) | collective-permute-done | bytes 131104 | tf_op jit(solution)/shard_map/ppermute | solution.py:75
  84.5 1.9 %collective-permute-done.26.refs_1_ = bf16[64,32,128]{2,1,0:T(8,128)(2,1)S(1)} collective-permute-done((bf16[64,32,128]{2,1,0:T(8,128)(2,1)S(1)}, bf16[64,32,128]{2,1,0:T(8,128)(2,1)S(1)}, u32[]{:S(2)}, u32[]{:S(2)}) %collective-permute-start.26) | collective-permute-done | bytes 524320 | tf_op jit(solution)/shard_map/ppermute | solution.py:76
  87.2 1.6 %collective-permute-start.29 = (f32[4,32,128]{2,1,0:T(8,128)S(1)}, f32[4,32,128]{2,1,0:T(8,128)S(1)}, u32[]{:S(2)}, u32[]{:S(2)}) collective-permute-start(f32[4,32,128]{2,1,0:T(8,128)S(1)} %shard_map.97.refs_0_), channel_id=1, source_target_pairs={{0,3},{1,0},{2,1},{3,2},{4,7},{5,4},{6,5},{7,6},{8,11},{9,8},{10,9... | collective-permute-start | bytes 196616 | tf_op jit(solution)/shard_map/ppermute | solution.py:270
  88.8 1.5 %collective-permute-start.28 = (f32[4,32,128]{2,1,0:T(8,128)S(1)}, f32[4,32,128]{2,1,0:T(8,128)S(1)}, u32[]{:S(2)}, u32[]{:S(2)}) collective-permute-start(f32[4,32,128]{2,1,0:T(8,128)S(1)} %shard_map.96.refs_0_), channel_id=1, source_target_pairs={{0,2},{1,3},{2,0},{3,1},{4,6},{5,7},{6,4},{7,5},{8,10},{9,11},{10,... | collective-permute-start | bytes 196616 | tf_op jit(solution)/shard_map/ppermute | solution.py:270
  91.9 2.9 %collective-permute-done.28.refs_1_ = f32[4,32,128]{2,1,0:T(8,128)S(1)} collective-permute-done((f32[4,32,128]{2,1,0:T(8,128)S(1)}, f32[4,32,128]{2,1,0:T(8,128)S(1)}, u32[]{:S(2)}, u32[]{:S(2)}) %collective-permute-start.28) | collective-permute-done | bytes 65568 | tf_op jit(solution)/shard_map/ppermute | solution.py:270
  94.7 1.3 %collective-permute-done.27.refs_0_ = f32[4,32,128]{2,1,0:T(8,128)S(1)} collective-permute-done((f32[4,32,128]{2,1,0:T(8,128)S(1)}, f32[4,32,128]{2,1,0:T(8,128)S(1)}, u32[]{:S(2)}, u32[]{:S(2)}) %collective-permute-start.27) | collective-permute-done | bytes 65568 | tf_op jit(solution)/shard_map/ppermute | solution.py:270
  (61 shorter events, 22.0 us)
Async XLA Ops:
  0.0 0.8 copy-start
  0.8 9.4 %collective-permute-start.2 = (bf16[4,32,128]{2,1,0:T(8,128)(2,1)S(1)}, bf16[4,32,128]{2,1,0:T(8,128)(2,1)S(1)}, u32[]{:S(2)}, u32[]{:S(2)}) collective-permute-start(bf16[4,32,128]{2,1,0:T(8,128)(2,1)S(1)} %shard_map.73._after.refs_0_), channel_id=1, source_target_pairs={{0,24},{4,28},{8,0},{12,4},{16,8},{20,12},{24,16},{28,20},{32,56},... | collective-permute-start | bytes 98312 | tf_op jit(solution)/shard_map/ppermute | solution.py:71
  4.0 6.3 %collective-permute-start.1 = (bf16[4,32,128]{2,1,0:T(8,128)(2,1)S(1)}, bf16[4,32,128]{2,1,0:T(8,128)(2,1)S(1)}, u32[]{:S(2)}, u32[]{:S(2)}) collective-permute-start(bf16[4,32,128]{2,1,0:T(8,128)(2,1)S(1)} %shard_map.73._after.refs_0_), channel_id=1, source_target_pairs={{0,16},{4,20},{8,24},{12,28},{16,0},{20,4},{24,8},{28,12},{32,48},... | collective-permute-start | bytes 98312 | tf_op jit(solution)/shard_map/ppermute | solution.py:71
  4.6 5.7 %collective-permute-start = (bf16[4,32,128]{2,1,0:T(8,128)(2,1)S(1)}, bf16[4,32,128]{2,1,0:T(8,128)(2,1)S(1)}, u32[]{:S(2)}, u32[]{:S(2)}) collective-permute-start(bf16[4,32,128]{2,1,0:T(8,128)(2,1)S(1)} %shard_map.73._after.refs_0_), channel_id=1, source_target_pairs={{0,8},{4,12},{8,16},{12,20},{16,24},{20,28},{24,0},{28,4},{32,40},... | collective-permute-start | bytes 98312 | tf_op jit(solution)/shard_map/ppermute | solution.py:71
  10.3 7.6 %collective-permute-start.5 = (bf16[16,32,128]{2,1,0:T(8,128)(2,1)S(1)}, bf16[16,32,128]{2,1,0:T(8,128)(2,1)S(1)}, u32[]{:S(2)}, u32[]{:S(2)}) collective-permute-start(bf16[16,32,128]{2,1,0:T(8,128)(2,1)S(1)} %shard_map.75._after.refs_0_), channel_id=1, source_target_pairs={{0,96},{4,100},{8,104},{12,108},{16,112},{20,116},{24,120},{28,124... | collective-permute-start | bytes 393224 | tf_op jit(solution)/shard_map/ppermute | solution.py:75
  13.1 7.0 %collective-permute-start.4 = (bf16[16,32,128]{2,1,0:T(8,128)(2,1)S(1)}, bf16[16,32,128]{2,1,0:T(8,128)(2,1)S(1)}, u32[]{:S(2)}, u32[]{:S(2)}) collective-permute-start(bf16[16,32,128]{2,1,0:T(8,128)(2,1)S(1)} %shard_map.75._after.refs_0_), channel_id=1, source_target_pairs={{0,64},{4,68},{8,72},{12,76},{16,80},{20,84},{24,88},{28,92},{32,9... | collective-permute-start | bytes 393224 | tf_op jit(solution)/shard_map/ppermute | solution.py:75
  13.9 7.6 %collective-permute-start.3 = (bf16[16,32,128]{2,1,0:T(8,128)(2,1)S(1)}, bf16[16,32,128]{2,1,0:T(8,128)(2,1)S(1)}, u32[]{:S(2)}, u32[]{:S(2)}) collective-permute-start(bf16[16,32,128]{2,1,0:T(8,128)(2,1)S(1)} %shard_map.75._after.refs_0_), channel_id=1, source_target_pairs={{0,32},{4,36},{8,40},{12,44},{16,48},{20,52},{24,56},{28,60},{32,6... | collective-permute-start | bytes 393224 | tf_op jit(solution)/shard_map/ppermute | solution.py:75
  21.6 2.0 %collective-permute-start.6 = (bf16[64,32,128]{2,1,0:T(8,128)(2,1)S(1)}, bf16[64,32,128]{2,1,0:T(8,128)(2,1)S(1)}, u32[]{:S(2)}, u32[]{:S(2)}) collective-permute-start(bf16[64,32,128]{2,1,0:T(8,128)(2,1)S(1)} %shard_map.77.refs_0_), channel_id=1, source_target_pairs={{0,4},{4,0},{8,12},{12,8},{16,20},{20,16},{24,28},{28,24},{32,36},... | collective-permute-start | bytes 1572872 | tf_op jit(solution)/shard_map/ppermute | solution.py:76
  23.7 12.5 %copy-start.1 = (f32[4,32,128]{2,1,0:T(8,128)S(1)}, f32[4,32,128]{2,1,0:T(8,128)}, u32[]{:S(2)}) copy-start(f32[4,32,128]{2,1,0:T(8,128)} %previous.1) | copy-start | bytes 196612
  24.4 8.4 %collective-permute-start.9 = (f32[4,32,128]{2,1,0:T(8,128)S(1)}, f32[4,32,128]{2,1,0:T(8,128)S(1)}, u32[]{:S(2)}, u32[]{:S(2)}) collective-permute-start(f32[4,32,128]{2,1,0:T(8,128)S(1)} %shard_map.81.refs_0_), channel_id=1, source_target_pairs={{0,3},{1,0},{2,1},{3,2},{4,7},{5,4},{6,5},{7,6},{8,11},{9,8},{10,9... | collective-permute-start | bytes 196616 | tf_op jit(solution)/shard_map/ppermute | solution.py:270
  29.1 6.5 %collective-permute-start.8 = (f32[4,32,128]{2,1,0:T(8,128)S(1)}, f32[4,32,128]{2,1,0:T(8,128)S(1)}, u32[]{:S(2)}, u32[]{:S(2)}) collective-permute-start(f32[4,32,128]{2,1,0:T(8,128)S(1)} %shard_map.80.refs_0_), channel_id=1, source_target_pairs={{0,2},{1,3},{2,0},{3,1},{4,6},{5,7},{6,4},{7,5},{8,10},{9,11},{10,... | collective-permute-start | bytes 196616 | tf_op jit(solution)/shard_map/ppermute | solution.py:270
  29.6 6.7 %collective-permute-start.7 = (f32[4,32,128]{2,1,0:T(8,128)S(1)}, f32[4,32,128]{2,1,0:T(8,128)S(1)}, u32[]{:S(2)}, u32[]{:S(2)}) collective-permute-start(f32[4,32,128]{2,1,0:T(8,128)S(1)} %shard_map.79.refs_0_), channel_id=1, source_target_pairs={{0,1},{1,2},{2,3},{3,0},{4,5},{5,6},{6,7},{7,4},{8,9},{9,10},{10,1... | collective-permute-start | bytes 196616 | tf_op jit(solution)/shard_map/ppermute | solution.py:270
  36.3 4.5 %collective-permute-start.12 = (bf16[4,32,128]{2,1,0:T(8,128)(2,1)S(1)}, bf16[4,32,128]{2,1,0:T(8,128)(2,1)S(1)}, u32[]{:S(2)}, u32[]{:S(2)}) collective-permute-start(bf16[4,32,128]{2,1,0:T(8,128)(2,1)S(1)} %get-tuple-element.14.refs_0_), channel_id=1, source_target_pairs={{0,24},{4,28},{8,0},{12,4},{16,8},{20,12},{24,16},{28,20},{32,56},... | collective-permute-start | bytes 98312 | tf_op jit(solution)/shard_map/ppermute | solution.py:71
  39.2 5.4 %collective-permute-start.11 = (bf16[4,32,128]{2,1,0:T(8,128)(2,1)S(1)}, bf16[4,32,128]{2,1,0:T(8,128)(2,1)S(1)}, u32[]{:S(2)}, u32[]{:S(2)}) collective-permute-start(bf16[4,32,128]{2,1,0:T(8,128)(2,1)S(1)} %get-tuple-element.14.refs_0_), channel_id=1, source_target_pairs={{0,16},{4,20},{8,24},{12,28},{16,0},{20,4},{24,8},{28,12},{32,48},... | collective-permute-start | bytes 98312 | tf_op jit(solution)/shard_map/ppermute | solution.py:71
  40.2 5.1 %collective-permute-start.10 = (bf16[4,32,128]{2,1,0:T(8,128)(2,1)S(1)}, bf16[4,32,128]{2,1,0:T(8,128)(2,1)S(1)}, u32[]{:S(2)}, u32[]{:S(2)}) collective-permute-start(bf16[4,32,128]{2,1,0:T(8,128)(2,1)S(1)} %get-tuple-element.14.refs_0_), channel_id=1, source_target_pairs={{0,8},{4,12},{8,16},{12,20},{16,24},{20,28},{24,0},{28,4},{32,40},... | collective-permute-start | bytes 98312 | tf_op jit(solution)/shard_map/ppermute | solution.py:71
  45.3 7.0 %collective-permute-start.15 = (bf16[16,32,128]{2,1,0:T(8,128)(2,1)S(1)}, bf16[16,32,128]{2,1,0:T(8,128)(2,1)S(1)}, u32[]{:S(2)}, u32[]{:S(2)}) collective-permute-start(bf16[16,32,128]{2,1,0:T(8,128)(2,1)S(1)} %shard_map.84.refs_0_), channel_id=1, source_target_pairs={{0,96},{4,100},{8,104},{12,108},{16,112},{20,116},{24,120},{28,124... | collective-permute-start | bytes 393224 | tf_op jit(solution)/shard_map/ppermute | solution.py:75
  48.5 6.6 %collective-permute-start.14 = (bf16[16,32,128]{2,1,0:T(8,128)(2,1)S(1)}, bf16[16,32,128]{2,1,0:T(8,128)(2,1)S(1)}, u32[]{:S(2)}, u32[]{:S(2)}) collective-permute-start(bf16[16,32,128]{2,1,0:T(8,128)(2,1)S(1)} %shard_map.84.refs_0_), channel_id=1, source_target_pairs={{0,64},{4,68},{8,72},{12,76},{16,80},{20,84},{24,88},{28,92},{32,9... | collective-permute-start | bytes 393224 | tf_op jit(solution)/shard_map/ppermute | solution.py:75
  48.5 7.6 %collective-permute-start.13 = (bf16[16,32,128]{2,1,0:T(8,128)(2,1)S(1)}, bf16[16,32,128]{2,1,0:T(8,128)(2,1)S(1)}, u32[]{:S(2)}, u32[]{:S(2)}) collective-permute-start(bf16[16,32,128]{2,1,0:T(8,128)(2,1)S(1)} %shard_map.84.refs_0_), channel_id=1, source_target_pairs={{0,32},{4,36},{8,40},{12,44},{16,48},{20,52},{24,56},{28,60},{32,6... | collective-permute-start | bytes 393224 | tf_op jit(solution)/shard_map/ppermute | solution.py:75
  56.1 2.0 %collective-permute-start.16 = (bf16[64,32,128]{2,1,0:T(8,128)(2,1)S(1)}, bf16[64,32,128]{2,1,0:T(8,128)(2,1)S(1)}, u32[]{:S(2)}, u32[]{:S(2)}) collective-permute-start(bf16[64,32,128]{2,1,0:T(8,128)(2,1)S(1)} %shard_map.85.refs_0_), channel_id=1, source_target_pairs={{0,4},{4,0},{8,12},{12,8},{16,20},{20,16},{24,28},{28,24},{32,36},... | collective-permute-start | bytes 1572872 | tf_op jit(solution)/shard_map/ppermute | solution.py:76
  58.8 4.7 %collective-permute-start.19 = (f32[4,32,128]{2,1,0:T(8,128)S(1)}, f32[4,32,128]{2,1,0:T(8,128)S(1)}, u32[]{:S(2)}, u32[]{:S(2)}) collective-permute-start(f32[4,32,128]{2,1,0:T(8,128)S(1)} %shard_map.89.refs_0_), channel_id=1, source_target_pairs={{0,3},{1,0},{2,1},{3,2},{4,7},{5,4},{6,5},{7,6},{8,11},{9,8},{10,9... | collective-permute-start | bytes 196616 | tf_op jit(solution)/shard_map/ppermute | solution.py:270
  59.4 6.4 %collective-permute-start.18 = (f32[4,32,128]{2,1,0:T(8,128)S(1)}, f32[4,32,128]{2,1,0:T(8,128)S(1)}, u32[]{:S(2)}, u32[]{:S(2)}) collective-permute-start(f32[4,32,128]{2,1,0:T(8,128)S(1)} %shard_map.88.refs_0_), channel_id=1, source_target_pairs={{0,2},{1,3},{2,0},{3,1},{4,6},{5,7},{6,4},{7,5},{8,10},{9,11},{10,... | collective-permute-start | bytes 196616 | tf_op jit(solution)/shard_map/ppermute | solution.py:270
  61.6 5.8 %collective-permute-start.17 = (f32[4,32,128]{2,1,0:T(8,128)S(1)}, f32[4,32,128]{2,1,0:T(8,128)S(1)}, u32[]{:S(2)}, u32[]{:S(2)}) collective-permute-start(f32[4,32,128]{2,1,0:T(8,128)S(1)} %shard_map.87.refs_0_), channel_id=1, source_target_pairs={{0,1},{1,2},{2,3},{3,0},{4,5},{5,6},{6,7},{7,4},{8,9},{9,10},{10,1... | collective-permute-start | bytes 196616 | tf_op jit(solution)/shard_map/ppermute | solution.py:270
  67.4 4.0 %collective-permute-start.22 = (bf16[4,32,128]{2,1,0:T(8,128)(2,1)S(1)}, bf16[4,32,128]{2,1,0:T(8,128)(2,1)S(1)}, u32[]{:S(2)}, u32[]{:S(2)}) collective-permute-start(bf16[4,32,128]{2,1,0:T(8,128)(2,1)S(1)} %get-tuple-element.16.refs_0_), channel_id=1, source_target_pairs={{0,24},{4,28},{8,0},{12,4},{16,8},{20,12},{24,16},{28,20},{32,56},... | collective-permute-start | bytes 98312 | tf_op jit(solution)/shard_map/ppermute | solution.py:71
  69.8 5.5 %collective-permute-start.21 = (bf16[4,32,128]{2,1,0:T(8,128)(2,1)S(1)}, bf16[4,32,128]{2,1,0:T(8,128)(2,1)S(1)}, u32[]{:S(2)}, u32[]{:S(2)}) collective-permute-start(bf16[4,32,128]{2,1,0:T(8,128)(2,1)S(1)} %get-tuple-element.16.refs_0_), channel_id=1, source_target_pairs={{0,16},{4,20},{8,24},{12,28},{16,0},{20,4},{24,8},{28,12},{32,48},... | collective-permute-start | bytes 98312 | tf_op jit(solution)/shard_map/ppermute | solution.py:71
  69.8 5.5 %collective-permute-start.20 = (bf16[4,32,128]{2,1,0:T(8,128)(2,1)S(1)}, bf16[4,32,128]{2,1,0:T(8,128)(2,1)S(1)}, u32[]{:S(2)}, u32[]{:S(2)}) collective-permute-start(bf16[4,32,128]{2,1,0:T(8,128)(2,1)S(1)} %get-tuple-element.16.refs_0_), channel_id=1, source_target_pairs={{0,8},{4,12},{8,16},{12,20},{16,24},{20,28},{24,0},{28,4},{32,40},... | collective-permute-start | bytes 98312 | tf_op jit(solution)/shard_map/ppermute | solution.py:71
  75.3 5.0 %collective-permute-start.25 = (bf16[16,32,128]{2,1,0:T(8,128)(2,1)S(1)}, bf16[16,32,128]{2,1,0:T(8,128)(2,1)S(1)}, u32[]{:S(2)}, u32[]{:S(2)}) collective-permute-start(bf16[16,32,128]{2,1,0:T(8,128)(2,1)S(1)} %shard_map.92.refs_0_), channel_id=1, source_target_pairs={{0,96},{4,100},{8,104},{12,108},{16,112},{20,116},{24,120},{28,124... | collective-permute-start | bytes 393224 | tf_op jit(solution)/shard_map/ppermute | solution.py:75
  76.6 6.6 %collective-permute-start.24 = (bf16[16,32,128]{2,1,0:T(8,128)(2,1)S(1)}, bf16[16,32,128]{2,1,0:T(8,128)(2,1)S(1)}, u32[]{:S(2)}, u32[]{:S(2)}) collective-permute-start(bf16[16,32,128]{2,1,0:T(8,128)(2,1)S(1)} %shard_map.92.refs_0_), channel_id=1, source_target_pairs={{0,64},{4,68},{8,72},{12,76},{16,80},{20,84},{24,88},{28,92},{32,9... | collective-permute-start | bytes 393224 | tf_op jit(solution)/shard_map/ppermute | solution.py:75
  76.8 7.6 %collective-permute-start.23 = (bf16[16,32,128]{2,1,0:T(8,128)(2,1)S(1)}, bf16[16,32,128]{2,1,0:T(8,128)(2,1)S(1)}, u32[]{:S(2)}, u32[]{:S(2)}) collective-permute-start(bf16[16,32,128]{2,1,0:T(8,128)(2,1)S(1)} %shard_map.92.refs_0_), channel_id=1, source_target_pairs={{0,32},{4,36},{8,40},{12,44},{16,48},{20,52},{24,56},{28,60},{32,6... | collective-permute-start | bytes 393224 | tf_op jit(solution)/shard_map/ppermute | solution.py:75
  84.4 2.0 %collective-permute-start.26 = (bf16[64,32,128]{2,1,0:T(8,128)(2,1)S(1)}, bf16[64,32,128]{2,1,0:T(8,128)(2,1)S(1)}, u32[]{:S(2)}, u32[]{:S(2)}) collective-permute-start(bf16[64,32,128]{2,1,0:T(8,128)(2,1)S(1)} %shard_map.93.refs_0_), channel_id=1, source_target_pairs={{0,4},{4,0},{8,12},{12,8},{16,20},{20,16},{24,28},{28,24},{32,36},... | collective-permute-start | bytes 1572872 | tf_op jit(solution)/shard_map/ppermute | solution.py:76
  87.2 4.7 %collective-permute-start.29 = (f32[4,32,128]{2,1,0:T(8,128)S(1)}, f32[4,32,128]{2,1,0:T(8,128)S(1)}, u32[]{:S(2)}, u32[]{:S(2)}) collective-permute-start(f32[4,32,128]{2,1,0:T(8,128)S(1)} %shard_map.97.refs_0_), channel_id=1, source_target_pairs={{0,3},{1,0},{2,1},{3,2},{4,7},{5,4},{6,5},{7,6},{8,11},{9,8},{10,9... | collective-permute-start | bytes 196616 | tf_op jit(solution)/shard_map/ppermute | solution.py:270
  88.8 6.0 %collective-permute-start.28 = (f32[4,32,128]{2,1,0:T(8,128)S(1)}, f32[4,32,128]{2,1,0:T(8,128)S(1)}, u32[]{:S(2)}, u32[]{:S(2)}) collective-permute-start(f32[4,32,128]{2,1,0:T(8,128)S(1)} %shard_map.96.refs_0_), channel_id=1, source_target_pairs={{0,2},{1,3},{2,0},{3,1},{4,6},{5,7},{6,4},{7,5},{8,10},{9,11},{10,... | collective-permute-start | bytes 196616 | tf_op jit(solution)/shard_map/ppermute | solution.py:270
  90.3 5.8 %collective-permute-start.27 = (f32[4,32,128]{2,1,0:T(8,128)S(1)}, f32[4,32,128]{2,1,0:T(8,128)S(1)}, u32[]{:S(2)}, u32[]{:S(2)}) collective-permute-start(f32[4,32,128]{2,1,0:T(8,128)S(1)} %shard_map.95.refs_0_), channel_id=1, source_target_pairs={{0,1},{1,2},{2,3},{3,0},{4,5},{5,6},{6,7},{7,4},{8,9},{9,10},{10,1... | collective-permute-start | bytes 196616 | tf_op jit(solution)/shard_map/ppermute | solution.py:270

commit v2 on v1

--- a/solution.py
+++ b/solution.py
@@ -16,6 +16,7 @@
 BATCH = 24
 LANES = 256
 HEAD = 2 * LANES
+PART_ORDER = (2, 1, 3)
 MIB = 1 << 20
 
 
@@ -86,11 +87,20 @@
     return lax.broadcasted_iota(jnp.int32, shape, dim)
 
 
-def plan_kernel(parts, owned, live_ref, rows_ref, cols_ref, _center, _half, _after, place_out, table_out, place_ref, table_ref, sems):
+def plan_kernel(parts, owned, live_ref, rows_hbm, cols_hbm, center, half_width, _after, *refs):
+    place_out, table_out, center_out, half_out, rows_ref, cols_ref, place_ref, table_ref, sems = refs
+    pairs = ((rows_hbm, rows_ref), (cols_hbm, cols_ref))
+    fetches = [pltpu.make_async_copy(source, target, sems.at[2 + k]) for k, (source, target) in enumerate(pairs)]
+    for fetch in fetches:
+        fetch.start()
+    center_out[0] = center[...]
+    half_out[0] = half_width[...]
+    for fetch in fetches:
+        fetch.wait()
     live = live_ref[0]
     me, here = lax.axis_index("row"), lax.axis_index("col")
-    rows, cols = rows_ref[...], cols_ref[...]
-    slots = rows.shape[1]
+    slots = rows_ref.shape[0]
+    rows, cols = rows_ref[...].reshape(1, slots), cols_ref[...].reshape(1, slots)
     span = parts * owned
     lanes = LANES
     head = HEAD
@@ -143,15 +153,19 @@
     slots = rows.shape[0]
     room = padded_room(slots, parts * owned)
     widths = (slots, HEAD + room + SPARE)
+    anywhere = pl.BlockSpec(memory_space=pltpu.HBM)
+    rows, cols = (pltpu.with_memory_space_constraint(a, pltpu.HBM) for a in (rows, cols))
     return pl.pallas_call(
         functools.partial(plan_kernel, parts, owned),
-        out_shape=[pltpu.SMEM((1, width), jnp.int32) for width in widths],
-        in_specs=[SMEM, VMEM, VMEM, SMEM, SMEM, VMEM],
-        out_specs=[SMEM] * len(widths),
-        scratch_shapes=[pltpu.VMEM((1, width), jnp.int32) for width in widths] + [pltpu.SemaphoreType.DMA((2,))],
+        out_shape=[pltpu.SMEM((1, width), jnp.int32) for width in widths] + [pltpu.SMEM((1,), jnp.float32)] * 2,
+        in_specs=[SMEM, anywhere, anywhere, SMEM, SMEM, VMEM],
+        out_specs=[SMEM] * 4,
+        scratch_shapes=[pltpu.VMEM((slots,), jnp.int32)] * 2
+        + [pltpu.VMEM((1, width), jnp.int32) for width in widths]
+        + [pltpu.SemaphoreType.DMA((4,))],
         compiler_params=pltpu.CompilerParams(vmem_limit_bytes=8 * MIB),
         cost_estimate=pl.CostEstimate(flops=1000, bytes_accessed=1000, transcendentals=0),
-    )(live, rows.reshape(1, slots), cols.reshape(1, slots), *scalars, after)
+    )(live, rows, cols, *scalars, after)
 
 
 def prepare_kernel(span, place, sizes, _after, blocks_hbm, store, raw, sems):
@@ -258,12 +272,12 @@
     parts = lax.axis_size("col")
     owned = start_vectors.shape[0]
     shape = start_vectors.shape
-    scalars = (center.reshape(1), half_width.reshape(1))
+    scalars = (center, half_width)
     outs = (jax.ShapeDtypeStruct(shape, jnp.float32), jax.ShapeDtypeStruct(shape, jnp.bfloat16))
 
     def image_pieces(vec):
         pieces, last = [], ()
-        for part in (*range(1, parts), 0):
+        for part in (*PART_ORDER, 0):
             piece = local_products(part, vec, prep, last, owned, parts)
             last = (piece,)
             if part:
@@ -272,7 +286,7 @@
         return pieces
 
     start_bf = rounded(start_vectors)
-    place, table = sort_plan(block_rows, block_cols, live_counts, scalars, start_bf, parts, owned)
+    place, table, *scalars = sort_plan(block_rows, block_cols, live_counts, scalars, start_bf, parts, owned)
     line = line_gathered(start_bf, (table,), (SMEM,))
     store = prepared(place, table, blocks, line, parts * owned)
     prep = (table, store)

time: 98.1 us -> 97 us (0.989)
  starting transfers between devices: 37.2 us -> 41.2 us
  waiting for transfers between devices: 47 us -> 43.4 us
  local copies, waits for them, and re-layouts: 2.23 us -> 0.85 us
    ppermute x9, starting transfers between devices: 13.5 us -> 17.4 us  [image_pieces(): lax.ppermute(piece, 'col', [(i, (i + part) % parts) for i in range(parts)])]
    ppermute x9, waiting for transfers between devices: 13.8 us -> 11.6 us  [image_pieces(): lax.ppermute(piece, 'col', [(i, (i + part) % parts) for i in range(parts)])]
    ppermute x9, waiting for transfers between devices: 17.9 us -> 16.4 us  [all_gathered(): lax.ppermute(line, 'row', chip_shifts(dx, 0))]
    reshape x2 -> x0, local copies, waits for them, and re-layouts: 1.38 us -> none  [the longest x1 0.69 us: sort_plan(): rows.reshape(1, slots)]
  transfers between devices with their start and end apart: 30 -> 30, of which waited for: 26 -> 22; matrix products, arithmetic and copies ran while one was open for 1% -> 0% of each run, Pallas kernels for 5% -> 6%
where the time goes in v2:
time: 97 us; the launch traced here: 96.6 us
  waiting for transfers between devices  43.4 us (45%)
  starting transfers between devices  41.2 us (42%)
  Pallas kernels  8.87 us (9%)
  between operations  2.2 us (2%)
    ppermute x9, starting transfers between devices, image_pieces(): lax.ppermute(piece, 'col', [(i, (i + part) % parts) for i in range(parts)])  17.4 us
    ppermute x9, waiting for transfers between devices, all_gathered(): lax.ppermute(line, 'row', chip_shifts(dx, 0))  16.4 us
    ppermute x9, starting transfers between devices, line_gathered(): lax.ppermute(owned, 'row', chip_shifts(0, dy))  12.4 us
    ppermute x9, waiting for transfers between devices, image_pieces(): lax.ppermute(piece, 'col', [(i, (i + part) % parts) for i in range(parts)])  11.6 us
    ppermute x9, starting transfers between devices, all_gathered(): lax.ppermute(line, 'row', chip_shifts(dx, 0))  11.2 us
    ppermute x9, waiting for transfers between devices, line_gathered(): lax.ppermute(owned, 'row', chip_shifts(0, dy))  9.75 us
    ppermute x3, waiting for transfers between devices, all_gathered(): theirs = lax.ppermute(mine, 'row', chip_shifts(0, 0, 1))  5.69 us
    pallas_call x12, Pallas kernels, local_products(): pl.pallas_call(functools.partial(products_kernel, part * owned), out_shap...  4.01 us
  transfers between devices with their start and end apart: 30, of which 22 were waited for; matrix products, arithmetic and copies ran while one was open for 0% of the time, Pallas kernels for 6%

profile of v2, /device:TPU:0, one launch (start us, length us, event | category | flops | bytes accessed | tf_op | source)
XLA Modules:
  0.0 96.6 jit_solution(13376314024317057085)
XLA Ops:
  0.8 3.1 %collective-permute-start.2 = (bf16[4,32,128]{2,1,0:T(8,128)(2,1)S(1)}, bf16[4,32,128]{2,1,0:T(8,128)(2,1)S(1)}, u32[]{:S(2)}, u32[]{:S(2)}) collective-permute-start(bf16[4,32,128]{2,1,0:T(8,128)(2,1)S(1)} %shard_map.73._after.refs_0_), channel_id=1, source_target_pairs={{0,24},{4,28},{8,0},{12,4},{16,8},{20,12},{24,16},{28,20},{32,56},... | collective-permute-start | bytes 98312 | tf_op jit(solution)/shard_map/ppermute | solution.py:72
  7.5 2.1 %shard_map.74 = (s32[1,640]{1,0:T(1,128)S(4)}, s32[1,1344]{1,0:T(1,128)S(4)}, f32[1]{0:T(128)S(4)}, f32[1]{0:T(128)S(4)}) custom-call(s32[1]{0:T(128)S(6)} %copy.8.live_ref, s32[640]{0:T(1024)} %rows_hbm.1, s32[640]{0:T(1024)} %cols_hbm.1, f32[]{:T(128)S(6)} %copy.9.center, f32[]{:T(128)S(6)} %copy.10.half_width, ...), custom_call_target="tpu_custom_call" | custom-call | flops 1000 | bytes 1000 | tf_op jit(solution)/shard_map/pallas_call | solution.py:158
  9.8 2.8 %collective-permute-start.5 = (bf16[16,32,128]{2,1,0:T(8,128)(2,1)S(1)}, bf16[16,32,128]{2,1,0:T(8,128)(2,1)S(1)}, u32[]{:S(2)}, u32[]{:S(2)}) collective-permute-start(bf16[16,32,128]{2,1,0:T(8,128)(2,1)S(1)} %shard_map.75._after.refs_0_), channel_id=1, source_target_pairs={{0,96},{4,100},{8,104},{12,108},{16,112},{20,116},{24,120},{28,124... | collective-permute-start | bytes 393224 | tf_op jit(solution)/shard_map/ppermute | solution.py:76
  14.3 1.7 %shard_map.76.refs_4_.store = bf16[832,128,128]{2,1,0:T(8,128)(2,1)S(1)} custom-call(s32[1,640]{1,0:T(1,128)S(4)} %get-tuple-element.16.place, s32[1,1344]{1,0:T(1,128)S(4)} %get-tuple-element.15.refs_4_.sizes.table, bf16[16,32,128]{2,1,0:T(8,128)(2,1)S(1)} %shard_map.75._after.refs_0_, bf16[640,128,128]{2,1,0:T(8,128)(2,1)} %blocks_hbm.1), custom_call_target="tpu_custom_call" | custom-call | flops 1000 | bytes 20971520 | tf_op jit(solution)/shard_map/pallas_call | solution.py:200
  16.0 1.3 %collective-permute-done.5.refs_3_ = bf16[16,32,128]{2,1,0:T(8,128)(2,1)S(1)} collective-permute-done((bf16[16,32,128]{2,1,0:T(8,128)(2,1)S(1)}, bf16[16,32,128]{2,1,0:T(8,128)(2,1)S(1)}, u32[]{:S(2)}, u32[]{:S(2)}) %collective-permute-start.5) | collective-permute-done | bytes 131104 | tf_op jit(solution)/shard_map/ppermute | solution.py:76
  17.3 2.2 %collective-permute-done.4.refs_2_ = bf16[16,32,128]{2,1,0:T(8,128)(2,1)S(1)} collective-permute-done((bf16[16,32,128]{2,1,0:T(8,128)(2,1)S(1)}, bf16[16,32,128]{2,1,0:T(8,128)(2,1)S(1)}, u32[]{:S(2)}, u32[]{:S(2)}) %collective-permute-start.4) | collective-permute-done | bytes 131104 | tf_op jit(solution)/shard_map/ppermute | solution.py:76
  19.5 1.4 %collective-permute-done.3.refs_1_ = bf16[16,32,128]{2,1,0:T(8,128)(2,1)S(1)} collective-permute-done((bf16[16,32,128]{2,1,0:T(8,128)(2,1)S(1)}, bf16[16,32,128]{2,1,0:T(8,128)(2,1)S(1)}, u32[]{:S(2)}, u32[]{:S(2)}) %collective-permute-start.3) | collective-permute-done | bytes 131104 | tf_op jit(solution)/shard_map/ppermute | solution.py:76
  21.1 1.9 %collective-permute-done.6.refs_1_ = bf16[64,32,128]{2,1,0:T(8,128)(2,1)S(1)} collective-permute-done((bf16[64,32,128]{2,1,0:T(8,128)(2,1)S(1)}, bf16[64,32,128]{2,1,0:T(8,128)(2,1)S(1)}, u32[]{:S(2)}, u32[]{:S(2)}) %collective-permute-start.6) | collective-permute-done | bytes 524320 | tf_op jit(solution)/shard_map/ppermute | solution.py:77
  23.7 4.7 %collective-permute-start.9 = (f32[4,32,128]{2,1,0:T(8,128)S(1)}, f32[4,32,128]{2,1,0:T(8,128)S(1)}, u32[]{:S(2)}, u32[]{:S(2)}) collective-permute-start(f32[4,32,128]{2,1,0:T(8,128)S(1)} %shard_map.81.refs_0_), channel_id=1, source_target_pairs={{0,3},{1,0},{2,1},{3,2},{4,7},{5,4},{6,5},{7,6},{8,11},{9,8},{10,9... | collective-permute-start | bytes 196616 | tf_op jit(solution)/shard_map/ppermute | solution.py:284
  28.4 2.5 %collective-permute-start.7 = (f32[4,32,128]{2,1,0:T(8,128)S(1)}, f32[4,32,128]{2,1,0:T(8,128)S(1)}, u32[]{:S(2)}, u32[]{:S(2)}) collective-permute-start(f32[4,32,128]{2,1,0:T(8,128)S(1)} %shard_map.79.refs_0_), channel_id=1, source_target_pairs={{0,2},{1,3},{2,0},{3,1},{4,6},{5,7},{6,4},{7,5},{8,10},{9,11},{10,... | collective-permute-start | bytes 196616 | tf_op jit(solution)/shard_map/ppermute | solution.py:284
  31.5 4.0 %collective-permute-done.8.refs_1_ = f32[4,32,128]{2,1,0:T(8,128)S(1)} collective-permute-done((f32[4,32,128]{2,1,0:T(8,128)S(1)}, f32[4,32,128]{2,1,0:T(8,128)S(1)}, u32[]{:S(2)}, u32[]{:S(2)}) %collective-permute-start.8) | collective-permute-done | bytes 65568 | tf_op jit(solution)/shard_map/ppermute | solution.py:284
  35.5 3.0 %collective-permute-start.12 = (bf16[4,32,128]{2,1,0:T(8,128)(2,1)S(1)}, bf16[4,32,128]{2,1,0:T(8,128)(2,1)S(1)}, u32[]{:S(2)}, u32[]{:S(2)}) collective-permute-start(bf16[4,32,128]{2,1,0:T(8,128)(2,1)S(1)} %get-tuple-element.18.refs_0_), channel_id=1, source_target_pairs={{0,24},{4,28},{8,0},{12,4},{16,8},{20,12},{24,16},{28,20},{32,56},... | collective-permute-start | bytes 98312 | tf_op jit(solution)/shard_map/ppermute | solution.py:72
  40.2 3.8 %collective-permute-done.11.refs_2_ = bf16[4,32,128]{2,1,0:T(8,128)(2,1)S(1)} collective-permute-done((bf16[4,32,128]{2,1,0:T(8,128)(2,1)S(1)}, bf16[4,32,128]{2,1,0:T(8,128)(2,1)S(1)}, u32[]{:S(2)}, u32[]{:S(2)}) %collective-permute-start.11) | collective-permute-done | bytes 32800 | tf_op jit(solution)/shard_map/ppermute | solution.py:72
  44.7 1.4 %collective-permute-start.15 = (bf16[16,32,128]{2,1,0:T(8,128)(2,1)S(1)}, bf16[16,32,128]{2,1,0:T(8,128)(2,1)S(1)}, u32[]{:S(2)}, u32[]{:S(2)}) collective-permute-start(bf16[16,32,128]{2,1,0:T(8,128)(2,1)S(1)} %shard_map.84.refs_0_), channel_id=1, source_target_pairs={{0,96},{4,100},{8,104},{12,108},{16,112},{20,116},{24,120},{28,124... | collective-permute-start | bytes 393224 | tf_op jit(solution)/shard_map/ppermute | solution.py:76
  47.0 1.3 %collective-permute-start.13 = (bf16[16,32,128]{2,1,0:T(8,128)(2,1)S(1)}, bf16[16,32,128]{2,1,0:T(8,128)(2,1)S(1)}, u32[]{:S(2)}, u32[]{:S(2)}) collective-permute-start(bf16[16,32,128]{2,1,0:T(8,128)(2,1)S(1)} %shard_map.84.refs_0_), channel_id=1, source_target_pairs={{0,32},{4,36},{8,40},{12,44},{16,48},{20,52},{24,56},{28,60},{32,6... | collective-permute-start | bytes 393224 | tf_op jit(solution)/shard_map/ppermute | solution.py:76
  48.4 1.4 %collective-permute-done.15.refs_3_ = bf16[16,32,128]{2,1,0:T(8,128)(2,1)S(1)} collective-permute-done((bf16[16,32,128]{2,1,0:T(8,128)(2,1)S(1)}, bf16[16,32,128]{2,1,0:T(8,128)(2,1)S(1)}, u32[]{:S(2)}, u32[]{:S(2)}) %collective-permute-start.15) | collective-permute-done | bytes 131104 | tf_op jit(solution)/shard_map/ppermute | solution.py:76
  49.8 2.9 %collective-permute-done.14.refs_2_ = bf16[16,32,128]{2,1,0:T(8,128)(2,1)S(1)} collective-permute-done((bf16[16,32,128]{2,1,0:T(8,128)(2,1)S(1)}, bf16[16,32,128]{2,1,0:T(8,128)(2,1)S(1)}, u32[]{:S(2)}, u32[]{:S(2)}) %collective-permute-start.14) | collective-permute-done | bytes 131104 | tf_op jit(solution)/shard_map/ppermute | solution.py:76
  52.7 1.3 %collective-permute-done.13.refs_1_ = bf16[16,32,128]{2,1,0:T(8,128)(2,1)S(1)} collective-permute-done((bf16[16,32,128]{2,1,0:T(8,128)(2,1)S(1)}, bf16[16,32,128]{2,1,0:T(8,128)(2,1)S(1)}, u32[]{:S(2)}, u32[]{:S(2)}) %collective-permute-start.13) | collective-permute-done | bytes 131104 | tf_op jit(solution)/shard_map/ppermute | solution.py:76
  54.1 1.9 %collective-permute-done.16.refs_1_ = bf16[64,32,128]{2,1,0:T(8,128)(2,1)S(1)} collective-permute-done((bf16[64,32,128]{2,1,0:T(8,128)(2,1)S(1)}, bf16[64,32,128]{2,1,0:T(8,128)(2,1)S(1)}, u32[]{:S(2)}, u32[]{:S(2)}) %collective-permute-start.16) | collective-permute-done | bytes 524320 | tf_op jit(solution)/shard_map/ppermute | solution.py:77
  56.8 2.4 %collective-permute-start.19 = (f32[4,32,128]{2,1,0:T(8,128)S(1)}, f32[4,32,128]{2,1,0:T(8,128)S(1)}, u32[]{:S(2)}, u32[]{:S(2)}) collective-permute-start(f32[4,32,128]{2,1,0:T(8,128)S(1)} %shard_map.89.refs_0_), channel_id=1, source_target_pairs={{0,3},{1,0},{2,1},{3,2},{4,7},{5,4},{6,5},{7,6},{8,11},{9,8},{10,9... | collective-permute-start | bytes 196616 | tf_op jit(solution)/shard_map/ppermute | solution.py:284
  59.8 2.3 %collective-permute-start.17 = (f32[4,32,128]{2,1,0:T(8,128)S(1)}, f32[4,32,128]{2,1,0:T(8,128)S(1)}, u32[]{:S(2)}, u32[]{:S(2)}) collective-permute-start(f32[4,32,128]{2,1,0:T(8,128)S(1)} %shard_map.87.refs_0_), channel_id=1, source_target_pairs={{0,2},{1,3},{2,0},{3,1},{4,6},{5,7},{6,4},{7,5},{8,10},{9,11},{10,... | collective-permute-start | bytes 196616 | tf_op jit(solution)/shard_map/ppermute | solution.py:284
  62.9 2.1 %collective-permute-done.18.refs_1_ = f32[4,32,128]{2,1,0:T(8,128)S(1)} collective-permute-done((f32[4,32,128]{2,1,0:T(8,128)S(1)}, f32[4,32,128]{2,1,0:T(8,128)S(1)}, u32[]{:S(2)}, u32[]{:S(2)}) %collective-permute-start.18) | collective-permute-done | bytes 65568 | tf_op jit(solution)/shard_map/ppermute | solution.py:284
  65.9 2.7 %collective-permute-start.22 = (bf16[4,32,128]{2,1,0:T(8,128)(2,1)S(1)}, bf16[4,32,128]{2,1,0:T(8,128)(2,1)S(1)}, u32[]{:S(2)}, u32[]{:S(2)}) collective-permute-start(bf16[4,32,128]{2,1,0:T(8,128)(2,1)S(1)} %get-tuple-element.20.refs_0_), channel_id=1, source_target_pairs={{0,24},{4,28},{8,0},{12,4},{16,8},{20,12},{24,16},{28,20},{32,56},... | collective-permute-start | bytes 98312 | tf_op jit(solution)/shard_map/ppermute | solution.py:72
  70.2 3.9 %collective-permute-done.21.refs_2_ = bf16[4,32,128]{2,1,0:T(8,128)(2,1)S(1)} collective-permute-done((bf16[4,32,128]{2,1,0:T(8,128)(2,1)S(1)}, bf16[4,32,128]{2,1,0:T(8,128)(2,1)S(1)}, u32[]{:S(2)}, u32[]{:S(2)}) %collective-permute-start.21) | collective-permute-done | bytes 32800 | tf_op jit(solution)/shard_map/ppermute | solution.py:72
  75.7 1.3 %collective-permute-start.23 = (bf16[16,32,128]{2,1,0:T(8,128)(2,1)S(1)}, bf16[16,32,128]{2,1,0:T(8,128)(2,1)S(1)}, u32[]{:S(2)}, u32[]{:S(2)}) collective-permute-start(bf16[16,32,128]{2,1,0:T(8,128)(2,1)S(1)} %shard_map.92.refs_0_), channel_id=1, source_target_pairs={{0,32},{4,36},{8,40},{12,44},{16,48},{20,52},{24,56},{28,60},{32,6... | collective-permute-start | bytes 393224 | tf_op jit(solution)/shard_map/ppermute | solution.py:76
  77.1 2.1 %collective-permute-done.25.refs_3_ = bf16[16,32,128]{2,1,0:T(8,128)(2,1)S(1)} collective-permute-done((bf16[16,32,128]{2,1,0:T(8,128)(2,1)S(1)}, bf16[16,32,128]{2,1,0:T(8,128)(2,1)S(1)}, u32[]{:S(2)}, u32[]{:S(2)}) %collective-permute-start.25) | collective-permute-done | bytes 131104 | tf_op jit(solution)/shard_map/ppermute | solution.py:76
  79.1 2.5 %collective-permute-done.24.refs_2_ = bf16[16,32,128]{2,1,0:T(8,128)(2,1)S(1)} collective-permute-done((bf16[16,32,128]{2,1,0:T(8,128)(2,1)S(1)}, bf16[16,32,128]{2,1,0:T(8,128)(2,1)S(1)}, u32[]{:S(2)}, u32[]{:S(2)}) %collective-permute-start.24) | collective-permute-done | bytes 131104 | tf_op jit(solution)/shard_map/ppermute | solution.py:76
  81.7 1.3 %collective-permute-done.23.refs_1_ = bf16[16,32,128]{2,1,0:T(8,128)(2,1)S(1)} collective-permute-done((bf16[16,32,128]{2,1,0:T(8,128)(2,1)S(1)}, bf16[16,32,128]{2,1,0:T(8,128)(2,1)S(1)}, u32[]{:S(2)}, u32[]{:S(2)}) %collective-permute-start.23) | collective-permute-done | bytes 131104 | tf_op jit(solution)/shard_map/ppermute | solution.py:76
  83.1 1.9 %collective-permute-done.26.refs_1_ = bf16[64,32,128]{2,1,0:T(8,128)(2,1)S(1)} collective-permute-done((bf16[64,32,128]{2,1,0:T(8,128)(2,1)S(1)}, bf16[64,32,128]{2,1,0:T(8,128)(2,1)S(1)}, u32[]{:S(2)}, u32[]{:S(2)}) %collective-permute-start.26) | collective-permute-done | bytes 524320 | tf_op jit(solution)/shard_map/ppermute | solution.py:77
  85.8 3.1 %collective-permute-start.29 = (f32[4,32,128]{2,1,0:T(8,128)S(1)}, f32[4,32,128]{2,1,0:T(8,128)S(1)}, u32[]{:S(2)}, u32[]{:S(2)}) collective-permute-start(f32[4,32,128]{2,1,0:T(8,128)S(1)} %shard_map.97.refs_0_), channel_id=1, source_target_pairs={{0,3},{1,0},{2,1},{3,2},{4,7},{5,4},{6,5},{7,6},{8,11},{9,8},{10,9... | collective-permute-start | bytes 196616 | tf_op jit(solution)/shard_map/ppermute | solution.py:284
  88.8 1.9 %collective-permute-start.27 = (f32[4,32,128]{2,1,0:T(8,128)S(1)}, f32[4,32,128]{2,1,0:T(8,128)S(1)}, u32[]{:S(2)}, u32[]{:S(2)}) collective-permute-start(f32[4,32,128]{2,1,0:T(8,128)S(1)} %shard_map.95.refs_0_), channel_id=1, source_target_pairs={{0,2},{1,3},{2,0},{3,1},{4,6},{5,7},{6,4},{7,5},{8,10},{9,11},{10,... | collective-permute-start | bytes 196616 | tf_op jit(solution)/shard_map/ppermute | solution.py:284
  91.3 4.6 %collective-permute-done.28.refs_1_ = f32[4,32,128]{2,1,0:T(8,128)S(1)} collective-permute-done((f32[4,32,128]{2,1,0:T(8,128)S(1)}, f32[4,32,128]{2,1,0:T(8,128)S(1)}, u32[]{:S(2)}, u32[]{:S(2)}) %collective-permute-start.28) | collective-permute-done | bytes 65568 | tf_op jit(solution)/shard_map/ppermute | solution.py:284
  (59 shorter events, 17.5 us)
Async XLA Ops:
  0.0 0.8 copy-start
  0.8 8.8 %collective-permute-start.2 = (bf16[4,32,128]{2,1,0:T(8,128)(2,1)S(1)}, bf16[4,32,128]{2,1,0:T(8,128)(2,1)S(1)}, u32[]{:S(2)}, u32[]{:S(2)}) collective-permute-start(bf16[4,32,128]{2,1,0:T(8,128)(2,1)S(1)} %shard_map.73._after.refs_0_), channel_id=1, source_target_pairs={{0,24},{4,28},{8,0},{12,4},{16,8},{20,12},{24,16},{28,20},{32,56},... | collective-permute-start | bytes 98312 | tf_op jit(solution)/shard_map/ppermute | solution.py:72
  4.0 5.7 %collective-permute-start.1 = (bf16[4,32,128]{2,1,0:T(8,128)(2,1)S(1)}, bf16[4,32,128]{2,1,0:T(8,128)(2,1)S(1)}, u32[]{:S(2)}, u32[]{:S(2)}) collective-permute-start(bf16[4,32,128]{2,1,0:T(8,128)(2,1)S(1)} %shard_map.73._after.refs_0_), channel_id=1, source_target_pairs={{0,16},{4,20},{8,24},{12,28},{16,0},{20,4},{24,8},{28,12},{32,48},... | collective-permute-start | bytes 98312 | tf_op jit(solution)/shard_map/ppermute | solution.py:72
  4.6 5.1 %collective-permute-start = (bf16[4,32,128]{2,1,0:T(8,128)(2,1)S(1)}, bf16[4,32,128]{2,1,0:T(8,128)(2,1)S(1)}, u32[]{:S(2)}, u32[]{:S(2)}) collective-permute-start(bf16[4,32,128]{2,1,0:T(8,128)(2,1)S(1)} %shard_map.73._after.refs_0_), channel_id=1, source_target_pairs={{0,8},{4,12},{8,16},{12,20},{16,24},{20,28},{24,0},{28,4},{32,40},... | collective-permute-start | bytes 98312 | tf_op jit(solution)/shard_map/ppermute | solution.py:72
  9.8 7.5 %collective-permute-start.5 = (bf16[16,32,128]{2,1,0:T(8,128)(2,1)S(1)}, bf16[16,32,128]{2,1,0:T(8,128)(2,1)S(1)}, u32[]{:S(2)}, u32[]{:S(2)}) collective-permute-start(bf16[16,32,128]{2,1,0:T(8,128)(2,1)S(1)} %shard_map.75._after.refs_0_), channel_id=1, source_target_pairs={{0,96},{4,100},{8,104},{12,108},{16,112},{20,116},{24,120},{28,124... | collective-permute-start | bytes 393224 | tf_op jit(solution)/shard_map/ppermute | solution.py:76
  12.6 6.9 %collective-permute-start.4 = (bf16[16,32,128]{2,1,0:T(8,128)(2,1)S(1)}, bf16[16,32,128]{2,1,0:T(8,128)(2,1)S(1)}, u32[]{:S(2)}, u32[]{:S(2)}) collective-permute-start(bf16[16,32,128]{2,1,0:T(8,128)(2,1)S(1)} %shard_map.75._after.refs_0_), channel_id=1, source_target_pairs={{0,64},{4,68},{8,72},{12,76},{16,80},{20,84},{24,88},{28,92},{32,9... | collective-permute-start | bytes 393224 | tf_op jit(solution)/shard_map/ppermute | solution.py:76
  13.4 7.5 %collective-permute-start.3 = (bf16[16,32,128]{2,1,0:T(8,128)(2,1)S(1)}, bf16[16,32,128]{2,1,0:T(8,128)(2,1)S(1)}, u32[]{:S(2)}, u32[]{:S(2)}) collective-permute-start(bf16[16,32,128]{2,1,0:T(8,128)(2,1)S(1)} %shard_map.75._after.refs_0_), channel_id=1, source_target_pairs={{0,32},{4,36},{8,40},{12,44},{16,48},{20,52},{24,56},{28,60},{32,6... | collective-permute-start | bytes 393224 | tf_op jit(solution)/shard_map/ppermute | solution.py:76
  21.0 2.0 %collective-permute-start.6 = (bf16[64,32,128]{2,1,0:T(8,128)(2,1)S(1)}, bf16[64,32,128]{2,1,0:T(8,128)(2,1)S(1)}, u32[]{:S(2)}, u32[]{:S(2)}) collective-permute-start(bf16[64,32,128]{2,1,0:T(8,128)(2,1)S(1)} %shard_map.77.refs_0_), channel_id=1, source_target_pairs={{0,4},{4,0},{8,12},{12,8},{16,20},{20,16},{24,28},{28,24},{32,36},... | collective-permute-start | bytes 1572872 | tf_op jit(solution)/shard_map/ppermute | solution.py:77
  23.1 12.4 %copy-start.1 = (f32[4,32,128]{2,1,0:T(8,128)S(1)}, f32[4,32,128]{2,1,0:T(8,128)}, u32[]{:S(2)}) copy-start(f32[4,32,128]{2,1,0:T(8,128)} %previous.1) | copy-start | bytes 196612
  23.7 7.8 %collective-permute-start.9 = (f32[4,32,128]{2,1,0:T(8,128)S(1)}, f32[4,32,128]{2,1,0:T(8,128)S(1)}, u32[]{:S(2)}, u32[]{:S(2)}) collective-permute-start(f32[4,32,128]{2,1,0:T(8,128)S(1)} %shard_map.81.refs_0_), channel_id=1, source_target_pairs={{0,3},{1,0},{2,1},{3,2},{4,7},{5,4},{6,5},{7,6},{8,11},{9,8},{10,9... | collective-permute-start | bytes 196616 | tf_op jit(solution)/shard_map/ppermute | solution.py:284
  28.4 7.1 %collective-permute-start.8 = (f32[4,32,128]{2,1,0:T(8,128)S(1)}, f32[4,32,128]{2,1,0:T(8,128)S(1)}, u32[]{:S(2)}, u32[]{:S(2)}) collective-permute-start(f32[4,32,128]{2,1,0:T(8,128)S(1)} %shard_map.80.refs_0_), channel_id=1, source_target_pairs={{0,1},{1,2},{2,3},{3,0},{4,5},{5,6},{6,7},{7,4},{8,9},{9,10},{10,1... | collective-permute-start | bytes 196616 | tf_op jit(solution)/shard_map/ppermute | solution.py:284
  28.4 7.1 %collective-permute-start.7 = (f32[4,32,128]{2,1,0:T(8,128)S(1)}, f32[4,32,128]{2,1,0:T(8,128)S(1)}, u32[]{:S(2)}, u32[]{:S(2)}) collective-permute-start(f32[4,32,128]{2,1,0:T(8,128)S(1)} %shard_map.79.refs_0_), channel_id=1, source_target_pairs={{0,2},{1,3},{2,0},{3,1},{4,6},{5,7},{6,4},{7,5},{8,10},{9,11},{10,... | collective-permute-start | bytes 196616 | tf_op jit(solution)/shard_map/ppermute | solution.py:284
  35.5 4.6 %collective-permute-start.12 = (bf16[4,32,128]{2,1,0:T(8,128)(2,1)S(1)}, bf16[4,32,128]{2,1,0:T(8,128)(2,1)S(1)}, u32[]{:S(2)}, u32[]{:S(2)}) collective-permute-start(bf16[4,32,128]{2,1,0:T(8,128)(2,1)S(1)} %get-tuple-element.18.refs_0_), channel_id=1, source_target_pairs={{0,24},{4,28},{8,0},{12,4},{16,8},{20,12},{24,16},{28,20},{32,56},... | collective-permute-start | bytes 98312 | tf_op jit(solution)/shard_map/ppermute | solution.py:72
  38.6 5.4 %collective-permute-start.11 = (bf16[4,32,128]{2,1,0:T(8,128)(2,1)S(1)}, bf16[4,32,128]{2,1,0:T(8,128)(2,1)S(1)}, u32[]{:S(2)}, u32[]{:S(2)}) collective-permute-start(bf16[4,32,128]{2,1,0:T(8,128)(2,1)S(1)} %get-tuple-element.18.refs_0_), channel_id=1, source_target_pairs={{0,16},{4,20},{8,24},{12,28},{16,0},{20,4},{24,8},{28,12},{32,48},... | collective-permute-start | bytes 98312 | tf_op jit(solution)/shard_map/ppermute | solution.py:72
  39.6 5.1 %collective-permute-start.10 = (bf16[4,32,128]{2,1,0:T(8,128)(2,1)S(1)}, bf16[4,32,128]{2,1,0:T(8,128)(2,1)S(1)}, u32[]{:S(2)}, u32[]{:S(2)}) collective-permute-start(bf16[4,32,128]{2,1,0:T(8,128)(2,1)S(1)} %get-tuple-element.18.refs_0_), channel_id=1, source_target_pairs={{0,8},{4,12},{8,16},{12,20},{16,24},{20,28},{24,0},{28,4},{32,40},... | collective-permute-start | bytes 98312 | tf_op jit(solution)/shard_map/ppermute | solution.py:72
  44.7 5.1 %collective-permute-start.15 = (bf16[16,32,128]{2,1,0:T(8,128)(2,1)S(1)}, bf16[16,32,128]{2,1,0:T(8,128)(2,1)S(1)}, u32[]{:S(2)}, u32[]{:S(2)}) collective-permute-start(bf16[16,32,128]{2,1,0:T(8,128)(2,1)S(1)} %shard_map.84.refs_0_), channel_id=1, source_target_pairs={{0,96},{4,100},{8,104},{12,108},{16,112},{20,116},{24,120},{28,124... | collective-permute-start | bytes 393224 | tf_op jit(solution)/shard_map/ppermute | solution.py:76
  46.1 6.6 %collective-permute-start.14 = (bf16[16,32,128]{2,1,0:T(8,128)(2,1)S(1)}, bf16[16,32,128]{2,1,0:T(8,128)(2,1)S(1)}, u32[]{:S(2)}, u32[]{:S(2)}) collective-permute-start(bf16[16,32,128]{2,1,0:T(8,128)(2,1)S(1)} %shard_map.84.refs_0_), channel_id=1, source_target_pairs={{0,64},{4,68},{8,72},{12,76},{16,80},{20,84},{24,88},{28,92},{32,9... | collective-permute-start | bytes 393224 | tf_op jit(solution)/shard_map/ppermute | solution.py:76
  47.0 7.0 %collective-permute-start.13 = (bf16[16,32,128]{2,1,0:T(8,128)(2,1)S(1)}, bf16[16,32,128]{2,1,0:T(8,128)(2,1)S(1)}, u32[]{:S(2)}, u32[]{:S(2)}) collective-permute-start(bf16[16,32,128]{2,1,0:T(8,128)(2,1)S(1)} %shard_map.84.refs_0_), channel_id=1, source_target_pairs={{0,32},{4,36},{8,40},{12,44},{16,48},{20,52},{24,56},{28,60},{32,6... | collective-permute-start | bytes 393224 | tf_op jit(solution)/shard_map/ppermute | solution.py:76
  54.0 2.0 %collective-permute-start.16 = (bf16[64,32,128]{2,1,0:T(8,128)(2,1)S(1)}, bf16[64,32,128]{2,1,0:T(8,128)(2,1)S(1)}, u32[]{:S(2)}, u32[]{:S(2)}) collective-permute-start(bf16[64,32,128]{2,1,0:T(8,128)(2,1)S(1)} %shard_map.85.refs_0_), channel_id=1, source_target_pairs={{0,4},{4,0},{8,12},{12,8},{16,20},{20,16},{24,28},{28,24},{32,36},... | collective-permute-start | bytes 1572872 | tf_op jit(solution)/shard_map/ppermute | solution.py:77
  56.8 6.1 %collective-permute-start.19 = (f32[4,32,128]{2,1,0:T(8,128)S(1)}, f32[4,32,128]{2,1,0:T(8,128)S(1)}, u32[]{:S(2)}, u32[]{:S(2)}) collective-permute-start(f32[4,32,128]{2,1,0:T(8,128)S(1)} %shard_map.89.refs_0_), channel_id=1, source_target_pairs={{0,3},{1,0},{2,1},{3,2},{4,7},{5,4},{6,5},{7,6},{8,11},{9,8},{10,9... | collective-permute-start | bytes 196616 | tf_op jit(solution)/shard_map/ppermute | solution.py:284
  59.2 5.7 %collective-permute-start.18 = (f32[4,32,128]{2,1,0:T(8,128)S(1)}, f32[4,32,128]{2,1,0:T(8,128)S(1)}, u32[]{:S(2)}, u32[]{:S(2)}) collective-permute-start(f32[4,32,128]{2,1,0:T(8,128)S(1)} %shard_map.88.refs_0_), channel_id=1, source_target_pairs={{0,1},{1,2},{2,3},{3,0},{4,5},{5,6},{6,7},{7,4},{8,9},{9,10},{10,1... | collective-permute-start | bytes 196616 | tf_op jit(solution)/shard_map/ppermute | solution.py:284
  59.8 6.1 %collective-permute-start.17 = (f32[4,32,128]{2,1,0:T(8,128)S(1)}, f32[4,32,128]{2,1,0:T(8,128)S(1)}, u32[]{:S(2)}, u32[]{:S(2)}) collective-permute-start(f32[4,32,128]{2,1,0:T(8,128)S(1)} %shard_map.87.refs_0_), channel_id=1, source_target_pairs={{0,2},{1,3},{2,0},{3,1},{4,6},{5,7},{6,4},{7,5},{8,10},{9,11},{10,... | collective-permute-start | bytes 196616 | tf_op jit(solution)/shard_map/ppermute | solution.py:284
  65.9 4.3 %collective-permute-start.22 = (bf16[4,32,128]{2,1,0:T(8,128)(2,1)S(1)}, bf16[4,32,128]{2,1,0:T(8,128)(2,1)S(1)}, u32[]{:S(2)}, u32[]{:S(2)}) collective-permute-start(bf16[4,32,128]{2,1,0:T(8,128)(2,1)S(1)} %get-tuple-element.20.refs_0_), channel_id=1, source_target_pairs={{0,24},{4,28},{8,0},{12,4},{16,8},{20,12},{24,16},{28,20},{32,56},... | collective-permute-start | bytes 98312 | tf_op jit(solution)/shard_map/ppermute | solution.py:72
  68.6 5.5 %collective-permute-start.21 = (bf16[4,32,128]{2,1,0:T(8,128)(2,1)S(1)}, bf16[4,32,128]{2,1,0:T(8,128)(2,1)S(1)}, u32[]{:S(2)}, u32[]{:S(2)}) collective-permute-start(bf16[4,32,128]{2,1,0:T(8,128)(2,1)S(1)} %get-tuple-element.20.refs_0_), channel_id=1, source_target_pairs={{0,16},{4,20},{8,24},{12,28},{16,0},{20,4},{24,8},{28,12},{32,48},... | collective-permute-start | bytes 98312 | tf_op jit(solution)/shard_map/ppermute | solution.py:72
  68.6 5.5 %collective-permute-start.20 = (bf16[4,32,128]{2,1,0:T(8,128)(2,1)S(1)}, bf16[4,32,128]{2,1,0:T(8,128)(2,1)S(1)}, u32[]{:S(2)}, u32[]{:S(2)}) collective-permute-start(bf16[4,32,128]{2,1,0:T(8,128)(2,1)S(1)} %get-tuple-element.20.refs_0_), channel_id=1, source_target_pairs={{0,8},{4,12},{8,16},{12,20},{16,24},{20,28},{24,0},{28,4},{32,40},... | collective-permute-start | bytes 98312 | tf_op jit(solution)/shard_map/ppermute | solution.py:72
  74.1 5.0 %collective-permute-start.25 = (bf16[16,32,128]{2,1,0:T(8,128)(2,1)S(1)}, bf16[16,32,128]{2,1,0:T(8,128)(2,1)S(1)}, u32[]{:S(2)}, u32[]{:S(2)}) collective-permute-start(bf16[16,32,128]{2,1,0:T(8,128)(2,1)S(1)} %shard_map.92.refs_0_), channel_id=1, source_target_pairs={{0,96},{4,100},{8,104},{12,108},{16,112},{20,116},{24,120},{28,124... | collective-permute-start | bytes 393224 | tf_op jit(solution)/shard_map/ppermute | solution.py:76
  74.8 6.9 %collective-permute-start.24 = (bf16[16,32,128]{2,1,0:T(8,128)(2,1)S(1)}, bf16[16,32,128]{2,1,0:T(8,128)(2,1)S(1)}, u32[]{:S(2)}, u32[]{:S(2)}) collective-permute-start(bf16[16,32,128]{2,1,0:T(8,128)(2,1)S(1)} %shard_map.92.refs_0_), channel_id=1, source_target_pairs={{0,64},{4,68},{8,72},{12,76},{16,80},{20,84},{24,88},{28,92},{32,9... | collective-permute-start | bytes 393224 | tf_op jit(solution)/shard_map/ppermute | solution.py:76
  75.7 7.2 %collective-permute-start.23 = (bf16[16,32,128]{2,1,0:T(8,128)(2,1)S(1)}, bf16[16,32,128]{2,1,0:T(8,128)(2,1)S(1)}, u32[]{:S(2)}, u32[]{:S(2)}) collective-permute-start(bf16[16,32,128]{2,1,0:T(8,128)(2,1)S(1)} %shard_map.92.refs_0_), channel_id=1, source_target_pairs={{0,32},{4,36},{8,40},{12,44},{16,48},{20,52},{24,56},{28,60},{32,6... | collective-permute-start | bytes 393224 | tf_op jit(solution)/shard_map/ppermute | solution.py:76
  83.0 2.0 %collective-permute-start.26 = (bf16[64,32,128]{2,1,0:T(8,128)(2,1)S(1)}, bf16[64,32,128]{2,1,0:T(8,128)(2,1)S(1)}, u32[]{:S(2)}, u32[]{:S(2)}) collective-permute-start(bf16[64,32,128]{2,1,0:T(8,128)(2,1)S(1)} %shard_map.93.refs_0_), channel_id=1, source_target_pairs={{0,4},{4,0},{8,12},{12,8},{16,20},{20,16},{24,28},{28,24},{32,36},... | collective-permute-start | bytes 1572872 | tf_op jit(solution)/shard_map/ppermute | solution.py:77
  85.8 5.6 %collective-permute-start.29 = (f32[4,32,128]{2,1,0:T(8,128)S(1)}, f32[4,32,128]{2,1,0:T(8,128)S(1)}, u32[]{:S(2)}, u32[]{:S(2)}) collective-permute-start(f32[4,32,128]{2,1,0:T(8,128)S(1)} %shard_map.97.refs_0_), channel_id=1, source_target_pairs={{0,3},{1,0},{2,1},{3,2},{4,7},{5,4},{6,5},{7,6},{8,11},{9,8},{10,9... | collective-permute-start | bytes 196616 | tf_op jit(solution)/shard_map/ppermute | solution.py:284
  88.8 7.1 %collective-permute-start.28 = (f32[4,32,128]{2,1,0:T(8,128)S(1)}, f32[4,32,128]{2,1,0:T(8,128)S(1)}, u32[]{:S(2)}, u32[]{:S(2)}) collective-permute-start(f32[4,32,128]{2,1,0:T(8,128)S(1)} %shard_map.96.refs_0_), channel_id=1, source_target_pairs={{0,1},{1,2},{2,3},{3,0},{4,5},{5,6},{6,7},{7,4},{8,9},{9,10},{10,1... | collective-permute-start | bytes 196616 | tf_op jit(solution)/shard_map/ppermute | solution.py:284
  88.8 7.1 %collective-permute-start.27 = (f32[4,32,128]{2,1,0:T(8,128)S(1)}, f32[4,32,128]{2,1,0:T(8,128)S(1)}, u32[]{:S(2)}, u32[]{:S(2)}) collective-permute-start(f32[4,32,128]{2,1,0:T(8,128)S(1)} %shard_map.95.refs_0_), channel_id=1, source_target_pairs={{0,2},{1,3},{2,0},{3,1},{4,6},{5,7},{6,4},{7,5},{8,10},{9,11},{10,... | collective-permute-start | bytes 196616 | tf_op jit(solution)/shard_map/ppermute | solution.py:284

commit v3 on v2

--- a/solution.py
+++ b/solution.py
@@ -58,23 +58,29 @@
     return small_call(round_kernel, jax.ShapeDtypeStruct(value.shape, jnp.bfloat16), [VMEM])(value)
 
 
-def chip_shifts(dx, dy, dcore=0):
+def chip_shifts(stage, step):
     pairs = []
     for x in range(SIDE):
         for y in range(SIDE):
             for core in range(CORES):
-                to = ((x + dx) % SIDE * SIDE + (y + dy) % SIDE) * CORES + (core + dcore) % CORES
-                pairs.append(((x * SIDE + y) * CORES + core, to))
+                along_y = stage == core
+                to_x = x if along_y else (x + step) % SIDE
+                to_y = (y + step) % SIDE if along_y else y
+                pairs.append(((x * SIDE + y) * CORES + core, (to_x * SIDE + to_y) * CORES + core))
     return pairs
 
 
+def core_swap():
+    return [(i, i ^ 1) for i in range(SIDE * SIDE * CORES)]
+
+
 def line_gathered(owned, after=(), specs=()):
-    return joined([owned] + [lax.ppermute(owned, "row", chip_shifts(0, dy)) for dy in range(1, SIDE)], after, specs)
+    return joined([owned] + [lax.ppermute(owned, "row", chip_shifts(0, step)) for step in range(1, SIDE)], after, specs)
 
 
 def all_gathered(line, after=()):
-    mine = joined([line] + [lax.ppermute(line, "row", chip_shifts(dx, 0)) for dx in range(1, SIDE)], after)
-    theirs = lax.ppermute(mine, "row", chip_shifts(0, 0, 1))
+    mine = joined([line] + [lax.ppermute(line, "row", chip_shifts(1, step)) for step in range(1, SIDE)], after)
+    theirs = lax.ppermute(mine, "row", core_swap())
     return joined([mine, theirs])
 
 
@@ -127,7 +133,8 @@
     dx = lax.rem(lax.div(my_chip, SIDE) + SIDE - lax.div(chip, SIDE), SIDE)
     dy = lax.rem(lax.rem(my_chip, SIDE) + SIDE - lax.rem(chip, SIDE), SIDE)
     dcore = lax.rem(me + owner, CORES)
-    source = ((dcore * SIDE + dx) * SIDE + dy) * owned + lax.rem(cols, owned)
+    within = jnp.where(lax.rem(owner, CORES) == 0, dx * SIDE + dy, dy * SIDE + dx)
+    source = (dcore * (SIDE * SIDE) + within) * owned + lax.rem(cols, owned)
     weights = jnp.broadcast_to(jnp.where(alive, source, 0).astype(jnp.float32), (8, slots)).astype(jnp.bfloat16)
     for block in range((room + SPARE) // SPARE):
         match = jnp.where(place == iota((SPARE, slots), 0) + block * SPARE, 1.0, 0.0).astype(jnp.bfloat16)

time: 97 us -> 97.2 us (level); the launches traced: 96.6 us -> 95.7 us
  waiting for transfers between devices: 43.4 us -> 42.3 us
    ppermute x9, waiting for transfers between devices: 11.6 us -> 10.4 us  [image_pieces(): lax.ppermute(piece, 'col', [(i, (i + part) % parts) for i in range(parts)])]
  transfers between devices with their start and end apart: 30 -> 30, of which waited for: 22 -> 23; matrix products, arithmetic and copies ran while one was open for 0% -> 0% of each run, Pallas kernels for 6% -> 6%
where the time goes in v3:
time: 97.2 us; the launch traced here: 95.7 us
  waiting for transfers between devices  42.3 us (44%)
  starting transfers between devices  41.5 us (43%)
  Pallas kernels  8.87 us (9%)
  between operations  2.2 us (2%)
    ppermute x9, starting transfers between devices, image_pieces(): lax.ppermute(piece, 'col', [(i, (i + part) % parts) for i in range(parts)])  17.7 us
    ppermute x9, waiting for transfers between devices, all_gathered(): lax.ppermute(line, 'row', chip_shifts(1, step))  16.8 us
    ppermute x9, starting transfers between devices, line_gathered(): lax.ppermute(owned, 'row', chip_shifts(0, step))  12.7 us
    ppermute x9, starting transfers between devices, all_gathered(): lax.ppermute(line, 'row', chip_shifts(1, step))  10.8 us
    ppermute x9, waiting for transfers between devices, image_pieces(): lax.ppermute(piece, 'col', [(i, (i + part) % parts) for i in range(parts)])  10.4 us
    ppermute x9, waiting for transfers between devices, line_gathered(): lax.ppermute(owned, 'row', chip_shifts(0, step))  9.38 us
    ppermute x3, waiting for transfers between devices, all_gathered(): theirs = lax.ppermute(mine, 'row', core_swap())  5.69 us
    pallas_call x12, Pallas kernels, local_products(): pl.pallas_call(functools.partial(products_kernel, part * owned), out_shap...  4.01 us
  transfers between devices with their start and end apart: 30, of which 23 were waited for; matrix products, arithmetic and copies ran while one was open for 0% of the time, Pallas kernels for 6%

profile of v3, /device:TPU:0, one launch (start us, length us, event | category | flops | bytes accessed | tf_op | source)
XLA Modules:
  0.0 95.7 jit_solution(396235885218550833)
XLA Ops:
  0.8 3.1 %collective-permute-start.2 = (bf16[4,32,128]{2,1,0:T(8,128)(2,1)S(1)}, bf16[4,32,128]{2,1,0:T(8,128)(2,1)S(1)}, u32[]{:S(2)}, u32[]{:S(2)}) collective-permute-start(bf16[4,32,128]{2,1,0:T(8,128)(2,1)S(1)} %shard_map.73._after.refs_0_), channel_id=1, source_target_pairs={{0,24},{4,100},{8,0},{12,108},{16,8},{20,116},{24,16},{28,124},{32... | collective-permute-start | bytes 98312 | tf_op jit(solution)/shard_map/ppermute | solution.py:78
  7.5 2.1 %shard_map.74 = (s32[1,640]{1,0:T(1,128)S(4)}, s32[1,1344]{1,0:T(1,128)S(4)}, f32[1]{0:T(128)S(4)}, f32[1]{0:T(128)S(4)}) custom-call(s32[1]{0:T(128)S(6)} %copy.8.live_ref, s32[640]{0:T(1024)} %rows_hbm.1, s32[640]{0:T(1024)} %cols_hbm.1, f32[]{:T(128)S(6)} %copy.9.center, f32[]{:T(128)S(6)} %copy.10.half_width, ...), custom_call_target="tpu_custom_call" | custom-call | flops 1000 | bytes 1000 | tf_op jit(solution)/shard_map/pallas_call | solution.py:165
  9.8 2.8 %collective-permute-start.5 = (bf16[16,32,128]{2,1,0:T(8,128)(2,1)S(1)}, bf16[16,32,128]{2,1,0:T(8,128)(2,1)S(1)}, u32[]{:S(2)}, u32[]{:S(2)}) collective-permute-start(bf16[16,32,128]{2,1,0:T(8,128)(2,1)S(1)} %shard_map.75._after.refs_0_), channel_id=1, source_target_pairs={{0,96},{4,28},{8,104},{12,4},{16,112},{20,12},{24,120},{28,20},{32... | collective-permute-start | bytes 393224 | tf_op jit(solution)/shard_map/ppermute | solution.py:82
  14.3 1.7 %shard_map.76.refs_4_.store = bf16[832,128,128]{2,1,0:T(8,128)(2,1)S(1)} custom-call(s32[1,640]{1,0:T(1,128)S(4)} %get-tuple-element.16.place, s32[1,1344]{1,0:T(1,128)S(4)} %get-tuple-element.15.refs_4_.sizes.table, bf16[16,32,128]{2,1,0:T(8,128)(2,1)S(1)} %shard_map.75._after.refs_0_, bf16[640,128,128]{2,1,0:T(8,128)(2,1)} %blocks_hbm.1), custom_call_target="tpu_custom_call" | custom-call | flops 1000 | bytes 20971520 | tf_op jit(solution)/shard_map/pallas_call | solution.py:207
  16.5 2.6 %collective-permute-done.4.refs_2_ = bf16[16,32,128]{2,1,0:T(8,128)(2,1)S(1)} collective-permute-done((bf16[16,32,128]{2,1,0:T(8,128)(2,1)S(1)}, bf16[16,32,128]{2,1,0:T(8,128)(2,1)S(1)}, u32[]{:S(2)}, u32[]{:S(2)}) %collective-permute-start.4) | collective-permute-done | bytes 131104 | tf_op jit(solution)/shard_map/ppermute | solution.py:82
  19.1 1.3 %collective-permute-done.3.refs_1_ = bf16[16,32,128]{2,1,0:T(8,128)(2,1)S(1)} collective-permute-done((bf16[16,32,128]{2,1,0:T(8,128)(2,1)S(1)}, bf16[16,32,128]{2,1,0:T(8,128)(2,1)S(1)}, u32[]{:S(2)}, u32[]{:S(2)}) %collective-permute-start.3) | collective-permute-done | bytes 131104 | tf_op jit(solution)/shard_map/ppermute | solution.py:82
  20.6 1.9 %collective-permute-done.6.refs_1_ = bf16[64,32,128]{2,1,0:T(8,128)(2,1)S(1)} collective-permute-done((bf16[64,32,128]{2,1,0:T(8,128)(2,1)S(1)}, bf16[64,32,128]{2,1,0:T(8,128)(2,1)S(1)}, u32[]{:S(2)}, u32[]{:S(2)}) %collective-permute-start.6) | collective-permute-done | bytes 524320 | tf_op jit(solution)/shard_map/ppermute | solution.py:83
  23.3 4.7 %collective-permute-start.9 = (f32[4,32,128]{2,1,0:T(8,128)S(1)}, f32[4,32,128]{2,1,0:T(8,128)S(1)}, u32[]{:S(2)}, u32[]{:S(2)}) collective-permute-start(f32[4,32,128]{2,1,0:T(8,128)S(1)} %shard_map.81.refs_0_), channel_id=1, source_target_pairs={{0,3},{1,0},{2,1},{3,2},{4,7},{5,4},{6,5},{7,6},{8,11},{9,8},{10,9... | collective-permute-start | bytes 196616 | tf_op jit(solution)/shard_map/ppermute | solution.py:291
  28.0 2.5 %collective-permute-start.7 = (f32[4,32,128]{2,1,0:T(8,128)S(1)}, f32[4,32,128]{2,1,0:T(8,128)S(1)}, u32[]{:S(2)}, u32[]{:S(2)}) collective-permute-start(f32[4,32,128]{2,1,0:T(8,128)S(1)} %shard_map.79.refs_0_), channel_id=1, source_target_pairs={{0,2},{1,3},{2,0},{3,1},{4,6},{5,7},{6,4},{7,5},{8,10},{9,11},{10,... | collective-permute-start | bytes 196616 | tf_op jit(solution)/shard_map/ppermute | solution.py:291
  31.1 4.0 %collective-permute-done.8.refs_1_ = f32[4,32,128]{2,1,0:T(8,128)S(1)} collective-permute-done((f32[4,32,128]{2,1,0:T(8,128)S(1)}, f32[4,32,128]{2,1,0:T(8,128)S(1)}, u32[]{:S(2)}, u32[]{:S(2)}) %collective-permute-start.8) | collective-permute-done | bytes 65568 | tf_op jit(solution)/shard_map/ppermute | solution.py:291
  35.1 3.0 %collective-permute-start.12 = (bf16[4,32,128]{2,1,0:T(8,128)(2,1)S(1)}, bf16[4,32,128]{2,1,0:T(8,128)(2,1)S(1)}, u32[]{:S(2)}, u32[]{:S(2)}) collective-permute-start(bf16[4,32,128]{2,1,0:T(8,128)(2,1)S(1)} %get-tuple-element.18.refs_0_), channel_id=1, source_target_pairs={{0,24},{4,100},{8,0},{12,108},{16,8},{20,116},{24,16},{28,124},{32... | collective-permute-start | bytes 98312 | tf_op jit(solution)/shard_map/ppermute | solution.py:78
  39.6 3.8 %collective-permute-done.11.refs_2_ = bf16[4,32,128]{2,1,0:T(8,128)(2,1)S(1)} collective-permute-done((bf16[4,32,128]{2,1,0:T(8,128)(2,1)S(1)}, bf16[4,32,128]{2,1,0:T(8,128)(2,1)S(1)}, u32[]{:S(2)}, u32[]{:S(2)}) %collective-permute-start.11) | collective-permute-done | bytes 32800 | tf_op jit(solution)/shard_map/ppermute | solution.py:78
  44.1 2.0 %collective-permute-start.15 = (bf16[16,32,128]{2,1,0:T(8,128)(2,1)S(1)}, bf16[16,32,128]{2,1,0:T(8,128)(2,1)S(1)}, u32[]{:S(2)}, u32[]{:S(2)}) collective-permute-start(bf16[16,32,128]{2,1,0:T(8,128)(2,1)S(1)} %shard_map.84.refs_0_), channel_id=1, source_target_pairs={{0,96},{4,28},{8,104},{12,4},{16,112},{20,12},{24,120},{28,20},{32... | collective-permute-start | bytes 393224 | tf_op jit(solution)/shard_map/ppermute | solution.py:82
  46.5 1.3 %collective-permute-start.13 = (bf16[16,32,128]{2,1,0:T(8,128)(2,1)S(1)}, bf16[16,32,128]{2,1,0:T(8,128)(2,1)S(1)}, u32[]{:S(2)}, u32[]{:S(2)}) collective-permute-start(bf16[16,32,128]{2,1,0:T(8,128)(2,1)S(1)} %shard_map.84.refs_0_), channel_id=1, source_target_pairs={{0,32},{4,12},{8,40},{12,20},{16,48},{20,28},{24,56},{28,4},{32,64... | collective-permute-start | bytes 393224 | tf_op jit(solution)/shard_map/ppermute | solution.py:82
  47.8 1.4 %collective-permute-done.15.refs_3_ = bf16[16,32,128]{2,1,0:T(8,128)(2,1)S(1)} collective-permute-done((bf16[16,32,128]{2,1,0:T(8,128)(2,1)S(1)}, bf16[16,32,128]{2,1,0:T(8,128)(2,1)S(1)}, u32[]{:S(2)}, u32[]{:S(2)}) %collective-permute-start.15) | collective-permute-done | bytes 131104 | tf_op jit(solution)/shard_map/ppermute | solution.py:82
  49.2 3.5 %collective-permute-done.14.refs_2_ = bf16[16,32,128]{2,1,0:T(8,128)(2,1)S(1)} collective-permute-done((bf16[16,32,128]{2,1,0:T(8,128)(2,1)S(1)}, bf16[16,32,128]{2,1,0:T(8,128)(2,1)S(1)}, u32[]{:S(2)}, u32[]{:S(2)}) %collective-permute-start.14) | collective-permute-done | bytes 131104 | tf_op jit(solution)/shard_map/ppermute | solution.py:82
  54.1 1.9 %collective-permute-done.16.refs_1_ = bf16[64,32,128]{2,1,0:T(8,128)(2,1)S(1)} collective-permute-done((bf16[64,32,128]{2,1,0:T(8,128)(2,1)S(1)}, bf16[64,32,128]{2,1,0:T(8,128)(2,1)S(1)}, u32[]{:S(2)}, u32[]{:S(2)}) %collective-permute-start.16) | collective-permute-done | bytes 524320 | tf_op jit(solution)/shard_map/ppermute | solution.py:83
  56.8 2.0 %collective-permute-start.19 = (f32[4,32,128]{2,1,0:T(8,128)S(1)}, f32[4,32,128]{2,1,0:T(8,128)S(1)}, u32[]{:S(2)}, u32[]{:S(2)}) collective-permute-start(f32[4,32,128]{2,1,0:T(8,128)S(1)} %shard_map.89.refs_0_), channel_id=1, source_target_pairs={{0,3},{1,0},{2,1},{3,2},{4,7},{5,4},{6,5},{7,6},{8,11},{9,8},{10,9... | collective-permute-start | bytes 196616 | tf_op jit(solution)/shard_map/ppermute | solution.py:291
  59.8 2.3 %collective-permute-start.17 = (f32[4,32,128]{2,1,0:T(8,128)S(1)}, f32[4,32,128]{2,1,0:T(8,128)S(1)}, u32[]{:S(2)}, u32[]{:S(2)}) collective-permute-start(f32[4,32,128]{2,1,0:T(8,128)S(1)} %shard_map.87.refs_0_), channel_id=1, source_target_pairs={{0,2},{1,3},{2,0},{3,1},{4,6},{5,7},{6,4},{7,5},{8,10},{9,11},{10,... | collective-permute-start | bytes 196616 | tf_op jit(solution)/shard_map/ppermute | solution.py:291
  62.9 1.6 %collective-permute-done.18.refs_1_ = f32[4,32,128]{2,1,0:T(8,128)S(1)} collective-permute-done((f32[4,32,128]{2,1,0:T(8,128)S(1)}, f32[4,32,128]{2,1,0:T(8,128)S(1)}, u32[]{:S(2)}, u32[]{:S(2)}) %collective-permute-start.18) | collective-permute-done | bytes 65568 | tf_op jit(solution)/shard_map/ppermute | solution.py:291
  64.5 1.4 %collective-permute-done.17.refs_0_ = f32[4,32,128]{2,1,0:T(8,128)S(1)} collective-permute-done((f32[4,32,128]{2,1,0:T(8,128)S(1)}, f32[4,32,128]{2,1,0:T(8,128)S(1)}, u32[]{:S(2)}, u32[]{:S(2)}) %collective-permute-start.17) | collective-permute-done | bytes 65568 | tf_op jit(solution)/shard_map/ppermute | solution.py:291
  65.9 2.7 %collective-permute-start.22 = (bf16[4,32,128]{2,1,0:T(8,128)(2,1)S(1)}, bf16[4,32,128]{2,1,0:T(8,128)(2,1)S(1)}, u32[]{:S(2)}, u32[]{:S(2)}) collective-permute-start(bf16[4,32,128]{2,1,0:T(8,128)(2,1)S(1)} %get-tuple-element.20.refs_0_), channel_id=1, source_target_pairs={{0,24},{4,100},{8,0},{12,108},{16,8},{20,116},{24,16},{28,124},{32... | collective-permute-start | bytes 98312 | tf_op jit(solution)/shard_map/ppermute | solution.py:78
  68.7 1.3 %collective-permute-start.20 = (bf16[4,32,128]{2,1,0:T(8,128)(2,1)S(1)}, bf16[4,32,128]{2,1,0:T(8,128)(2,1)S(1)}, u32[]{:S(2)}, u32[]{:S(2)}) collective-permute-start(bf16[4,32,128]{2,1,0:T(8,128)(2,1)S(1)} %get-tuple-element.20.refs_0_), channel_id=1, source_target_pairs={{0,8},{4,36},{8,16},{12,44},{16,24},{20,52},{24,0},{28,60},{32,40}... | collective-permute-start | bytes 98312 | tf_op jit(solution)/shard_map/ppermute | solution.py:78
  70.2 3.9 %collective-permute-done.21.refs_2_ = bf16[4,32,128]{2,1,0:T(8,128)(2,1)S(1)} collective-permute-done((bf16[4,32,128]{2,1,0:T(8,128)(2,1)S(1)}, bf16[4,32,128]{2,1,0:T(8,128)(2,1)S(1)}, u32[]{:S(2)}, u32[]{:S(2)}) %collective-permute-start.21) | collective-permute-done | bytes 32800 | tf_op jit(solution)/shard_map/ppermute | solution.py:78
  76.8 2.4 %collective-permute-done.25.refs_3_ = bf16[16,32,128]{2,1,0:T(8,128)(2,1)S(1)} collective-permute-done((bf16[16,32,128]{2,1,0:T(8,128)(2,1)S(1)}, bf16[16,32,128]{2,1,0:T(8,128)(2,1)S(1)}, u32[]{:S(2)}, u32[]{:S(2)}) %collective-permute-start.25) | collective-permute-done | bytes 131104 | tf_op jit(solution)/shard_map/ppermute | solution.py:82
  79.2 2.4 %collective-permute-done.24.refs_2_ = bf16[16,32,128]{2,1,0:T(8,128)(2,1)S(1)} collective-permute-done((bf16[16,32,128]{2,1,0:T(8,128)(2,1)S(1)}, bf16[16,32,128]{2,1,0:T(8,128)(2,1)S(1)}, u32[]{:S(2)}, u32[]{:S(2)}) %collective-permute-start.24) | collective-permute-done | bytes 131104 | tf_op jit(solution)/shard_map/ppermute | solution.py:82
  81.6 1.3 %collective-permute-done.23.refs_1_ = bf16[16,32,128]{2,1,0:T(8,128)(2,1)S(1)} collective-permute-done((bf16[16,32,128]{2,1,0:T(8,128)(2,1)S(1)}, bf16[16,32,128]{2,1,0:T(8,128)(2,1)S(1)}, u32[]{:S(2)}, u32[]{:S(2)}) %collective-permute-start.23) | collective-permute-done | bytes 131104 | tf_op jit(solution)/shard_map/ppermute | solution.py:82
  83.1 1.9 %collective-permute-done.26.refs_1_ = bf16[64,32,128]{2,1,0:T(8,128)(2,1)S(1)} collective-permute-done((bf16[64,32,128]{2,1,0:T(8,128)(2,1)S(1)}, bf16[64,32,128]{2,1,0:T(8,128)(2,1)S(1)}, u32[]{:S(2)}, u32[]{:S(2)}) %collective-permute-start.26) | collective-permute-done | bytes 524320 | tf_op jit(solution)/shard_map/ppermute | solution.py:83
  85.7 2.2 %collective-permute-start.29 = (f32[4,32,128]{2,1,0:T(8,128)S(1)}, f32[4,32,128]{2,1,0:T(8,128)S(1)}, u32[]{:S(2)}, u32[]{:S(2)}) collective-permute-start(f32[4,32,128]{2,1,0:T(8,128)S(1)} %shard_map.97.refs_0_), channel_id=1, source_target_pairs={{0,3},{1,0},{2,1},{3,2},{4,7},{5,4},{6,5},{7,6},{8,11},{9,8},{10,9... | collective-permute-start | bytes 196616 | tf_op jit(solution)/shard_map/ppermute | solution.py:291
  89.0 2.0 %collective-permute-start.27 = (f32[4,32,128]{2,1,0:T(8,128)S(1)}, f32[4,32,128]{2,1,0:T(8,128)S(1)}, u32[]{:S(2)}, u32[]{:S(2)}) collective-permute-start(f32[4,32,128]{2,1,0:T(8,128)S(1)} %shard_map.95.refs_0_), channel_id=1, source_target_pairs={{0,2},{1,3},{2,0},{3,1},{4,6},{5,7},{6,4},{7,5},{8,10},{9,11},{10,... | collective-permute-start | bytes 196616 | tf_op jit(solution)/shard_map/ppermute | solution.py:291
  91.6 2.0 %collective-permute-done.28.refs_1_ = f32[4,32,128]{2,1,0:T(8,128)S(1)} collective-permute-done((f32[4,32,128]{2,1,0:T(8,128)S(1)}, f32[4,32,128]{2,1,0:T(8,128)S(1)}, u32[]{:S(2)}, u32[]{:S(2)}) %collective-permute-start.28) | collective-permute-done | bytes 65568 | tf_op jit(solution)/shard_map/ppermute | solution.py:291
  93.6 1.4 %collective-permute-done.27.refs_0_ = f32[4,32,128]{2,1,0:T(8,128)S(1)} collective-permute-done((f32[4,32,128]{2,1,0:T(8,128)S(1)}, f32[4,32,128]{2,1,0:T(8,128)S(1)}, u32[]{:S(2)}, u32[]{:S(2)}) %collective-permute-start.27) | collective-permute-done | bytes 65568 | tf_op jit(solution)/shard_map/ppermute | solution.py:291
  (59 shorter events, 18.9 us)
Async XLA Ops:
  0.0 0.8 copy-start
  0.8 8.8 %collective-permute-start.2 = (bf16[4,32,128]{2,1,0:T(8,128)(2,1)S(1)}, bf16[4,32,128]{2,1,0:T(8,128)(2,1)S(1)}, u32[]{:S(2)}, u32[]{:S(2)}) collective-permute-start(bf16[4,32,128]{2,1,0:T(8,128)(2,1)S(1)} %shard_map.73._after.refs_0_), channel_id=1, source_target_pairs={{0,24},{4,100},{8,0},{12,108},{16,8},{20,116},{24,16},{28,124},{32... | collective-permute-start | bytes 98312 | tf_op jit(solution)/shard_map/ppermute | solution.py:78
  4.0 5.7 %collective-permute-start.1 = (bf16[4,32,128]{2,1,0:T(8,128)(2,1)S(1)}, bf16[4,32,128]{2,1,0:T(8,128)(2,1)S(1)}, u32[]{:S(2)}, u32[]{:S(2)}) collective-permute-start(bf16[4,32,128]{2,1,0:T(8,128)(2,1)S(1)} %shard_map.73._after.refs_0_), channel_id=1, source_target_pairs={{0,16},{4,68},{8,24},{12,76},{16,0},{20,84},{24,8},{28,92},{32,48}... | collective-permute-start | bytes 98312 | tf_op jit(solution)/shard_map/ppermute | solution.py:78
  4.6 5.1 %collective-permute-start = (bf16[4,32,128]{2,1,0:T(8,128)(2,1)S(1)}, bf16[4,32,128]{2,1,0:T(8,128)(2,1)S(1)}, u32[]{:S(2)}, u32[]{:S(2)}) collective-permute-start(bf16[4,32,128]{2,1,0:T(8,128)(2,1)S(1)} %shard_map.73._after.refs_0_), channel_id=1, source_target_pairs={{0,8},{4,36},{8,16},{12,44},{16,24},{20,52},{24,0},{28,60},{32,40}... | collective-permute-start | bytes 98312 | tf_op jit(solution)/shard_map/ppermute | solution.py:78
  9.8 6.8 %collective-permute-start.5 = (bf16[16,32,128]{2,1,0:T(8,128)(2,1)S(1)}, bf16[16,32,128]{2,1,0:T(8,128)(2,1)S(1)}, u32[]{:S(2)}, u32[]{:S(2)}) collective-permute-start(bf16[16,32,128]{2,1,0:T(8,128)(2,1)S(1)} %shard_map.75._after.refs_0_), channel_id=1, source_target_pairs={{0,96},{4,28},{8,104},{12,4},{16,112},{20,12},{24,120},{28,20},{32... | collective-permute-start | bytes 393224 | tf_op jit(solution)/shard_map/ppermute | solution.py:82
  12.6 6.6 %collective-permute-start.4 = (bf16[16,32,128]{2,1,0:T(8,128)(2,1)S(1)}, bf16[16,32,128]{2,1,0:T(8,128)(2,1)S(1)}, u32[]{:S(2)}, u32[]{:S(2)}) collective-permute-start(bf16[16,32,128]{2,1,0:T(8,128)(2,1)S(1)} %shard_map.75._after.refs_0_), channel_id=1, source_target_pairs={{0,64},{4,20},{8,72},{12,28},{16,80},{20,4},{24,88},{28,12},{32,96... | collective-permute-start | bytes 393224 | tf_op jit(solution)/shard_map/ppermute | solution.py:82
  13.4 7.1 %collective-permute-start.3 = (bf16[16,32,128]{2,1,0:T(8,128)(2,1)S(1)}, bf16[16,32,128]{2,1,0:T(8,128)(2,1)S(1)}, u32[]{:S(2)}, u32[]{:S(2)}) collective-permute-start(bf16[16,32,128]{2,1,0:T(8,128)(2,1)S(1)} %shard_map.75._after.refs_0_), channel_id=1, source_target_pairs={{0,32},{4,12},{8,40},{12,20},{16,48},{20,28},{24,56},{28,4},{32,64... | collective-permute-start | bytes 393224 | tf_op jit(solution)/shard_map/ppermute | solution.py:82
  20.5 2.0 %collective-permute-start.6 = (bf16[64,32,128]{2,1,0:T(8,128)(2,1)S(1)}, bf16[64,32,128]{2,1,0:T(8,128)(2,1)S(1)}, u32[]{:S(2)}, u32[]{:S(2)}) collective-permute-start(bf16[64,32,128]{2,1,0:T(8,128)(2,1)S(1)} %shard_map.77.refs_0_), channel_id=1, source_target_pairs={{0,4},{4,0},{8,12},{12,8},{16,20},{20,16},{24,28},{28,24},{32,36},... | collective-permute-start | bytes 1572872 | tf_op jit(solution)/shard_map/ppermute | solution.py:83
  22.6 12.4 %copy-start.1 = (f32[4,32,128]{2,1,0:T(8,128)S(1)}, f32[4,32,128]{2,1,0:T(8,128)}, u32[]{:S(2)}) copy-start(f32[4,32,128]{2,1,0:T(8,128)} %previous.1) | copy-start | bytes 196612
  23.3 7.8 %collective-permute-start.9 = (f32[4,32,128]{2,1,0:T(8,128)S(1)}, f32[4,32,128]{2,1,0:T(8,128)S(1)}, u32[]{:S(2)}, u32[]{:S(2)}) collective-permute-start(f32[4,32,128]{2,1,0:T(8,128)S(1)} %shard_map.81.refs_0_), channel_id=1, source_target_pairs={{0,3},{1,0},{2,1},{3,2},{4,7},{5,4},{6,5},{7,6},{8,11},{9,8},{10,9... | collective-permute-start | bytes 196616 | tf_op jit(solution)/shard_map/ppermute | solution.py:291
  28.0 7.1 %collective-permute-start.8 = (f32[4,32,128]{2,1,0:T(8,128)S(1)}, f32[4,32,128]{2,1,0:T(8,128)S(1)}, u32[]{:S(2)}, u32[]{:S(2)}) collective-permute-start(f32[4,32,128]{2,1,0:T(8,128)S(1)} %shard_map.80.refs_0_), channel_id=1, source_target_pairs={{0,1},{1,2},{2,3},{3,0},{4,5},{5,6},{6,7},{7,4},{8,9},{9,10},{10,1... | collective-permute-start | bytes 196616 | tf_op jit(solution)/shard_map/ppermute | solution.py:291
  28.0 7.1 %collective-permute-start.7 = (f32[4,32,128]{2,1,0:T(8,128)S(1)}, f32[4,32,128]{2,1,0:T(8,128)S(1)}, u32[]{:S(2)}, u32[]{:S(2)}) collective-permute-start(f32[4,32,128]{2,1,0:T(8,128)S(1)} %shard_map.79.refs_0_), channel_id=1, source_target_pairs={{0,2},{1,3},{2,0},{3,1},{4,6},{5,7},{6,4},{7,5},{8,10},{9,11},{10,... | collective-permute-start | bytes 196616 | tf_op jit(solution)/shard_map/ppermute | solution.py:291
  35.1 4.6 %collective-permute-start.12 = (bf16[4,32,128]{2,1,0:T(8,128)(2,1)S(1)}, bf16[4,32,128]{2,1,0:T(8,128)(2,1)S(1)}, u32[]{:S(2)}, u32[]{:S(2)}) collective-permute-start(bf16[4,32,128]{2,1,0:T(8,128)(2,1)S(1)} %get-tuple-element.18.refs_0_), channel_id=1, source_target_pairs={{0,24},{4,100},{8,0},{12,108},{16,8},{20,116},{24,16},{28,124},{32... | collective-permute-start | bytes 98312 | tf_op jit(solution)/shard_map/ppermute | solution.py:78
  38.0 5.4 %collective-permute-start.11 = (bf16[4,32,128]{2,1,0:T(8,128)(2,1)S(1)}, bf16[4,32,128]{2,1,0:T(8,128)(2,1)S(1)}, u32[]{:S(2)}, u32[]{:S(2)}) collective-permute-start(bf16[4,32,128]{2,1,0:T(8,128)(2,1)S(1)} %get-tuple-element.18.refs_0_), channel_id=1, source_target_pairs={{0,16},{4,68},{8,24},{12,76},{16,0},{20,84},{24,8},{28,92},{32,48}... | collective-permute-start | bytes 98312 | tf_op jit(solution)/shard_map/ppermute | solution.py:78
  39.0 5.1 %collective-permute-start.10 = (bf16[4,32,128]{2,1,0:T(8,128)(2,1)S(1)}, bf16[4,32,128]{2,1,0:T(8,128)(2,1)S(1)}, u32[]{:S(2)}, u32[]{:S(2)}) collective-permute-start(bf16[4,32,128]{2,1,0:T(8,128)(2,1)S(1)} %get-tuple-element.18.refs_0_), channel_id=1, source_target_pairs={{0,8},{4,36},{8,16},{12,44},{16,24},{20,52},{24,0},{28,60},{32,40}... | collective-permute-start | bytes 98312 | tf_op jit(solution)/shard_map/ppermute | solution.py:78
  44.1 5.0 %collective-permute-start.15 = (bf16[16,32,128]{2,1,0:T(8,128)(2,1)S(1)}, bf16[16,32,128]{2,1,0:T(8,128)(2,1)S(1)}, u32[]{:S(2)}, u32[]{:S(2)}) collective-permute-start(bf16[16,32,128]{2,1,0:T(8,128)(2,1)S(1)} %shard_map.84.refs_0_), channel_id=1, source_target_pairs={{0,96},{4,28},{8,104},{12,4},{16,112},{20,12},{24,120},{28,20},{32... | collective-permute-start | bytes 393224 | tf_op jit(solution)/shard_map/ppermute | solution.py:82
  46.1 6.6 %collective-permute-start.14 = (bf16[16,32,128]{2,1,0:T(8,128)(2,1)S(1)}, bf16[16,32,128]{2,1,0:T(8,128)(2,1)S(1)}, u32[]{:S(2)}, u32[]{:S(2)}) collective-permute-start(bf16[16,32,128]{2,1,0:T(8,128)(2,1)S(1)} %shard_map.84.refs_0_), channel_id=1, source_target_pairs={{0,64},{4,20},{8,72},{12,28},{16,80},{20,4},{24,88},{28,12},{32,96... | collective-permute-start | bytes 393224 | tf_op jit(solution)/shard_map/ppermute | solution.py:82
  46.5 7.5 %collective-permute-start.13 = (bf16[16,32,128]{2,1,0:T(8,128)(2,1)S(1)}, bf16[16,32,128]{2,1,0:T(8,128)(2,1)S(1)}, u32[]{:S(2)}, u32[]{:S(2)}) collective-permute-start(bf16[16,32,128]{2,1,0:T(8,128)(2,1)S(1)} %shard_map.84.refs_0_), channel_id=1, source_target_pairs={{0,32},{4,12},{8,40},{12,20},{16,48},{20,28},{24,56},{28,4},{32,64... | collective-permute-start | bytes 393224 | tf_op jit(solution)/shard_map/ppermute | solution.py:82
  54.0 2.0 %collective-permute-start.16 = (bf16[64,32,128]{2,1,0:T(8,128)(2,1)S(1)}, bf16[64,32,128]{2,1,0:T(8,128)(2,1)S(1)}, u32[]{:S(2)}, u32[]{:S(2)}) collective-permute-start(bf16[64,32,128]{2,1,0:T(8,128)(2,1)S(1)} %shard_map.85.refs_0_), channel_id=1, source_target_pairs={{0,4},{4,0},{8,12},{12,8},{16,20},{20,16},{24,28},{28,24},{32,36},... | collective-permute-start | bytes 1572872 | tf_op jit(solution)/shard_map/ppermute | solution.py:83
  56.8 6.1 %collective-permute-start.19 = (f32[4,32,128]{2,1,0:T(8,128)S(1)}, f32[4,32,128]{2,1,0:T(8,128)S(1)}, u32[]{:S(2)}, u32[]{:S(2)}) collective-permute-start(f32[4,32,128]{2,1,0:T(8,128)S(1)} %shard_map.89.refs_0_), channel_id=1, source_target_pairs={{0,3},{1,0},{2,1},{3,2},{4,7},{5,4},{6,5},{7,6},{8,11},{9,8},{10,9... | collective-permute-start | bytes 196616 | tf_op jit(solution)/shard_map/ppermute | solution.py:291
  58.8 5.7 %collective-permute-start.18 = (f32[4,32,128]{2,1,0:T(8,128)S(1)}, f32[4,32,128]{2,1,0:T(8,128)S(1)}, u32[]{:S(2)}, u32[]{:S(2)}) collective-permute-start(f32[4,32,128]{2,1,0:T(8,128)S(1)} %shard_map.88.refs_0_), channel_id=1, source_target_pairs={{0,1},{1,2},{2,3},{3,0},{4,5},{5,6},{6,7},{7,4},{8,9},{9,10},{10,1... | collective-permute-start | bytes 196616 | tf_op jit(solution)/shard_map/ppermute | solution.py:291
  59.8 6.1 %collective-permute-start.17 = (f32[4,32,128]{2,1,0:T(8,128)S(1)}, f32[4,32,128]{2,1,0:T(8,128)S(1)}, u32[]{:S(2)}, u32[]{:S(2)}) collective-permute-start(f32[4,32,128]{2,1,0:T(8,128)S(1)} %shard_map.87.refs_0_), channel_id=1, source_target_pairs={{0,2},{1,3},{2,0},{3,1},{4,6},{5,7},{6,4},{7,5},{8,10},{9,11},{10,... | collective-permute-start | bytes 196616 | tf_op jit(solution)/shard_map/ppermute | solution.py:291
  65.9 4.3 %collective-permute-start.22 = (bf16[4,32,128]{2,1,0:T(8,128)(2,1)S(1)}, bf16[4,32,128]{2,1,0:T(8,128)(2,1)S(1)}, u32[]{:S(2)}, u32[]{:S(2)}) collective-permute-start(bf16[4,32,128]{2,1,0:T(8,128)(2,1)S(1)} %get-tuple-element.20.refs_0_), channel_id=1, source_target_pairs={{0,24},{4,100},{8,0},{12,108},{16,8},{20,116},{24,16},{28,124},{32... | collective-permute-start | bytes 98312 | tf_op jit(solution)/shard_map/ppermute | solution.py:78
  68.6 5.5 %collective-permute-start.21 = (bf16[4,32,128]{2,1,0:T(8,128)(2,1)S(1)}, bf16[4,32,128]{2,1,0:T(8,128)(2,1)S(1)}, u32[]{:S(2)}, u32[]{:S(2)}) collective-permute-start(bf16[4,32,128]{2,1,0:T(8,128)(2,1)S(1)} %get-tuple-element.20.refs_0_), channel_id=1, source_target_pairs={{0,16},{4,68},{8,24},{12,76},{16,0},{20,84},{24,8},{28,92},{32,48}... | collective-permute-start | bytes 98312 | tf_op jit(solution)/shard_map/ppermute | solution.py:78
  68.7 5.5 %collective-permute-start.20 = (bf16[4,32,128]{2,1,0:T(8,128)(2,1)S(1)}, bf16[4,32,128]{2,1,0:T(8,128)(2,1)S(1)}, u32[]{:S(2)}, u32[]{:S(2)}) collective-permute-start(bf16[4,32,128]{2,1,0:T(8,128)(2,1)S(1)} %get-tuple-element.20.refs_0_), channel_id=1, source_target_pairs={{0,8},{4,36},{8,16},{12,44},{16,24},{20,52},{24,0},{28,60},{32,40}... | collective-permute-start | bytes 98312 | tf_op jit(solution)/shard_map/ppermute | solution.py:78
  74.2 5.0 %collective-permute-start.25 = (bf16[16,32,128]{2,1,0:T(8,128)(2,1)S(1)}, bf16[16,32,128]{2,1,0:T(8,128)(2,1)S(1)}, u32[]{:S(2)}, u32[]{:S(2)}) collective-permute-start(bf16[16,32,128]{2,1,0:T(8,128)(2,1)S(1)} %shard_map.92.refs_0_), channel_id=1, source_target_pairs={{0,96},{4,28},{8,104},{12,4},{16,112},{20,12},{24,120},{28,20},{32... | collective-permute-start | bytes 393224 | tf_op jit(solution)/shard_map/ppermute | solution.py:82
  75.0 6.6 %collective-permute-start.24 = (bf16[16,32,128]{2,1,0:T(8,128)(2,1)S(1)}, bf16[16,32,128]{2,1,0:T(8,128)(2,1)S(1)}, u32[]{:S(2)}, u32[]{:S(2)}) collective-permute-start(bf16[16,32,128]{2,1,0:T(8,128)(2,1)S(1)} %shard_map.92.refs_0_), channel_id=1, source_target_pairs={{0,64},{4,20},{8,72},{12,28},{16,80},{20,4},{24,88},{28,12},{32,96... | collective-permute-start | bytes 393224 | tf_op jit(solution)/shard_map/ppermute | solution.py:82
  75.7 7.2 %collective-permute-start.23 = (bf16[16,32,128]{2,1,0:T(8,128)(2,1)S(1)}, bf16[16,32,128]{2,1,0:T(8,128)(2,1)S(1)}, u32[]{:S(2)}, u32[]{:S(2)}) collective-permute-start(bf16[16,32,128]{2,1,0:T(8,128)(2,1)S(1)} %shard_map.92.refs_0_), channel_id=1, source_target_pairs={{0,32},{4,12},{8,40},{12,20},{16,48},{20,28},{24,56},{28,4},{32,64... | collective-permute-start | bytes 393224 | tf_op jit(solution)/shard_map/ppermute | solution.py:82
  83.0 2.0 %collective-permute-start.26 = (bf16[64,32,128]{2,1,0:T(8,128)(2,1)S(1)}, bf16[64,32,128]{2,1,0:T(8,128)(2,1)S(1)}, u32[]{:S(2)}, u32[]{:S(2)}) collective-permute-start(bf16[64,32,128]{2,1,0:T(8,128)(2,1)S(1)} %shard_map.93.refs_0_), channel_id=1, source_target_pairs={{0,4},{4,0},{8,12},{12,8},{16,20},{20,16},{24,28},{28,24},{32,36},... | collective-permute-start | bytes 1572872 | tf_op jit(solution)/shard_map/ppermute | solution.py:83
  85.7 5.9 %collective-permute-start.29 = (f32[4,32,128]{2,1,0:T(8,128)S(1)}, f32[4,32,128]{2,1,0:T(8,128)S(1)}, u32[]{:S(2)}, u32[]{:S(2)}) collective-permute-start(f32[4,32,128]{2,1,0:T(8,128)S(1)} %shard_map.97.refs_0_), channel_id=1, source_target_pairs={{0,3},{1,0},{2,1},{3,2},{4,7},{5,4},{6,5},{7,6},{8,11},{9,8},{10,9... | collective-permute-start | bytes 196616 | tf_op jit(solution)/shard_map/ppermute | solution.py:291
  87.9 5.7 %collective-permute-start.28 = (f32[4,32,128]{2,1,0:T(8,128)S(1)}, f32[4,32,128]{2,1,0:T(8,128)S(1)}, u32[]{:S(2)}, u32[]{:S(2)}) collective-permute-start(f32[4,32,128]{2,1,0:T(8,128)S(1)} %shard_map.96.refs_0_), channel_id=1, source_target_pairs={{0,1},{1,2},{2,3},{3,0},{4,5},{5,6},{6,7},{7,4},{8,9},{9,10},{10,1... | collective-permute-start | bytes 196616 | tf_op jit(solution)/shard_map/ppermute | solution.py:291
  89.0 6.0 %collective-permute-start.27 = (f32[4,32,128]{2,1,0:T(8,128)S(1)}, f32[4,32,128]{2,1,0:T(8,128)S(1)}, u32[]{:S(2)}, u32[]{:S(2)}) collective-permute-start(f32[4,32,128]{2,1,0:T(8,128)S(1)} %shard_map.95.refs_0_), channel_id=1, source_target_pairs={{0,2},{1,3},{2,0},{3,1},{4,6},{5,7},{6,4},{7,5},{8,10},{9,11},{10,... | collective-permute-start | bytes 196616 | tf_op jit(solution)/shard_map/ppermute | solution.py:291

commit v4 on v3

--- a/solution.py
+++ b/solution.py
@@ -17,6 +17,7 @@
 LANES = 256
 HEAD = 2 * LANES
 PART_ORDER = (2, 1, 3)
+STEP_ORDER = (1, 3, 2)
 MIB = 1 << 20
 
 
@@ -36,16 +37,16 @@
     )
 
 
-def join_kernel(count, *refs):
-    parts, out = refs[:count], refs[-1]
+def join_kernel(places, *refs):
+    parts, out = refs[: len(places)], refs[-1]
     size = parts[0].shape[0]
-    for place, part in enumerate(parts):
+    for place, part in zip(places, parts):
         out[place * size : (place + 1) * size] = part[...]
 
 
-def joined(parts, after=(), after_specs=()):
+def joined(parts, after=(), after_specs=(), places=(0, 1)):
     shape = (len(parts) * parts[0].shape[0], *parts[0].shape[1:])
-    kernel = functools.partial(join_kernel, len(parts))
+    kernel = functools.partial(join_kernel, places)
     specs = [VMEM] * len(parts) + list(after_specs or [VMEM] * len(after))
     return small_call(kernel, jax.ShapeDtypeStruct(shape, parts[0].dtype), specs)(*parts, *after)
 
@@ -74,14 +75,17 @@
     return [(i, i ^ 1) for i in range(SIDE * SIDE * CORES)]
 
 
+def shifted(value, stage):
+    return [value] + [lax.ppermute(value, "row", chip_shifts(stage, step)) for step in STEP_ORDER]
+
+
 def line_gathered(owned, after=(), specs=()):
-    return joined([owned] + [lax.ppermute(owned, "row", chip_shifts(0, step)) for step in range(1, SIDE)], after, specs)
+    return joined(shifted(owned, 0), after, specs, (0, *STEP_ORDER))
 
 
 def all_gathered(line, after=()):
-    mine = joined([line] + [lax.ppermute(line, "row", chip_shifts(1, step)) for step in range(1, SIDE)], after)
-    theirs = lax.ppermute(mine, "row", core_swap())
-    return joined([mine, theirs])
+    mine = joined(shifted(line, 1), after, (), (0, *STEP_ORDER))
+    return joined([mine, lax.ppermute(mine, "row", core_swap())])
 
 
 def padded_room(slots, span):

time: 97.2 us -> 97.7 us (level); the launches traced: 95.7 us -> 97.4 us
  starting transfers between devices: 41.5 us -> 48.8 us
  waiting for transfers between devices: 42.3 us -> 36.7 us
    ppermute x21, waiting for transfers between devices: 31.9 us -> 26.9 us  [the longest x18 21.2 us: shifted(): lax.ppermute(value, 'row', chip_shifts(stage, step))]
    ppermute x21, starting transfers between devices: 23.8 us -> 27.8 us  [the longest x18 27.6 us: shifted(): lax.ppermute(value, 'row', chip_shifts(stage, step))]
    ppermute x9, starting transfers between devices: 17.7 us -> 21 us  [image_pieces(): lax.ppermute(piece, 'col', [(i, (i + part) % parts) for i in range(parts)])]
where the time goes in v4:
time: 97.7 us; the launch traced here: 97.4 us
  starting transfers between devices  48.8 us (50%)
  waiting for transfers between devices  36.7 us (38%)
  Pallas kernels  8.88 us (9%)
  between operations  2.21 us (2%)
    ppermute x18, starting transfers between devices, shifted(): lax.ppermute(value, 'row', chip_shifts(stage, step))  27.6 us
    ppermute x18, waiting for transfers between devices, shifted(): lax.ppermute(value, 'row', chip_shifts(stage, step))  21.2 us
    ppermute x9, starting transfers between devices, image_pieces(): lax.ppermute(piece, 'col', [(i, (i + part) % parts) for i in range(parts)])  21 us
    ppermute x9, waiting for transfers between devices, image_pieces(): lax.ppermute(piece, 'col', [(i, (i + part) % parts) for i in range(parts)])  9.74 us
    ppermute x3, waiting for transfers between devices, all_gathered(): return joined([mine, lax.ppermute(mine, 'row', core_swap())])  5.69 us
    pallas_call x12, Pallas kernels, local_products(): pl.pallas_call(functools.partial(products_kernel, part * owned), out_shap...  4.01 us
    pallas_call x1, Pallas kernels, sort_plan(): pl.pallas_call(functools.partial(plan_kernel, parts, owned), out_shape=[p...  2.09 us
  transfers between devices with their start and end apart: 30, of which 23 were waited for; matrix products, arithmetic and copies ran while one was open for 0% of the time, Pallas kernels for 6%

profile of v4, /device:TPU:0, one launch (start us, length us, event | category | flops | bytes accessed | tf_op | source)
XLA Modules:
  0.0 97.4 jit_solution(9601231815407310307)
XLA Ops:
  0.8 3.3 %collective-permute-start.2 = (bf16[4,32,128]{2,1,0:T(8,128)(2,1)S(1)}, bf16[4,32,128]{2,1,0:T(8,128)(2,1)S(1)}, u32[]{:S(2)}, u32[]{:S(2)}) collective-permute-start(bf16[4,32,128]{2,1,0:T(8,128)(2,1)S(1)} %shard_map.73._after.refs_0_), channel_id=1, source_target_pairs={{0,16},{4,68},{8,24},{12,76},{16,0},{20,84},{24,8},{28,92},{32,48}... | collective-permute-start | bytes 98312 | tf_op jit(solution)/shard_map/ppermute | solution.py:79
  8.1 2.1 %shard_map.74 = (s32[1,640]{1,0:T(1,128)S(4)}, s32[1,1344]{1,0:T(1,128)S(4)}, f32[1]{0:T(128)S(4)}, f32[1]{0:T(128)S(4)}) custom-call(s32[1]{0:T(128)S(6)} %copy.8.live_ref, s32[640]{0:T(1024)} %rows_hbm.1, s32[640]{0:T(1024)} %cols_hbm.1, f32[]{:T(128)S(6)} %copy.9.center, f32[]{:T(128)S(6)} %copy.10.half_width, ...), custom_call_target="tpu_custom_call" | custom-call | flops 1000 | bytes 1000 | tf_op jit(solution)/shard_map/pallas_call | solution.py:169
  10.3 3.1 %collective-permute-start.5 = (bf16[16,32,128]{2,1,0:T(8,128)(2,1)S(1)}, bf16[16,32,128]{2,1,0:T(8,128)(2,1)S(1)}, u32[]{:S(2)}, u32[]{:S(2)}) collective-permute-start(bf16[16,32,128]{2,1,0:T(8,128)(2,1)S(1)} %shard_map.75._after.refs_0_), channel_id=1, source_target_pairs={{0,64},{4,20},{8,72},{12,28},{16,80},{20,4},{24,88},{28,12},{32,96... | collective-permute-start | bytes 393224 | tf_op jit(solution)/shard_map/ppermute | solution.py:79
  15.5 1.7 %shard_map.76.refs_4_.store = bf16[832,128,128]{2,1,0:T(8,128)(2,1)S(1)} custom-call(s32[1,640]{1,0:T(1,128)S(4)} %get-tuple-element.16.place, s32[1,1344]{1,0:T(1,128)S(4)} %get-tuple-element.15.refs_4_.sizes.table, bf16[16,32,128]{2,1,0:T(8,128)(2,1)S(1)} %shard_map.75._after.refs_0_, bf16[640,128,128]{2,1,0:T(8,128)(2,1)} %blocks_hbm.1), custom_call_target="tpu_custom_call" | custom-call | flops 1000 | bytes 20971520 | tf_op jit(solution)/shard_map/pallas_call | solution.py:211
  18.4 2.4 %collective-permute-done.3.refs_1_ = bf16[16,32,128]{2,1,0:T(8,128)(2,1)S(1)} collective-permute-done((bf16[16,32,128]{2,1,0:T(8,128)(2,1)S(1)}, bf16[16,32,128]{2,1,0:T(8,128)(2,1)S(1)}, u32[]{:S(2)}, u32[]{:S(2)}) %collective-permute-start.3) | collective-permute-done | bytes 131104 | tf_op jit(solution)/shard_map/ppermute | solution.py:79
  20.9 1.9 %collective-permute-done.6.refs_1_ = bf16[64,32,128]{2,1,0:T(8,128)(2,1)S(1)} collective-permute-done((bf16[64,32,128]{2,1,0:T(8,128)(2,1)S(1)}, bf16[64,32,128]{2,1,0:T(8,128)(2,1)S(1)}, u32[]{:S(2)}, u32[]{:S(2)}) %collective-permute-start.6) | collective-permute-done | bytes 524320 | tf_op jit(solution)/shard_map/ppermute | solution.py:88
  23.6 4.7 %collective-permute-start.9 = (f32[4,32,128]{2,1,0:T(8,128)S(1)}, f32[4,32,128]{2,1,0:T(8,128)S(1)}, u32[]{:S(2)}, u32[]{:S(2)}) collective-permute-start(f32[4,32,128]{2,1,0:T(8,128)S(1)} %shard_map.81.refs_0_), channel_id=1, source_target_pairs={{0,3},{1,0},{2,1},{3,2},{4,7},{5,4},{6,5},{7,6},{8,11},{9,8},{10,9... | collective-permute-start | bytes 196616 | tf_op jit(solution)/shard_map/ppermute | solution.py:295
  28.3 2.5 %collective-permute-start.7 = (f32[4,32,128]{2,1,0:T(8,128)S(1)}, f32[4,32,128]{2,1,0:T(8,128)S(1)}, u32[]{:S(2)}, u32[]{:S(2)}) collective-permute-start(f32[4,32,128]{2,1,0:T(8,128)S(1)} %shard_map.79.refs_0_), channel_id=1, source_target_pairs={{0,2},{1,3},{2,0},{3,1},{4,6},{5,7},{6,4},{7,5},{8,10},{9,11},{10,... | collective-permute-start | bytes 196616 | tf_op jit(solution)/shard_map/ppermute | solution.py:295
  31.4 4.0 %collective-permute-done.8.refs_1_ = f32[4,32,128]{2,1,0:T(8,128)S(1)} collective-permute-done((f32[4,32,128]{2,1,0:T(8,128)S(1)}, f32[4,32,128]{2,1,0:T(8,128)S(1)}, u32[]{:S(2)}, u32[]{:S(2)}) %collective-permute-start.8) | collective-permute-done | bytes 65568 | tf_op jit(solution)/shard_map/ppermute | solution.py:295
  36.1 2.6 %collective-permute-start.11 = (bf16[4,32,128]{2,1,0:T(8,128)(2,1)S(1)}, bf16[4,32,128]{2,1,0:T(8,128)(2,1)S(1)}, u32[]{:S(2)}, u32[]{:S(2)}) collective-permute-start(bf16[4,32,128]{2,1,0:T(8,128)(2,1)S(1)} %get-tuple-element.18.refs_0_), channel_id=1, source_target_pairs={{0,24},{4,100},{8,0},{12,108},{16,8},{20,116},{24,16},{28,124},{32... | collective-permute-start | bytes 98312 | tf_op jit(solution)/shard_map/ppermute | solution.py:79
  39.3 1.6 %collective-permute-done.12.refs_3_ = bf16[4,32,128]{2,1,0:T(8,128)(2,1)S(1)} collective-permute-done((bf16[4,32,128]{2,1,0:T(8,128)(2,1)S(1)}, bf16[4,32,128]{2,1,0:T(8,128)(2,1)S(1)}, u32[]{:S(2)}, u32[]{:S(2)}) %collective-permute-start.12) | collective-permute-done | bytes 32800 | tf_op jit(solution)/shard_map/ppermute | solution.py:79
  41.5 2.3 %collective-permute-done.10.refs_1_ = bf16[4,32,128]{2,1,0:T(8,128)(2,1)S(1)} collective-permute-done((bf16[4,32,128]{2,1,0:T(8,128)(2,1)S(1)}, bf16[4,32,128]{2,1,0:T(8,128)(2,1)S(1)}, u32[]{:S(2)}, u32[]{:S(2)}) %collective-permute-start.10) | collective-permute-done | bytes 32800 | tf_op jit(solution)/shard_map/ppermute | solution.py:79
  43.9 2.0 %collective-permute-start.15 = (bf16[16,32,128]{2,1,0:T(8,128)(2,1)S(1)}, bf16[16,32,128]{2,1,0:T(8,128)(2,1)S(1)}, u32[]{:S(2)}, u32[]{:S(2)}) collective-permute-start(bf16[16,32,128]{2,1,0:T(8,128)(2,1)S(1)} %shard_map.84.refs_0_), channel_id=1, source_target_pairs={{0,64},{4,20},{8,72},{12,28},{16,80},{20,4},{24,88},{28,12},{32,96... | collective-permute-start | bytes 393224 | tf_op jit(solution)/shard_map/ppermute | solution.py:79
  45.9 1.3 %collective-permute-start.14 = (bf16[16,32,128]{2,1,0:T(8,128)(2,1)S(1)}, bf16[16,32,128]{2,1,0:T(8,128)(2,1)S(1)}, u32[]{:S(2)}, u32[]{:S(2)}) collective-permute-start(bf16[16,32,128]{2,1,0:T(8,128)(2,1)S(1)} %shard_map.84.refs_0_), channel_id=1, source_target_pairs={{0,96},{4,28},{8,104},{12,4},{16,112},{20,12},{24,120},{28,20},{32... | collective-permute-start | bytes 393224 | tf_op jit(solution)/shard_map/ppermute | solution.py:79
  47.9 2.5 %collective-permute-done.15.refs_3_ = bf16[16,32,128]{2,1,0:T(8,128)(2,1)S(1)} collective-permute-done((bf16[16,32,128]{2,1,0:T(8,128)(2,1)S(1)}, bf16[16,32,128]{2,1,0:T(8,128)(2,1)S(1)}, u32[]{:S(2)}, u32[]{:S(2)}) %collective-permute-start.15) | collective-permute-done | bytes 131104 | tf_op jit(solution)/shard_map/ppermute | solution.py:79
  50.4 1.9 %collective-permute-done.14.refs_2_ = bf16[16,32,128]{2,1,0:T(8,128)(2,1)S(1)} collective-permute-done((bf16[16,32,128]{2,1,0:T(8,128)(2,1)S(1)}, bf16[16,32,128]{2,1,0:T(8,128)(2,1)S(1)}, u32[]{:S(2)}, u32[]{:S(2)}) %collective-permute-start.14) | collective-permute-done | bytes 131104 | tf_op jit(solution)/shard_map/ppermute | solution.py:79
  53.5 1.9 %collective-permute-done.16.refs_1_ = bf16[64,32,128]{2,1,0:T(8,128)(2,1)S(1)} collective-permute-done((bf16[64,32,128]{2,1,0:T(8,128)(2,1)S(1)}, bf16[64,32,128]{2,1,0:T(8,128)(2,1)S(1)}, u32[]{:S(2)}, u32[]{:S(2)}) %collective-permute-start.16) | collective-permute-done | bytes 524320 | tf_op jit(solution)/shard_map/ppermute | solution.py:88
  56.1 2.3 %collective-permute-start.19 = (f32[4,32,128]{2,1,0:T(8,128)S(1)}, f32[4,32,128]{2,1,0:T(8,128)S(1)}, u32[]{:S(2)}, u32[]{:S(2)}) collective-permute-start(f32[4,32,128]{2,1,0:T(8,128)S(1)} %shard_map.89.refs_0_), channel_id=1, source_target_pairs={{0,3},{1,0},{2,1},{3,2},{4,7},{5,4},{6,5},{7,6},{8,11},{9,8},{10,9... | collective-permute-start | bytes 196616 | tf_op jit(solution)/shard_map/ppermute | solution.py:295
  58.5 1.4 %collective-permute-start.18 = (f32[4,32,128]{2,1,0:T(8,128)S(1)}, f32[4,32,128]{2,1,0:T(8,128)S(1)}, u32[]{:S(2)}, u32[]{:S(2)}) collective-permute-start(f32[4,32,128]{2,1,0:T(8,128)S(1)} %shard_map.88.refs_0_), channel_id=1, source_target_pairs={{0,1},{1,2},{2,3},{3,0},{4,5},{5,6},{6,7},{7,4},{8,9},{9,10},{10,1... | collective-permute-start | bytes 196616 | tf_op jit(solution)/shard_map/ppermute | solution.py:295
  59.9 2.5 %collective-permute-start.17 = (f32[4,32,128]{2,1,0:T(8,128)S(1)}, f32[4,32,128]{2,1,0:T(8,128)S(1)}, u32[]{:S(2)}, u32[]{:S(2)}) collective-permute-start(f32[4,32,128]{2,1,0:T(8,128)S(1)} %shard_map.87.refs_0_), channel_id=1, source_target_pairs={{0,2},{1,3},{2,0},{3,1},{4,6},{5,7},{6,4},{7,5},{8,10},{9,11},{10,... | collective-permute-start | bytes 196616 | tf_op jit(solution)/shard_map/ppermute | solution.py:295
  64.1 2.2 %collective-permute-done.17.refs_0_ = f32[4,32,128]{2,1,0:T(8,128)S(1)} collective-permute-done((f32[4,32,128]{2,1,0:T(8,128)S(1)}, f32[4,32,128]{2,1,0:T(8,128)S(1)}, u32[]{:S(2)}, u32[]{:S(2)}) %collective-permute-start.17) | collective-permute-done | bytes 65568 | tf_op jit(solution)/shard_map/ppermute | solution.py:295
  66.4 1.7 %collective-permute-start.22 = (bf16[4,32,128]{2,1,0:T(8,128)(2,1)S(1)}, bf16[4,32,128]{2,1,0:T(8,128)(2,1)S(1)}, u32[]{:S(2)}, u32[]{:S(2)}) collective-permute-start(bf16[4,32,128]{2,1,0:T(8,128)(2,1)S(1)} %get-tuple-element.20.refs_0_), channel_id=1, source_target_pairs={{0,16},{4,68},{8,24},{12,76},{16,0},{20,84},{24,8},{28,92},{32,48}... | collective-permute-start | bytes 98312 | tf_op jit(solution)/shard_map/ppermute | solution.py:79
  68.5 1.6 %collective-permute-start.20 = (bf16[4,32,128]{2,1,0:T(8,128)(2,1)S(1)}, bf16[4,32,128]{2,1,0:T(8,128)(2,1)S(1)}, u32[]{:S(2)}, u32[]{:S(2)}) collective-permute-start(bf16[4,32,128]{2,1,0:T(8,128)(2,1)S(1)} %get-tuple-element.20.refs_0_), channel_id=1, source_target_pairs={{0,8},{4,36},{8,16},{12,44},{16,24},{20,52},{24,0},{28,60},{32,40}... | collective-permute-start | bytes 98312 | tf_op jit(solution)/shard_map/ppermute | solution.py:79
  70.1 1.7 %collective-permute-done.22.refs_3_ = bf16[4,32,128]{2,1,0:T(8,128)(2,1)S(1)} collective-permute-done((bf16[4,32,128]{2,1,0:T(8,128)(2,1)S(1)}, bf16[4,32,128]{2,1,0:T(8,128)(2,1)S(1)}, u32[]{:S(2)}, u32[]{:S(2)}) %collective-permute-start.22) | collective-permute-done | bytes 32800 | tf_op jit(solution)/shard_map/ppermute | solution.py:79
  72.0 1.6 %collective-permute-done.20.refs_1_ = bf16[4,32,128]{2,1,0:T(8,128)(2,1)S(1)} collective-permute-done((bf16[4,32,128]{2,1,0:T(8,128)(2,1)S(1)}, bf16[4,32,128]{2,1,0:T(8,128)(2,1)S(1)}, u32[]{:S(2)}, u32[]{:S(2)}) %collective-permute-start.20) | collective-permute-done | bytes 32800 | tf_op jit(solution)/shard_map/ppermute | solution.py:79
  73.7 3.3 %collective-permute-start.25 = (bf16[16,32,128]{2,1,0:T(8,128)(2,1)S(1)}, bf16[16,32,128]{2,1,0:T(8,128)(2,1)S(1)}, u32[]{:S(2)}, u32[]{:S(2)}) collective-permute-start(bf16[16,32,128]{2,1,0:T(8,128)(2,1)S(1)} %shard_map.92.refs_0_), channel_id=1, source_target_pairs={{0,64},{4,20},{8,72},{12,28},{16,80},{20,4},{24,88},{28,12},{32,96... | collective-permute-start | bytes 393224 | tf_op jit(solution)/shard_map/ppermute | solution.py:79
  77.0 2.0 %collective-permute-start.23 = (bf16[16,32,128]{2,1,0:T(8,128)(2,1)S(1)}, bf16[16,32,128]{2,1,0:T(8,128)(2,1)S(1)}, u32[]{:S(2)}, u32[]{:S(2)}) collective-permute-start(bf16[16,32,128]{2,1,0:T(8,128)(2,1)S(1)} %shard_map.92.refs_0_), channel_id=1, source_target_pairs={{0,32},{4,12},{8,40},{12,20},{16,48},{20,28},{24,56},{28,4},{32,64... | collective-permute-start | bytes 393224 | tf_op jit(solution)/shard_map/ppermute | solution.py:79
  80.2 1.7 %collective-permute-done.24.refs_2_ = bf16[16,32,128]{2,1,0:T(8,128)(2,1)S(1)} collective-permute-done((bf16[16,32,128]{2,1,0:T(8,128)(2,1)S(1)}, bf16[16,32,128]{2,1,0:T(8,128)(2,1)S(1)}, u32[]{:S(2)}, u32[]{:S(2)}) %collective-permute-start.24) | collective-permute-done | bytes 131104 | tf_op jit(solution)/shard_map/ppermute | solution.py:79
  83.3 1.9 %collective-permute-done.26.refs_1_ = bf16[64,32,128]{2,1,0:T(8,128)(2,1)S(1)} collective-permute-done((bf16[64,32,128]{2,1,0:T(8,128)(2,1)S(1)}, bf16[64,32,128]{2,1,0:T(8,128)(2,1)S(1)}, u32[]{:S(2)}, u32[]{:S(2)}) %collective-permute-start.26) | collective-permute-done | bytes 524320 | tf_op jit(solution)/shard_map/ppermute | solution.py:88
  85.9 1.9 %collective-permute-start.29 = (f32[4,32,128]{2,1,0:T(8,128)S(1)}, f32[4,32,128]{2,1,0:T(8,128)S(1)}, u32[]{:S(2)}, u32[]{:S(2)}) collective-permute-start(f32[4,32,128]{2,1,0:T(8,128)S(1)} %shard_map.97.refs_0_), channel_id=1, source_target_pairs={{0,3},{1,0},{2,1},{3,2},{4,7},{5,4},{6,5},{7,6},{8,11},{9,8},{10,9... | collective-permute-start | bytes 196616 | tf_op jit(solution)/shard_map/ppermute | solution.py:295
  88.3 5.2 %collective-permute-start.27 = (f32[4,32,128]{2,1,0:T(8,128)S(1)}, f32[4,32,128]{2,1,0:T(8,128)S(1)}, u32[]{:S(2)}, u32[]{:S(2)}) collective-permute-start(f32[4,32,128]{2,1,0:T(8,128)S(1)} %shard_map.95.refs_0_), channel_id=1, source_target_pairs={{0,2},{1,3},{2,0},{3,1},{4,6},{5,7},{6,4},{7,5},{8,10},{9,11},{10,... | collective-permute-start | bytes 196616 | tf_op jit(solution)/shard_map/ppermute | solution.py:295
  94.3 2.5 %collective-permute-done.27.refs_0_ = f32[4,32,128]{2,1,0:T(8,128)S(1)} collective-permute-done((f32[4,32,128]{2,1,0:T(8,128)S(1)}, f32[4,32,128]{2,1,0:T(8,128)S(1)}, u32[]{:S(2)}, u32[]{:S(2)}) %collective-permute-start.27) | collective-permute-done | bytes 65568 | tf_op jit(solution)/shard_map/ppermute | solution.py:295
  (59 shorter events, 19.7 us)
Async XLA Ops:
  0.0 0.8 copy-start
  0.8 9.4 %collective-permute-start.2 = (bf16[4,32,128]{2,1,0:T(8,128)(2,1)S(1)}, bf16[4,32,128]{2,1,0:T(8,128)(2,1)S(1)}, u32[]{:S(2)}, u32[]{:S(2)}) collective-permute-start(bf16[4,32,128]{2,1,0:T(8,128)(2,1)S(1)} %shard_map.73._after.refs_0_), channel_id=1, source_target_pairs={{0,16},{4,68},{8,24},{12,76},{16,0},{20,84},{24,8},{28,92},{32,48}... | collective-permute-start | bytes 98312 | tf_op jit(solution)/shard_map/ppermute | solution.py:79
  4.2 6.1 %collective-permute-start.1 = (bf16[4,32,128]{2,1,0:T(8,128)(2,1)S(1)}, bf16[4,32,128]{2,1,0:T(8,128)(2,1)S(1)}, u32[]{:S(2)}, u32[]{:S(2)}) collective-permute-start(bf16[4,32,128]{2,1,0:T(8,128)(2,1)S(1)} %shard_map.73._after.refs_0_), channel_id=1, source_target_pairs={{0,24},{4,100},{8,0},{12,108},{16,8},{20,116},{24,16},{28,124},{32... | collective-permute-start | bytes 98312 | tf_op jit(solution)/shard_map/ppermute | solution.py:79
  5.2 5.1 %collective-permute-start = (bf16[4,32,128]{2,1,0:T(8,128)(2,1)S(1)}, bf16[4,32,128]{2,1,0:T(8,128)(2,1)S(1)}, u32[]{:S(2)}, u32[]{:S(2)}) collective-permute-start(bf16[4,32,128]{2,1,0:T(8,128)(2,1)S(1)} %shard_map.73._after.refs_0_), channel_id=1, source_target_pairs={{0,8},{4,36},{8,16},{12,44},{16,24},{20,52},{24,0},{28,60},{32,40}... | collective-permute-start | bytes 98312 | tf_op jit(solution)/shard_map/ppermute | solution.py:79
  10.3 6.9 %collective-permute-start.5 = (bf16[16,32,128]{2,1,0:T(8,128)(2,1)S(1)}, bf16[16,32,128]{2,1,0:T(8,128)(2,1)S(1)}, u32[]{:S(2)}, u32[]{:S(2)}) collective-permute-start(bf16[16,32,128]{2,1,0:T(8,128)(2,1)S(1)} %shard_map.75._after.refs_0_), channel_id=1, source_target_pairs={{0,64},{4,20},{8,72},{12,28},{16,80},{20,4},{24,88},{28,12},{32,96... | collective-permute-start | bytes 393224 | tf_op jit(solution)/shard_map/ppermute | solution.py:79
  13.5 5.0 %collective-permute-start.4 = (bf16[16,32,128]{2,1,0:T(8,128)(2,1)S(1)}, bf16[16,32,128]{2,1,0:T(8,128)(2,1)S(1)}, u32[]{:S(2)}, u32[]{:S(2)}) collective-permute-start(bf16[16,32,128]{2,1,0:T(8,128)(2,1)S(1)} %shard_map.75._after.refs_0_), channel_id=1, source_target_pairs={{0,96},{4,28},{8,104},{12,4},{16,112},{20,12},{24,120},{28,20},{32... | collective-permute-start | bytes 393224 | tf_op jit(solution)/shard_map/ppermute | solution.py:79
  14.6 6.2 %collective-permute-start.3 = (bf16[16,32,128]{2,1,0:T(8,128)(2,1)S(1)}, bf16[16,32,128]{2,1,0:T(8,128)(2,1)S(1)}, u32[]{:S(2)}, u32[]{:S(2)}) collective-permute-start(bf16[16,32,128]{2,1,0:T(8,128)(2,1)S(1)} %shard_map.75._after.refs_0_), channel_id=1, source_target_pairs={{0,32},{4,12},{8,40},{12,20},{16,48},{20,28},{24,56},{28,4},{32,64... | collective-permute-start | bytes 393224 | tf_op jit(solution)/shard_map/ppermute | solution.py:79
  20.8 2.0 %collective-permute-start.6 = (bf16[64,32,128]{2,1,0:T(8,128)(2,1)S(1)}, bf16[64,32,128]{2,1,0:T(8,128)(2,1)S(1)}, u32[]{:S(2)}, u32[]{:S(2)}) collective-permute-start(bf16[64,32,128]{2,1,0:T(8,128)(2,1)S(1)} %shard_map.77.refs_0_), channel_id=1, source_target_pairs={{0,4},{4,0},{8,12},{12,8},{16,20},{20,16},{24,28},{28,24},{32,36},... | collective-permute-start | bytes 1572872 | tf_op jit(solution)/shard_map/ppermute | solution.py:88
  22.9 12.4 %copy-start.1 = (f32[4,32,128]{2,1,0:T(8,128)S(1)}, f32[4,32,128]{2,1,0:T(8,128)}, u32[]{:S(2)}) copy-start(f32[4,32,128]{2,1,0:T(8,128)} %previous.1) | copy-start | bytes 196612
  23.6 7.8 %collective-permute-start.9 = (f32[4,32,128]{2,1,0:T(8,128)S(1)}, f32[4,32,128]{2,1,0:T(8,128)S(1)}, u32[]{:S(2)}, u32[]{:S(2)}) collective-permute-start(f32[4,32,128]{2,1,0:T(8,128)S(1)} %shard_map.81.refs_0_), channel_id=1, source_target_pairs={{0,3},{1,0},{2,1},{3,2},{4,7},{5,4},{6,5},{7,6},{8,11},{9,8},{10,9... | collective-permute-start | bytes 196616 | tf_op jit(solution)/shard_map/ppermute | solution.py:295
  28.3 7.1 %collective-permute-start.8 = (f32[4,32,128]{2,1,0:T(8,128)S(1)}, f32[4,32,128]{2,1,0:T(8,128)S(1)}, u32[]{:S(2)}, u32[]{:S(2)}) collective-permute-start(f32[4,32,128]{2,1,0:T(8,128)S(1)} %shard_map.80.refs_0_), channel_id=1, source_target_pairs={{0,1},{1,2},{2,3},{3,0},{4,5},{5,6},{6,7},{7,4},{8,9},{9,10},{10,1... | collective-permute-start | bytes 196616 | tf_op jit(solution)/shard_map/ppermute | solution.py:295
  28.3 7.1 %collective-permute-start.7 = (f32[4,32,128]{2,1,0:T(8,128)S(1)}, f32[4,32,128]{2,1,0:T(8,128)S(1)}, u32[]{:S(2)}, u32[]{:S(2)}) collective-permute-start(f32[4,32,128]{2,1,0:T(8,128)S(1)} %shard_map.79.refs_0_), channel_id=1, source_target_pairs={{0,2},{1,3},{2,0},{3,1},{4,6},{5,7},{6,4},{7,5},{8,10},{9,11},{10,... | collective-permute-start | bytes 196616 | tf_op jit(solution)/shard_map/ppermute | solution.py:295
  35.4 5.5 %collective-permute-start.12 = (bf16[4,32,128]{2,1,0:T(8,128)(2,1)S(1)}, bf16[4,32,128]{2,1,0:T(8,128)(2,1)S(1)}, u32[]{:S(2)}, u32[]{:S(2)}) collective-permute-start(bf16[4,32,128]{2,1,0:T(8,128)(2,1)S(1)} %get-tuple-element.18.refs_0_), channel_id=1, source_target_pairs={{0,16},{4,68},{8,24},{12,76},{16,0},{20,84},{24,8},{28,92},{32,48}... | collective-permute-start | bytes 98312 | tf_op jit(solution)/shard_map/ppermute | solution.py:79
  36.1 5.4 %collective-permute-start.11 = (bf16[4,32,128]{2,1,0:T(8,128)(2,1)S(1)}, bf16[4,32,128]{2,1,0:T(8,128)(2,1)S(1)}, u32[]{:S(2)}, u32[]{:S(2)}) collective-permute-start(bf16[4,32,128]{2,1,0:T(8,128)(2,1)S(1)} %get-tuple-element.18.refs_0_), channel_id=1, source_target_pairs={{0,24},{4,100},{8,0},{12,108},{16,8},{20,116},{24,16},{28,124},{32... | collective-permute-start | bytes 98312 | tf_op jit(solution)/shard_map/ppermute | solution.py:79
  38.7 5.1 %collective-permute-start.10 = (bf16[4,32,128]{2,1,0:T(8,128)(2,1)S(1)}, bf16[4,32,128]{2,1,0:T(8,128)(2,1)S(1)}, u32[]{:S(2)}, u32[]{:S(2)}) collective-permute-start(bf16[4,32,128]{2,1,0:T(8,128)(2,1)S(1)} %get-tuple-element.18.refs_0_), channel_id=1, source_target_pairs={{0,8},{4,36},{8,16},{12,44},{16,24},{20,52},{24,0},{28,60},{32,40}... | collective-permute-start | bytes 98312 | tf_op jit(solution)/shard_map/ppermute | solution.py:79
  43.9 6.6 %collective-permute-start.15 = (bf16[16,32,128]{2,1,0:T(8,128)(2,1)S(1)}, bf16[16,32,128]{2,1,0:T(8,128)(2,1)S(1)}, u32[]{:S(2)}, u32[]{:S(2)}) collective-permute-start(bf16[16,32,128]{2,1,0:T(8,128)(2,1)S(1)} %shard_map.84.refs_0_), channel_id=1, source_target_pairs={{0,64},{4,20},{8,72},{12,28},{16,80},{20,4},{24,88},{28,12},{32,96... | collective-permute-start | bytes 393224 | tf_op jit(solution)/shard_map/ppermute | solution.py:79
  45.9 6.4 %collective-permute-start.14 = (bf16[16,32,128]{2,1,0:T(8,128)(2,1)S(1)}, bf16[16,32,128]{2,1,0:T(8,128)(2,1)S(1)}, u32[]{:S(2)}, u32[]{:S(2)}) collective-permute-start(bf16[16,32,128]{2,1,0:T(8,128)(2,1)S(1)} %shard_map.84.refs_0_), channel_id=1, source_target_pairs={{0,96},{4,28},{8,104},{12,4},{16,112},{20,12},{24,120},{28,20},{32... | collective-permute-start | bytes 393224 | tf_op jit(solution)/shard_map/ppermute | solution.py:79
  47.2 6.2 %collective-permute-start.13 = (bf16[16,32,128]{2,1,0:T(8,128)(2,1)S(1)}, bf16[16,32,128]{2,1,0:T(8,128)(2,1)S(1)}, u32[]{:S(2)}, u32[]{:S(2)}) collective-permute-start(bf16[16,32,128]{2,1,0:T(8,128)(2,1)S(1)} %shard_map.84.refs_0_), channel_id=1, source_target_pairs={{0,32},{4,12},{8,40},{12,20},{16,48},{20,28},{24,56},{28,4},{32,64... | collective-permute-start | bytes 393224 | tf_op jit(solution)/shard_map/ppermute | solution.py:79
  53.4 2.0 %collective-permute-start.16 = (bf16[64,32,128]{2,1,0:T(8,128)(2,1)S(1)}, bf16[64,32,128]{2,1,0:T(8,128)(2,1)S(1)}, u32[]{:S(2)}, u32[]{:S(2)}) collective-permute-start(bf16[64,32,128]{2,1,0:T(8,128)(2,1)S(1)} %shard_map.85.refs_0_), channel_id=1, source_target_pairs={{0,4},{4,0},{8,12},{12,8},{16,20},{20,16},{24,28},{28,24},{32,36},... | collective-permute-start | bytes 1572872 | tf_op jit(solution)/shard_map/ppermute | solution.py:88
  56.1 7.0 %collective-permute-start.19 = (f32[4,32,128]{2,1,0:T(8,128)S(1)}, f32[4,32,128]{2,1,0:T(8,128)S(1)}, u32[]{:S(2)}, u32[]{:S(2)}) collective-permute-start(f32[4,32,128]{2,1,0:T(8,128)S(1)} %shard_map.89.refs_0_), channel_id=1, source_target_pairs={{0,3},{1,0},{2,1},{3,2},{4,7},{5,4},{6,5},{7,6},{8,11},{9,8},{10,9... | collective-permute-start | bytes 196616 | tf_op jit(solution)/shard_map/ppermute | solution.py:295
  58.5 5.7 %collective-permute-start.18 = (f32[4,32,128]{2,1,0:T(8,128)S(1)}, f32[4,32,128]{2,1,0:T(8,128)S(1)}, u32[]{:S(2)}, u32[]{:S(2)}) collective-permute-start(f32[4,32,128]{2,1,0:T(8,128)S(1)} %shard_map.88.refs_0_), channel_id=1, source_target_pairs={{0,1},{1,2},{2,3},{3,0},{4,5},{5,6},{6,7},{7,4},{8,9},{9,10},{10,1... | collective-permute-start | bytes 196616 | tf_op jit(solution)/shard_map/ppermute | solution.py:295
  59.9 6.5 %collective-permute-start.17 = (f32[4,32,128]{2,1,0:T(8,128)S(1)}, f32[4,32,128]{2,1,0:T(8,128)S(1)}, u32[]{:S(2)}, u32[]{:S(2)}) collective-permute-start(f32[4,32,128]{2,1,0:T(8,128)S(1)} %shard_map.87.refs_0_), channel_id=1, source_target_pairs={{0,2},{1,3},{2,0},{3,1},{4,6},{5,7},{6,4},{7,5},{8,10},{9,11},{10,... | collective-permute-start | bytes 196616 | tf_op jit(solution)/shard_map/ppermute | solution.py:295
  66.4 5.5 %collective-permute-start.22 = (bf16[4,32,128]{2,1,0:T(8,128)(2,1)S(1)}, bf16[4,32,128]{2,1,0:T(8,128)(2,1)S(1)}, u32[]{:S(2)}, u32[]{:S(2)}) collective-permute-start(bf16[4,32,128]{2,1,0:T(8,128)(2,1)S(1)} %get-tuple-element.20.refs_0_), channel_id=1, source_target_pairs={{0,16},{4,68},{8,24},{12,76},{16,0},{20,84},{24,8},{28,92},{32,48}... | collective-permute-start | bytes 98312 | tf_op jit(solution)/shard_map/ppermute | solution.py:79
  68.1 3.9 %collective-permute-start.21 = (bf16[4,32,128]{2,1,0:T(8,128)(2,1)S(1)}, bf16[4,32,128]{2,1,0:T(8,128)(2,1)S(1)}, u32[]{:S(2)}, u32[]{:S(2)}) collective-permute-start(bf16[4,32,128]{2,1,0:T(8,128)(2,1)S(1)} %get-tuple-element.20.refs_0_), channel_id=1, source_target_pairs={{0,24},{4,100},{8,0},{12,108},{16,8},{20,116},{24,16},{28,124},{32... | collective-permute-start | bytes 98312 | tf_op jit(solution)/shard_map/ppermute | solution.py:79
  68.5 5.1 %collective-permute-start.20 = (bf16[4,32,128]{2,1,0:T(8,128)(2,1)S(1)}, bf16[4,32,128]{2,1,0:T(8,128)(2,1)S(1)}, u32[]{:S(2)}, u32[]{:S(2)}) collective-permute-start(bf16[4,32,128]{2,1,0:T(8,128)(2,1)S(1)} %get-tuple-element.20.refs_0_), channel_id=1, source_target_pairs={{0,8},{4,36},{8,16},{12,44},{16,24},{20,52},{24,0},{28,60},{32,40}... | collective-permute-start | bytes 98312 | tf_op jit(solution)/shard_map/ppermute | solution.py:79
  73.7 6.6 %collective-permute-start.25 = (bf16[16,32,128]{2,1,0:T(8,128)(2,1)S(1)}, bf16[16,32,128]{2,1,0:T(8,128)(2,1)S(1)}, u32[]{:S(2)}, u32[]{:S(2)}) collective-permute-start(bf16[16,32,128]{2,1,0:T(8,128)(2,1)S(1)} %shard_map.92.refs_0_), channel_id=1, source_target_pairs={{0,64},{4,20},{8,72},{12,28},{16,80},{20,4},{24,88},{28,12},{32,96... | collective-permute-start | bytes 393224 | tf_op jit(solution)/shard_map/ppermute | solution.py:79
  77.0 5.0 %collective-permute-start.24 = (bf16[16,32,128]{2,1,0:T(8,128)(2,1)S(1)}, bf16[16,32,128]{2,1,0:T(8,128)(2,1)S(1)}, u32[]{:S(2)}, u32[]{:S(2)}) collective-permute-start(bf16[16,32,128]{2,1,0:T(8,128)(2,1)S(1)} %shard_map.92.refs_0_), channel_id=1, source_target_pairs={{0,96},{4,28},{8,104},{12,4},{16,112},{20,12},{24,120},{28,20},{32... | collective-permute-start | bytes 393224 | tf_op jit(solution)/shard_map/ppermute | solution.py:79
  77.0 6.2 %collective-permute-start.23 = (bf16[16,32,128]{2,1,0:T(8,128)(2,1)S(1)}, bf16[16,32,128]{2,1,0:T(8,128)(2,1)S(1)}, u32[]{:S(2)}, u32[]{:S(2)}) collective-permute-start(bf16[16,32,128]{2,1,0:T(8,128)(2,1)S(1)} %shard_map.92.refs_0_), channel_id=1, source_target_pairs={{0,32},{4,12},{8,40},{12,20},{16,48},{20,28},{24,56},{28,4},{32,64... | collective-permute-start | bytes 393224 | tf_op jit(solution)/shard_map/ppermute | solution.py:79
  83.2 2.0 %collective-permute-start.26 = (bf16[64,32,128]{2,1,0:T(8,128)(2,1)S(1)}, bf16[64,32,128]{2,1,0:T(8,128)(2,1)S(1)}, u32[]{:S(2)}, u32[]{:S(2)}) collective-permute-start(bf16[64,32,128]{2,1,0:T(8,128)(2,1)S(1)} %shard_map.93.refs_0_), channel_id=1, source_target_pairs={{0,4},{4,0},{8,12},{12,8},{16,20},{20,16},{24,28},{28,24},{32,36},... | collective-permute-start | bytes 1572872 | tf_op jit(solution)/shard_map/ppermute | solution.py:88
  85.9 8.2 %collective-permute-start.29 = (f32[4,32,128]{2,1,0:T(8,128)S(1)}, f32[4,32,128]{2,1,0:T(8,128)S(1)}, u32[]{:S(2)}, u32[]{:S(2)}) collective-permute-start(f32[4,32,128]{2,1,0:T(8,128)S(1)} %shard_map.97.refs_0_), channel_id=1, source_target_pairs={{0,3},{1,0},{2,1},{3,2},{4,7},{5,4},{6,5},{7,6},{8,11},{9,8},{10,9... | collective-permute-start | bytes 196616 | tf_op jit(solution)/shard_map/ppermute | solution.py:295
  87.9 6.4 %collective-permute-start.28 = (f32[4,32,128]{2,1,0:T(8,128)S(1)}, f32[4,32,128]{2,1,0:T(8,128)S(1)}, u32[]{:S(2)}, u32[]{:S(2)}) collective-permute-start(f32[4,32,128]{2,1,0:T(8,128)S(1)} %shard_map.96.refs_0_), channel_id=1, source_target_pairs={{0,1},{1,2},{2,3},{3,0},{4,5},{5,6},{6,7},{7,4},{8,9},{9,10},{10,1... | collective-permute-start | bytes 196616 | tf_op jit(solution)/shard_map/ppermute | solution.py:295
  88.3 8.5 %collective-permute-start.27 = (f32[4,32,128]{2,1,0:T(8,128)S(1)}, f32[4,32,128]{2,1,0:T(8,128)S(1)}, u32[]{:S(2)}, u32[]{:S(2)}) collective-permute-start(f32[4,32,128]{2,1,0:T(8,128)S(1)} %shard_map.95.refs_0_), channel_id=1, source_target_pairs={{0,2},{1,3},{2,0},{3,1},{4,6},{5,7},{6,4},{7,5},{8,10},{9,11},{10,... | collective-permute-start | bytes 196616 | tf_op jit(solution)/shard_map/ppermute | solution.py:295

commit v5 on v4

--- a/solution.py
+++ b/solution.py
@@ -238,7 +238,7 @@
             right = store[pl.ds(group * GROUP, GROUP)].reshape(GROUP * size, size)
             sums[table[0, LANES + group]] += jnp.dot(left, right, preferred_element_type=jnp.float32)
 
-    out[...] = sums[first_row : first_row + owned]
+    out[...] = sums[first_row : first_row + owned].astype(out.dtype)
 
 
 def local_products(part, vec, prep, after, owned, parts):
@@ -246,7 +246,7 @@
     _, vecs, size = vec.shape
     return pl.pallas_call(
         functools.partial(products_kernel, part * owned),
-        out_shape=jax.ShapeDtypeStruct((owned, vecs, size), jnp.float32),
+        out_shape=jax.ShapeDtypeStruct((owned, vecs, size), jnp.bfloat16 if part else jnp.float32),
         in_specs=[SMEM] + [VMEM] * (2 + len(after)),
         out_specs=VMEM,
         scratch_shapes=[pltpu.VMEM((owned * parts + 1, vecs, size), jnp.float32)],
@@ -263,7 +263,7 @@
     pieces, (out, out_bf) = refs[:-2], refs[-2:]
     image = pieces[0][...]
     for piece in pieces[1:]:
-        image += piece[...]
+        image += piece[...].astype(jnp.float32)
     value = (image - center[0] * current[...]) / half_width[0]
     out[...] = value
     out_bf[...] = value.astype(out_bf.dtype)
@@ -273,7 +273,7 @@
     pieces, outs = refs[:count], refs[count:]
     image = pieces[0][...]
     for piece in pieces[1:]:
-        image += piece[...]
+        image += piece[...].astype(jnp.float32)
     value = 2.0 * (image - center[0] * current[...]) / half_width[0] - previous[...]
     for out in outs:
         out[...] = value.astype(out.dtype)

time: 97.7 us -> 96.7 us (0.990)
  waiting for transfers between devices: 36.7 us -> 34.8 us
    ppermute x18, starting transfers between devices: 27.6 us -> 31.6 us  [shifted(): lax.ppermute(value, 'row', chip_shifts(stage, step))]
    ppermute x9, starting transfers between devices: 21 us -> 17.4 us  [image_pieces(): lax.ppermute(piece, 'col', [(i, (i + part) % parts) for i in range(parts)])]
    ppermute x9, waiting for transfers between devices: 9.74 us -> 8.09 us  [image_pieces(): lax.ppermute(piece, 'col', [(i, (i + part) % parts) for i in range(parts)])]
  transfers between devices with their start and end apart: 30 -> 30, of which waited for: 23 -> 22; matrix products, arithmetic and copies ran while one was open for 0% -> 0% of each run, Pallas kernels for 6% -> 6%
where the time goes in v5:
time: 96.7 us; the launch traced here: 95.9 us
  starting transfers between devices  49.2 us (51%)
  waiting for transfers between devices  34.8 us (36%)
  Pallas kernels  8.89 us (9%)
  between operations  2.2 us (2%)
    ppermute x18, starting transfers between devices, shifted(): lax.ppermute(value, 'row', chip_shifts(stage, step))  31.6 us
    ppermute x18, waiting for transfers between devices, shifted(): lax.ppermute(value, 'row', chip_shifts(stage, step))  21 us
    ppermute x9, starting transfers between devices, image_pieces(): lax.ppermute(piece, 'col', [(i, (i + part) % parts) for i in range(parts)])  17.4 us
    ppermute x9, waiting for transfers between devices, image_pieces(): lax.ppermute(piece, 'col', [(i, (i + part) % parts) for i in range(parts)])  8.09 us
    ppermute x3, waiting for transfers between devices, all_gathered(): return joined([mine, lax.ppermute(mine, 'row', core_swap())])  5.69 us
    pallas_call x12, Pallas kernels, local_products(): pl.pallas_call(functools.partial(products_kernel, part * owned), out_shap...  4.01 us
    pallas_call x1, Pallas kernels, sort_plan(): pl.pallas_call(functools.partial(plan_kernel, parts, owned), out_shape=[p...  2.09 us
  transfers between devices with their start and end apart: 30, of which 22 were waited for; matrix products, arithmetic and copies ran while one was open for 0% of the time, Pallas kernels for 6%

profile of v5, /device:TPU:0, one launch (start us, length us, event | category | flops | bytes accessed | tf_op | source)
XLA Modules:
  0.0 95.9 jit_solution(11581627954296697523)
XLA Ops:
  0.8 3.3 %collective-permute-start.2 = (bf16[4,32,128]{2,1,0:T(8,128)(2,1)S(1)}, bf16[4,32,128]{2,1,0:T(8,128)(2,1)S(1)}, u32[]{:S(2)}, u32[]{:S(2)}) collective-permute-start(bf16[4,32,128]{2,1,0:T(8,128)(2,1)S(1)} %shard_map.73._after.refs_0_), channel_id=1, source_target_pairs={{0,16},{4,68},{8,24},{12,76},{16,0},{20,84},{24,8},{28,92},{32,48}... | collective-permute-start | bytes 98312 | tf_op jit(solution)/shard_map/ppermute | solution.py:79
  8.1 2.1 %shard_map.74 = (s32[1,640]{1,0:T(1,128)S(4)}, s32[1,1344]{1,0:T(1,128)S(4)}, f32[1]{0:T(128)S(4)}, f32[1]{0:T(128)S(4)}) custom-call(s32[1]{0:T(128)S(6)} %copy.8.live_ref, s32[640]{0:T(1024)} %rows_hbm.1, s32[640]{0:T(1024)} %cols_hbm.1, f32[]{:T(128)S(6)} %copy.9.center, f32[]{:T(128)S(6)} %copy.10.half_width, ...), custom_call_target="tpu_custom_call" | custom-call | flops 1000 | bytes 1000 | tf_op jit(solution)/shard_map/pallas_call | solution.py:169
  10.3 3.1 %collective-permute-start.5 = (bf16[16,32,128]{2,1,0:T(8,128)(2,1)S(1)}, bf16[16,32,128]{2,1,0:T(8,128)(2,1)S(1)}, u32[]{:S(2)}, u32[]{:S(2)}) collective-permute-start(bf16[16,32,128]{2,1,0:T(8,128)(2,1)S(1)} %shard_map.75._after.refs_0_), channel_id=1, source_target_pairs={{0,64},{4,20},{8,72},{12,28},{16,80},{20,4},{24,88},{28,12},{32,96... | collective-permute-start | bytes 393224 | tf_op jit(solution)/shard_map/ppermute | solution.py:79
  15.5 1.7 %shard_map.76.refs_4_.store = bf16[832,128,128]{2,1,0:T(8,128)(2,1)S(1)} custom-call(s32[1,640]{1,0:T(1,128)S(4)} %get-tuple-element.16.place, s32[1,1344]{1,0:T(1,128)S(4)} %get-tuple-element.15.refs_4_.sizes.table, bf16[16,32,128]{2,1,0:T(8,128)(2,1)S(1)} %shard_map.75._after.refs_0_, bf16[640,128,128]{2,1,0:T(8,128)(2,1)} %blocks_hbm.1), custom_call_target="tpu_custom_call" | custom-call | flops 1000 | bytes 20971520 | tf_op jit(solution)/shard_map/pallas_call | solution.py:211
  18.4 2.4 %collective-permute-done.3.refs_1_ = bf16[16,32,128]{2,1,0:T(8,128)(2,1)S(1)} collective-permute-done((bf16[16,32,128]{2,1,0:T(8,128)(2,1)S(1)}, bf16[16,32,128]{2,1,0:T(8,128)(2,1)S(1)}, u32[]{:S(2)}, u32[]{:S(2)}) %collective-permute-start.3) | collective-permute-done | bytes 131104 | tf_op jit(solution)/shard_map/ppermute | solution.py:79
  20.9 1.9 %collective-permute-done.6.refs_1_ = bf16[64,32,128]{2,1,0:T(8,128)(2,1)S(1)} collective-permute-done((bf16[64,32,128]{2,1,0:T(8,128)(2,1)S(1)}, bf16[64,32,128]{2,1,0:T(8,128)(2,1)S(1)}, u32[]{:S(2)}, u32[]{:S(2)}) %collective-permute-start.6) | collective-permute-done | bytes 524320 | tf_op jit(solution)/shard_map/ppermute | solution.py:88
  23.6 4.7 %collective-permute-start.9 = (bf16[4,32,128]{2,1,0:T(8,128)(2,1)S(1)}, bf16[4,32,128]{2,1,0:T(8,128)(2,1)S(1)}, u32[]{:S(2)}, u32[]{:S(2)}) collective-permute-start(bf16[4,32,128]{2,1,0:T(8,128)(2,1)S(1)} %shard_map.81.refs_0_), channel_id=1, source_target_pairs={{0,3},{1,0},{2,1},{3,2},{4,7},{5,4},{6,5},{7,6},{8,11},{9,8},{10,9... | collective-permute-start | bytes 98312 | tf_op jit(solution)/shard_map/ppermute | solution.py:295
  28.3 2.5 %collective-permute-start.7 = (bf16[4,32,128]{2,1,0:T(8,128)(2,1)S(1)}, bf16[4,32,128]{2,1,0:T(8,128)(2,1)S(1)}, u32[]{:S(2)}, u32[]{:S(2)}) collective-permute-start(bf16[4,32,128]{2,1,0:T(8,128)(2,1)S(1)} %shard_map.79.refs_0_), channel_id=1, source_target_pairs={{0,2},{1,3},{2,0},{3,1},{4,6},{5,7},{6,4},{7,5},{8,10},{9,11},{10,... | collective-permute-start | bytes 98312 | tf_op jit(solution)/shard_map/ppermute | solution.py:295
  31.4 2.6 %collective-permute-done.8.refs_1_ = bf16[4,32,128]{2,1,0:T(8,128)(2,1)S(1)} collective-permute-done((bf16[4,32,128]{2,1,0:T(8,128)(2,1)S(1)}, bf16[4,32,128]{2,1,0:T(8,128)(2,1)S(1)}, u32[]{:S(2)}, u32[]{:S(2)}) %collective-permute-start.8) | collective-permute-done | bytes 32800 | tf_op jit(solution)/shard_map/ppermute | solution.py:295
  35.1 2.7 %collective-permute-start.11 = (bf16[4,32,128]{2,1,0:T(8,128)(2,1)S(1)}, bf16[4,32,128]{2,1,0:T(8,128)(2,1)S(1)}, u32[]{:S(2)}, u32[]{:S(2)}) collective-permute-start(bf16[4,32,128]{2,1,0:T(8,128)(2,1)S(1)} %get-tuple-element.18.refs_0_), channel_id=1, source_target_pairs={{0,24},{4,100},{8,0},{12,108},{16,8},{20,116},{24,16},{28,124},{32... | collective-permute-start | bytes 98312 | tf_op jit(solution)/shard_map/ppermute | solution.py:79
  39.5 1.3 %collective-permute-done.11.refs_2_ = bf16[4,32,128]{2,1,0:T(8,128)(2,1)S(1)} collective-permute-done((bf16[4,32,128]{2,1,0:T(8,128)(2,1)S(1)}, bf16[4,32,128]{2,1,0:T(8,128)(2,1)S(1)}, u32[]{:S(2)}, u32[]{:S(2)}) %collective-permute-start.11) | collective-permute-done | bytes 32800 | tf_op jit(solution)/shard_map/ppermute | solution.py:79
  40.8 2.1 %collective-permute-done.10.refs_1_ = bf16[4,32,128]{2,1,0:T(8,128)(2,1)S(1)} collective-permute-done((bf16[4,32,128]{2,1,0:T(8,128)(2,1)S(1)}, bf16[4,32,128]{2,1,0:T(8,128)(2,1)S(1)}, u32[]{:S(2)}, u32[]{:S(2)}) %collective-permute-start.10) | collective-permute-done | bytes 32800 | tf_op jit(solution)/shard_map/ppermute | solution.py:79
  42.9 2.2 %collective-permute-start.15 = (bf16[16,32,128]{2,1,0:T(8,128)(2,1)S(1)}, bf16[16,32,128]{2,1,0:T(8,128)(2,1)S(1)}, u32[]{:S(2)}, u32[]{:S(2)}) collective-permute-start(bf16[16,32,128]{2,1,0:T(8,128)(2,1)S(1)} %shard_map.84.refs_0_), channel_id=1, source_target_pairs={{0,64},{4,20},{8,72},{12,28},{16,80},{20,4},{24,88},{28,12},{32,96... | collective-permute-start | bytes 393224 | tf_op jit(solution)/shard_map/ppermute | solution.py:79
  45.1 1.7 %collective-permute-start.14 = (bf16[16,32,128]{2,1,0:T(8,128)(2,1)S(1)}, bf16[16,32,128]{2,1,0:T(8,128)(2,1)S(1)}, u32[]{:S(2)}, u32[]{:S(2)}) collective-permute-start(bf16[16,32,128]{2,1,0:T(8,128)(2,1)S(1)} %shard_map.84.refs_0_), channel_id=1, source_target_pairs={{0,96},{4,28},{8,104},{12,4},{16,112},{20,12},{24,120},{28,20},{32... | collective-permute-start | bytes 393224 | tf_op jit(solution)/shard_map/ppermute | solution.py:79
  47.6 1.9 %collective-permute-done.15.refs_3_ = bf16[16,32,128]{2,1,0:T(8,128)(2,1)S(1)} collective-permute-done((bf16[16,32,128]{2,1,0:T(8,128)(2,1)S(1)}, bf16[16,32,128]{2,1,0:T(8,128)(2,1)S(1)}, u32[]{:S(2)}, u32[]{:S(2)}) %collective-permute-start.15) | collective-permute-done | bytes 131104 | tf_op jit(solution)/shard_map/ppermute | solution.py:79
  49.5 2.5 %collective-permute-done.14.refs_2_ = bf16[16,32,128]{2,1,0:T(8,128)(2,1)S(1)} collective-permute-done((bf16[16,32,128]{2,1,0:T(8,128)(2,1)S(1)}, bf16[16,32,128]{2,1,0:T(8,128)(2,1)S(1)}, u32[]{:S(2)}, u32[]{:S(2)}) %collective-permute-start.14) | collective-permute-done | bytes 131104 | tf_op jit(solution)/shard_map/ppermute | solution.py:79
  53.1 1.9 %collective-permute-done.16.refs_1_ = bf16[64,32,128]{2,1,0:T(8,128)(2,1)S(1)} collective-permute-done((bf16[64,32,128]{2,1,0:T(8,128)(2,1)S(1)}, bf16[64,32,128]{2,1,0:T(8,128)(2,1)S(1)}, u32[]{:S(2)}, u32[]{:S(2)}) %collective-permute-start.16) | collective-permute-done | bytes 524320 | tf_op jit(solution)/shard_map/ppermute | solution.py:88
  55.8 2.3 %collective-permute-start.19 = (bf16[4,32,128]{2,1,0:T(8,128)(2,1)S(1)}, bf16[4,32,128]{2,1,0:T(8,128)(2,1)S(1)}, u32[]{:S(2)}, u32[]{:S(2)}) collective-permute-start(bf16[4,32,128]{2,1,0:T(8,128)(2,1)S(1)} %shard_map.89.refs_0_), channel_id=1, source_target_pairs={{0,3},{1,0},{2,1},{3,2},{4,7},{5,4},{6,5},{7,6},{8,11},{9,8},{10,9... | collective-permute-start | bytes 98312 | tf_op jit(solution)/shard_map/ppermute | solution.py:295
  58.1 1.4 %collective-permute-start.18 = (bf16[4,32,128]{2,1,0:T(8,128)(2,1)S(1)}, bf16[4,32,128]{2,1,0:T(8,128)(2,1)S(1)}, u32[]{:S(2)}, u32[]{:S(2)}) collective-permute-start(bf16[4,32,128]{2,1,0:T(8,128)(2,1)S(1)} %shard_map.88.refs_0_), channel_id=1, source_target_pairs={{0,1},{1,2},{2,3},{3,0},{4,5},{5,6},{6,7},{7,4},{8,9},{9,10},{10,1... | collective-permute-start | bytes 98312 | tf_op jit(solution)/shard_map/ppermute | solution.py:295
  59.5 2.7 %collective-permute-start.17 = (bf16[4,32,128]{2,1,0:T(8,128)(2,1)S(1)}, bf16[4,32,128]{2,1,0:T(8,128)(2,1)S(1)}, u32[]{:S(2)}, u32[]{:S(2)}) collective-permute-start(bf16[4,32,128]{2,1,0:T(8,128)(2,1)S(1)} %shard_map.87.refs_0_), channel_id=1, source_target_pairs={{0,2},{1,3},{2,0},{3,1},{4,6},{5,7},{6,4},{7,5},{8,10},{9,11},{10,... | collective-permute-start | bytes 98312 | tf_op jit(solution)/shard_map/ppermute | solution.py:295
  63.2 1.7 %collective-permute-done.17.refs_0_ = bf16[4,32,128]{2,1,0:T(8,128)(2,1)S(1)} collective-permute-done((bf16[4,32,128]{2,1,0:T(8,128)(2,1)S(1)}, bf16[4,32,128]{2,1,0:T(8,128)(2,1)S(1)}, u32[]{:S(2)}, u32[]{:S(2)}) %collective-permute-start.17) | collective-permute-done | bytes 32800 | tf_op jit(solution)/shard_map/ppermute | solution.py:295
  65.0 1.9 %collective-permute-start.22 = (bf16[4,32,128]{2,1,0:T(8,128)(2,1)S(1)}, bf16[4,32,128]{2,1,0:T(8,128)(2,1)S(1)}, u32[]{:S(2)}, u32[]{:S(2)}) collective-permute-start(bf16[4,32,128]{2,1,0:T(8,128)(2,1)S(1)} %get-tuple-element.20.refs_0_), channel_id=1, source_target_pairs={{0,16},{4,68},{8,24},{12,76},{16,0},{20,84},{24,8},{28,92},{32,48}... | collective-permute-start | bytes 98312 | tf_op jit(solution)/shard_map/ppermute | solution.py:79
  67.3 1.6 %collective-permute-start.20 = (bf16[4,32,128]{2,1,0:T(8,128)(2,1)S(1)}, bf16[4,32,128]{2,1,0:T(8,128)(2,1)S(1)}, u32[]{:S(2)}, u32[]{:S(2)}) collective-permute-start(bf16[4,32,128]{2,1,0:T(8,128)(2,1)S(1)} %get-tuple-element.20.refs_0_), channel_id=1, source_target_pairs={{0,8},{4,36},{8,16},{12,44},{16,24},{20,52},{24,0},{28,60},{32,40}... | collective-permute-start | bytes 98312 | tf_op jit(solution)/shard_map/ppermute | solution.py:79
  68.9 1.6 %collective-permute-done.22.refs_3_ = bf16[4,32,128]{2,1,0:T(8,128)(2,1)S(1)} collective-permute-done((bf16[4,32,128]{2,1,0:T(8,128)(2,1)S(1)}, bf16[4,32,128]{2,1,0:T(8,128)(2,1)S(1)}, u32[]{:S(2)}, u32[]{:S(2)}) %collective-permute-start.22) | collective-permute-done | bytes 32800 | tf_op jit(solution)/shard_map/ppermute | solution.py:79
  70.8 1.6 %collective-permute-done.20.refs_1_ = bf16[4,32,128]{2,1,0:T(8,128)(2,1)S(1)} collective-permute-done((bf16[4,32,128]{2,1,0:T(8,128)(2,1)S(1)}, bf16[4,32,128]{2,1,0:T(8,128)(2,1)S(1)}, u32[]{:S(2)}, u32[]{:S(2)}) %collective-permute-start.20) | collective-permute-done | bytes 32800 | tf_op jit(solution)/shard_map/ppermute | solution.py:79
  72.4 5.8 %collective-permute-start.25 = (bf16[16,32,128]{2,1,0:T(8,128)(2,1)S(1)}, bf16[16,32,128]{2,1,0:T(8,128)(2,1)S(1)}, u32[]{:S(2)}, u32[]{:S(2)}) collective-permute-start(bf16[16,32,128]{2,1,0:T(8,128)(2,1)S(1)} %shard_map.92.refs_0_), channel_id=1, source_target_pairs={{0,64},{4,20},{8,72},{12,28},{16,80},{20,4},{24,88},{28,12},{32,96... | collective-permute-start | bytes 393224 | tf_op jit(solution)/shard_map/ppermute | solution.py:79
  78.3 2.0 %collective-permute-start.23 = (bf16[16,32,128]{2,1,0:T(8,128)(2,1)S(1)}, bf16[16,32,128]{2,1,0:T(8,128)(2,1)S(1)}, u32[]{:S(2)}, u32[]{:S(2)}) collective-permute-start(bf16[16,32,128]{2,1,0:T(8,128)(2,1)S(1)} %shard_map.92.refs_0_), channel_id=1, source_target_pairs={{0,32},{4,12},{8,40},{12,20},{16,48},{20,28},{24,56},{28,4},{32,64... | collective-permute-start | bytes 393224 | tf_op jit(solution)/shard_map/ppermute | solution.py:79
  81.2 2.0 %collective-permute-done.24.refs_2_ = bf16[16,32,128]{2,1,0:T(8,128)(2,1)S(1)} collective-permute-done((bf16[16,32,128]{2,1,0:T(8,128)(2,1)S(1)}, bf16[16,32,128]{2,1,0:T(8,128)(2,1)S(1)}, u32[]{:S(2)}, u32[]{:S(2)}) %collective-permute-start.24) | collective-permute-done | bytes 131104 | tf_op jit(solution)/shard_map/ppermute | solution.py:79
  84.6 1.9 %collective-permute-done.26.refs_1_ = bf16[64,32,128]{2,1,0:T(8,128)(2,1)S(1)} collective-permute-done((bf16[64,32,128]{2,1,0:T(8,128)(2,1)S(1)}, bf16[64,32,128]{2,1,0:T(8,128)(2,1)S(1)}, u32[]{:S(2)}, u32[]{:S(2)}) %collective-permute-start.26) | collective-permute-done | bytes 524320 | tf_op jit(solution)/shard_map/ppermute | solution.py:88
  87.2 2.3 %collective-permute-start.29 = (bf16[4,32,128]{2,1,0:T(8,128)(2,1)S(1)}, bf16[4,32,128]{2,1,0:T(8,128)(2,1)S(1)}, u32[]{:S(2)}, u32[]{:S(2)}) collective-permute-start(bf16[4,32,128]{2,1,0:T(8,128)(2,1)S(1)} %shard_map.97.refs_0_), channel_id=1, source_target_pairs={{0,3},{1,0},{2,1},{3,2},{4,7},{5,4},{6,5},{7,6},{8,11},{9,8},{10,9... | collective-permute-start | bytes 98312 | tf_op jit(solution)/shard_map/ppermute | solution.py:295
  89.5 1.5 %collective-permute-start.27 = (bf16[4,32,128]{2,1,0:T(8,128)(2,1)S(1)}, bf16[4,32,128]{2,1,0:T(8,128)(2,1)S(1)}, u32[]{:S(2)}, u32[]{:S(2)}) collective-permute-start(bf16[4,32,128]{2,1,0:T(8,128)(2,1)S(1)} %shard_map.95.refs_0_), channel_id=1, source_target_pairs={{0,2},{1,3},{2,0},{3,1},{4,6},{5,7},{6,4},{7,5},{8,10},{9,11},{10,... | collective-permute-start | bytes 98312 | tf_op jit(solution)/shard_map/ppermute | solution.py:295
  91.7 3.6 %collective-permute-done.28.refs_1_ = bf16[4,32,128]{2,1,0:T(8,128)(2,1)S(1)} collective-permute-done((bf16[4,32,128]{2,1,0:T(8,128)(2,1)S(1)}, bf16[4,32,128]{2,1,0:T(8,128)(2,1)S(1)}, u32[]{:S(2)}, u32[]{:S(2)}) %collective-permute-start.28) | collective-permute-done | bytes 32800 | tf_op jit(solution)/shard_map/ppermute | solution.py:295
  (59 shorter events, 19.3 us)
Async XLA Ops:
  0.0 0.8 copy-start
  0.8 9.4 %collective-permute-start.2 = (bf16[4,32,128]{2,1,0:T(8,128)(2,1)S(1)}, bf16[4,32,128]{2,1,0:T(8,128)(2,1)S(1)}, u32[]{:S(2)}, u32[]{:S(2)}) collective-permute-start(bf16[4,32,128]{2,1,0:T(8,128)(2,1)S(1)} %shard_map.73._after.refs_0_), channel_id=1, source_target_pairs={{0,16},{4,68},{8,24},{12,76},{16,0},{20,84},{24,8},{28,92},{32,48}... | collective-permute-start | bytes 98312 | tf_op jit(solution)/shard_map/ppermute | solution.py:79
  4.2 6.1 %collective-permute-start.1 = (bf16[4,32,128]{2,1,0:T(8,128)(2,1)S(1)}, bf16[4,32,128]{2,1,0:T(8,128)(2,1)S(1)}, u32[]{:S(2)}, u32[]{:S(2)}) collective-permute-start(bf16[4,32,128]{2,1,0:T(8,128)(2,1)S(1)} %shard_map.73._after.refs_0_), channel_id=1, source_target_pairs={{0,24},{4,100},{8,0},{12,108},{16,8},{20,116},{24,16},{28,124},{32... | collective-permute-start | bytes 98312 | tf_op jit(solution)/shard_map/ppermute | solution.py:79
  5.2 5.1 %collective-permute-start = (bf16[4,32,128]{2,1,0:T(8,128)(2,1)S(1)}, bf16[4,32,128]{2,1,0:T(8,128)(2,1)S(1)}, u32[]{:S(2)}, u32[]{:S(2)}) collective-permute-start(bf16[4,32,128]{2,1,0:T(8,128)(2,1)S(1)} %shard_map.73._after.refs_0_), channel_id=1, source_target_pairs={{0,8},{4,36},{8,16},{12,44},{16,24},{20,52},{24,0},{28,60},{32,40}... | collective-permute-start | bytes 98312 | tf_op jit(solution)/shard_map/ppermute | solution.py:79
  10.3 6.9 %collective-permute-start.5 = (bf16[16,32,128]{2,1,0:T(8,128)(2,1)S(1)}, bf16[16,32,128]{2,1,0:T(8,128)(2,1)S(1)}, u32[]{:S(2)}, u32[]{:S(2)}) collective-permute-start(bf16[16,32,128]{2,1,0:T(8,128)(2,1)S(1)} %shard_map.75._after.refs_0_), channel_id=1, source_target_pairs={{0,64},{4,20},{8,72},{12,28},{16,80},{20,4},{24,88},{28,12},{32,96... | collective-permute-start | bytes 393224 | tf_op jit(solution)/shard_map/ppermute | solution.py:79
  13.5 5.0 %collective-permute-start.4 = (bf16[16,32,128]{2,1,0:T(8,128)(2,1)S(1)}, bf16[16,32,128]{2,1,0:T(8,128)(2,1)S(1)}, u32[]{:S(2)}, u32[]{:S(2)}) collective-permute-start(bf16[16,32,128]{2,1,0:T(8,128)(2,1)S(1)} %shard_map.75._after.refs_0_), channel_id=1, source_target_pairs={{0,96},{4,28},{8,104},{12,4},{16,112},{20,12},{24,120},{28,20},{32... | collective-permute-start | bytes 393224 | tf_op jit(solution)/shard_map/ppermute | solution.py:79
  14.6 6.2 %collective-permute-start.3 = (bf16[16,32,128]{2,1,0:T(8,128)(2,1)S(1)}, bf16[16,32,128]{2,1,0:T(8,128)(2,1)S(1)}, u32[]{:S(2)}, u32[]{:S(2)}) collective-permute-start(bf16[16,32,128]{2,1,0:T(8,128)(2,1)S(1)} %shard_map.75._after.refs_0_), channel_id=1, source_target_pairs={{0,32},{4,12},{8,40},{12,20},{16,48},{20,28},{24,56},{28,4},{32,64... | collective-permute-start | bytes 393224 | tf_op jit(solution)/shard_map/ppermute | solution.py:79
  20.8 2.0 %collective-permute-start.6 = (bf16[64,32,128]{2,1,0:T(8,128)(2,1)S(1)}, bf16[64,32,128]{2,1,0:T(8,128)(2,1)S(1)}, u32[]{:S(2)}, u32[]{:S(2)}) collective-permute-start(bf16[64,32,128]{2,1,0:T(8,128)(2,1)S(1)} %shard_map.77.refs_0_), channel_id=1, source_target_pairs={{0,4},{4,0},{8,12},{12,8},{16,20},{20,16},{24,28},{28,24},{32,36},... | collective-permute-start | bytes 1572872 | tf_op jit(solution)/shard_map/ppermute | solution.py:88
  22.9 11.0 %copy-start.1 = (f32[4,32,128]{2,1,0:T(8,128)S(1)}, f32[4,32,128]{2,1,0:T(8,128)}, u32[]{:S(2)}) copy-start(f32[4,32,128]{2,1,0:T(8,128)} %previous.1) | copy-start | bytes 196612
  23.6 7.8 %collective-permute-start.9 = (bf16[4,32,128]{2,1,0:T(8,128)(2,1)S(1)}, bf16[4,32,128]{2,1,0:T(8,128)(2,1)S(1)}, u32[]{:S(2)}, u32[]{:S(2)}) collective-permute-start(bf16[4,32,128]{2,1,0:T(8,128)(2,1)S(1)} %shard_map.81.refs_0_), channel_id=1, source_target_pairs={{0,3},{1,0},{2,1},{3,2},{4,7},{5,4},{6,5},{7,6},{8,11},{9,8},{10,9... | collective-permute-start | bytes 98312 | tf_op jit(solution)/shard_map/ppermute | solution.py:295
  28.3 5.7 %collective-permute-start.8 = (bf16[4,32,128]{2,1,0:T(8,128)(2,1)S(1)}, bf16[4,32,128]{2,1,0:T(8,128)(2,1)S(1)}, u32[]{:S(2)}, u32[]{:S(2)}) collective-permute-start(bf16[4,32,128]{2,1,0:T(8,128)(2,1)S(1)} %shard_map.80.refs_0_), channel_id=1, source_target_pairs={{0,1},{1,2},{2,3},{3,0},{4,5},{5,6},{6,7},{7,4},{8,9},{9,10},{10,1... | collective-permute-start | bytes 98312 | tf_op jit(solution)/shard_map/ppermute | solution.py:295
  28.3 5.7 %collective-permute-start.7 = (bf16[4,32,128]{2,1,0:T(8,128)(2,1)S(1)}, bf16[4,32,128]{2,1,0:T(8,128)(2,1)S(1)}, u32[]{:S(2)}, u32[]{:S(2)}) collective-permute-start(bf16[4,32,128]{2,1,0:T(8,128)(2,1)S(1)} %shard_map.79.refs_0_), channel_id=1, source_target_pairs={{0,2},{1,3},{2,0},{3,1},{4,6},{5,7},{6,4},{7,5},{8,10},{9,11},{10,... | collective-permute-start | bytes 98312 | tf_op jit(solution)/shard_map/ppermute | solution.py:295
  34.0 5.5 %collective-permute-start.12 = (bf16[4,32,128]{2,1,0:T(8,128)(2,1)S(1)}, bf16[4,32,128]{2,1,0:T(8,128)(2,1)S(1)}, u32[]{:S(2)}, u32[]{:S(2)}) collective-permute-start(bf16[4,32,128]{2,1,0:T(8,128)(2,1)S(1)} %get-tuple-element.18.refs_0_), channel_id=1, source_target_pairs={{0,16},{4,68},{8,24},{12,76},{16,0},{20,84},{24,8},{28,92},{32,48}... | collective-permute-start | bytes 98312 | tf_op jit(solution)/shard_map/ppermute | solution.py:79
  35.1 5.7 %collective-permute-start.11 = (bf16[4,32,128]{2,1,0:T(8,128)(2,1)S(1)}, bf16[4,32,128]{2,1,0:T(8,128)(2,1)S(1)}, u32[]{:S(2)}, u32[]{:S(2)}) collective-permute-start(bf16[4,32,128]{2,1,0:T(8,128)(2,1)S(1)} %get-tuple-element.18.refs_0_), channel_id=1, source_target_pairs={{0,24},{4,100},{8,0},{12,108},{16,8},{20,116},{24,16},{28,124},{32... | collective-permute-start | bytes 98312 | tf_op jit(solution)/shard_map/ppermute | solution.py:79
  37.8 5.1 %collective-permute-start.10 = (bf16[4,32,128]{2,1,0:T(8,128)(2,1)S(1)}, bf16[4,32,128]{2,1,0:T(8,128)(2,1)S(1)}, u32[]{:S(2)}, u32[]{:S(2)}) collective-permute-start(bf16[4,32,128]{2,1,0:T(8,128)(2,1)S(1)} %get-tuple-element.18.refs_0_), channel_id=1, source_target_pairs={{0,8},{4,36},{8,16},{12,44},{16,24},{20,52},{24,0},{28,60},{32,40}... | collective-permute-start | bytes 98312 | tf_op jit(solution)/shard_map/ppermute | solution.py:79
  42.9 6.6 %collective-permute-start.15 = (bf16[16,32,128]{2,1,0:T(8,128)(2,1)S(1)}, bf16[16,32,128]{2,1,0:T(8,128)(2,1)S(1)}, u32[]{:S(2)}, u32[]{:S(2)}) collective-permute-start(bf16[16,32,128]{2,1,0:T(8,128)(2,1)S(1)} %shard_map.84.refs_0_), channel_id=1, source_target_pairs={{0,64},{4,20},{8,72},{12,28},{16,80},{20,4},{24,88},{28,12},{32,96... | collective-permute-start | bytes 393224 | tf_op jit(solution)/shard_map/ppermute | solution.py:79
  45.1 6.9 %collective-permute-start.14 = (bf16[16,32,128]{2,1,0:T(8,128)(2,1)S(1)}, bf16[16,32,128]{2,1,0:T(8,128)(2,1)S(1)}, u32[]{:S(2)}, u32[]{:S(2)}) collective-permute-start(bf16[16,32,128]{2,1,0:T(8,128)(2,1)S(1)} %shard_map.84.refs_0_), channel_id=1, source_target_pairs={{0,96},{4,28},{8,104},{12,4},{16,112},{20,12},{24,120},{28,20},{32... | collective-permute-start | bytes 393224 | tf_op jit(solution)/shard_map/ppermute | solution.py:79
  46.8 6.2 %collective-permute-start.13 = (bf16[16,32,128]{2,1,0:T(8,128)(2,1)S(1)}, bf16[16,32,128]{2,1,0:T(8,128)(2,1)S(1)}, u32[]{:S(2)}, u32[]{:S(2)}) collective-permute-start(bf16[16,32,128]{2,1,0:T(8,128)(2,1)S(1)} %shard_map.84.refs_0_), channel_id=1, source_target_pairs={{0,32},{4,12},{8,40},{12,20},{16,48},{20,28},{24,56},{28,4},{32,64... | collective-permute-start | bytes 393224 | tf_op jit(solution)/shard_map/ppermute | solution.py:79
  53.1 2.0 %collective-permute-start.16 = (bf16[64,32,128]{2,1,0:T(8,128)(2,1)S(1)}, bf16[64,32,128]{2,1,0:T(8,128)(2,1)S(1)}, u32[]{:S(2)}, u32[]{:S(2)}) collective-permute-start(bf16[64,32,128]{2,1,0:T(8,128)(2,1)S(1)} %shard_map.85.refs_0_), channel_id=1, source_target_pairs={{0,4},{4,0},{8,12},{12,8},{16,20},{20,16},{24,28},{28,24},{32,36},... | collective-permute-start | bytes 1572872 | tf_op jit(solution)/shard_map/ppermute | solution.py:88
  55.8 7.2 %collective-permute-start.19 = (bf16[4,32,128]{2,1,0:T(8,128)(2,1)S(1)}, bf16[4,32,128]{2,1,0:T(8,128)(2,1)S(1)}, u32[]{:S(2)}, u32[]{:S(2)}) collective-permute-start(bf16[4,32,128]{2,1,0:T(8,128)(2,1)S(1)} %shard_map.89.refs_0_), channel_id=1, source_target_pairs={{0,3},{1,0},{2,1},{3,2},{4,7},{5,4},{6,5},{7,6},{8,11},{9,8},{10,9... | collective-permute-start | bytes 98312 | tf_op jit(solution)/shard_map/ppermute | solution.py:295
  58.1 5.1 %collective-permute-start.18 = (bf16[4,32,128]{2,1,0:T(8,128)(2,1)S(1)}, bf16[4,32,128]{2,1,0:T(8,128)(2,1)S(1)}, u32[]{:S(2)}, u32[]{:S(2)}) collective-permute-start(bf16[4,32,128]{2,1,0:T(8,128)(2,1)S(1)} %shard_map.88.refs_0_), channel_id=1, source_target_pairs={{0,1},{1,2},{2,3},{3,0},{4,5},{5,6},{6,7},{7,4},{8,9},{9,10},{10,1... | collective-permute-start | bytes 98312 | tf_op jit(solution)/shard_map/ppermute | solution.py:295
  59.5 5.4 %collective-permute-start.17 = (bf16[4,32,128]{2,1,0:T(8,128)(2,1)S(1)}, bf16[4,32,128]{2,1,0:T(8,128)(2,1)S(1)}, u32[]{:S(2)}, u32[]{:S(2)}) collective-permute-start(bf16[4,32,128]{2,1,0:T(8,128)(2,1)S(1)} %shard_map.87.refs_0_), channel_id=1, source_target_pairs={{0,2},{1,3},{2,0},{3,1},{4,6},{5,7},{6,4},{7,5},{8,10},{9,11},{10,... | collective-permute-start | bytes 98312 | tf_op jit(solution)/shard_map/ppermute | solution.py:295
  65.0 5.5 %collective-permute-start.22 = (bf16[4,32,128]{2,1,0:T(8,128)(2,1)S(1)}, bf16[4,32,128]{2,1,0:T(8,128)(2,1)S(1)}, u32[]{:S(2)}, u32[]{:S(2)}) collective-permute-start(bf16[4,32,128]{2,1,0:T(8,128)(2,1)S(1)} %get-tuple-element.20.refs_0_), channel_id=1, source_target_pairs={{0,16},{4,68},{8,24},{12,76},{16,0},{20,84},{24,8},{28,92},{32,48}... | collective-permute-start | bytes 98312 | tf_op jit(solution)/shard_map/ppermute | solution.py:79
  66.9 3.9 %collective-permute-start.21 = (bf16[4,32,128]{2,1,0:T(8,128)(2,1)S(1)}, bf16[4,32,128]{2,1,0:T(8,128)(2,1)S(1)}, u32[]{:S(2)}, u32[]{:S(2)}) collective-permute-start(bf16[4,32,128]{2,1,0:T(8,128)(2,1)S(1)} %get-tuple-element.20.refs_0_), channel_id=1, source_target_pairs={{0,24},{4,100},{8,0},{12,108},{16,8},{20,116},{24,16},{28,124},{32... | collective-permute-start | bytes 98312 | tf_op jit(solution)/shard_map/ppermute | solution.py:79
  67.3 5.1 %collective-permute-start.20 = (bf16[4,32,128]{2,1,0:T(8,128)(2,1)S(1)}, bf16[4,32,128]{2,1,0:T(8,128)(2,1)S(1)}, u32[]{:S(2)}, u32[]{:S(2)}) collective-permute-start(bf16[4,32,128]{2,1,0:T(8,128)(2,1)S(1)} %get-tuple-element.20.refs_0_), channel_id=1, source_target_pairs={{0,8},{4,36},{8,16},{12,44},{16,24},{20,52},{24,0},{28,60},{32,40}... | collective-permute-start | bytes 98312 | tf_op jit(solution)/shard_map/ppermute | solution.py:79
  72.4 8.8 %collective-permute-start.25 = (bf16[16,32,128]{2,1,0:T(8,128)(2,1)S(1)}, bf16[16,32,128]{2,1,0:T(8,128)(2,1)S(1)}, u32[]{:S(2)}, u32[]{:S(2)}) collective-permute-start(bf16[16,32,128]{2,1,0:T(8,128)(2,1)S(1)} %shard_map.92.refs_0_), channel_id=1, source_target_pairs={{0,64},{4,20},{8,72},{12,28},{16,80},{20,4},{24,88},{28,12},{32,96... | collective-permute-start | bytes 393224 | tf_op jit(solution)/shard_map/ppermute | solution.py:79
  78.3 5.0 %collective-permute-start.24 = (bf16[16,32,128]{2,1,0:T(8,128)(2,1)S(1)}, bf16[16,32,128]{2,1,0:T(8,128)(2,1)S(1)}, u32[]{:S(2)}, u32[]{:S(2)}) collective-permute-start(bf16[16,32,128]{2,1,0:T(8,128)(2,1)S(1)} %shard_map.92.refs_0_), channel_id=1, source_target_pairs={{0,96},{4,28},{8,104},{12,4},{16,112},{20,12},{24,120},{28,20},{32... | collective-permute-start | bytes 393224 | tf_op jit(solution)/shard_map/ppermute | solution.py:79
  78.3 6.2 %collective-permute-start.23 = (bf16[16,32,128]{2,1,0:T(8,128)(2,1)S(1)}, bf16[16,32,128]{2,1,0:T(8,128)(2,1)S(1)}, u32[]{:S(2)}, u32[]{:S(2)}) collective-permute-start(bf16[16,32,128]{2,1,0:T(8,128)(2,1)S(1)} %shard_map.92.refs_0_), channel_id=1, source_target_pairs={{0,32},{4,12},{8,40},{12,20},{16,48},{20,28},{24,56},{28,4},{32,64... | collective-permute-start | bytes 393224 | tf_op jit(solution)/shard_map/ppermute | solution.py:79
  84.5 2.0 %collective-permute-start.26 = (bf16[64,32,128]{2,1,0:T(8,128)(2,1)S(1)}, bf16[64,32,128]{2,1,0:T(8,128)(2,1)S(1)}, u32[]{:S(2)}, u32[]{:S(2)}) collective-permute-start(bf16[64,32,128]{2,1,0:T(8,128)(2,1)S(1)} %shard_map.93.refs_0_), channel_id=1, source_target_pairs={{0,4},{4,0},{8,12},{12,8},{16,20},{20,16},{24,28},{28,24},{32,36},... | collective-permute-start | bytes 1572872 | tf_op jit(solution)/shard_map/ppermute | solution.py:88
  87.2 4.4 %collective-permute-start.29 = (bf16[4,32,128]{2,1,0:T(8,128)(2,1)S(1)}, bf16[4,32,128]{2,1,0:T(8,128)(2,1)S(1)}, u32[]{:S(2)}, u32[]{:S(2)}) collective-permute-start(bf16[4,32,128]{2,1,0:T(8,128)(2,1)S(1)} %shard_map.97.refs_0_), channel_id=1, source_target_pairs={{0,3},{1,0},{2,1},{3,2},{4,7},{5,4},{6,5},{7,6},{8,11},{9,8},{10,9... | collective-permute-start | bytes 98312 | tf_op jit(solution)/shard_map/ppermute | solution.py:295
  89.5 5.7 %collective-permute-start.28 = (bf16[4,32,128]{2,1,0:T(8,128)(2,1)S(1)}, bf16[4,32,128]{2,1,0:T(8,128)(2,1)S(1)}, u32[]{:S(2)}, u32[]{:S(2)}) collective-permute-start(bf16[4,32,128]{2,1,0:T(8,128)(2,1)S(1)} %shard_map.96.refs_0_), channel_id=1, source_target_pairs={{0,1},{1,2},{2,3},{3,0},{4,5},{5,6},{6,7},{7,4},{8,9},{9,10},{10,1... | collective-permute-start | bytes 98312 | tf_op jit(solution)/shard_map/ppermute | solution.py:295
  89.5 5.7 %collective-permute-start.27 = (bf16[4,32,128]{2,1,0:T(8,128)(2,1)S(1)}, bf16[4,32,128]{2,1,0:T(8,128)(2,1)S(1)}, u32[]{:S(2)}, u32[]{:S(2)}) collective-permute-start(bf16[4,32,128]{2,1,0:T(8,128)(2,1)S(1)} %shard_map.95.refs_0_), channel_id=1, source_target_pairs={{0,2},{1,3},{2,0},{3,1},{4,6},{5,7},{6,4},{7,5},{8,10},{9,11},{10,... | collective-permute-start | bytes 98312 | tf_op jit(solution)/shard_map/ppermute | solution.py:295

commit v6 on v4

--- a/solution.py
+++ b/solution.py
@@ -37,16 +37,18 @@
     )
 
 
-def join_kernel(places, *refs):
-    parts, out = refs[: len(places)], refs[-1]
-    size = parts[0].shape[0]
-    for place, part in zip(places, parts):
-        out[place * size : (place + 1) * size] = part[...]
-
-
-def joined(parts, after=(), after_specs=(), places=(0, 1)):
-    shape = (len(parts) * parts[0].shape[0], *parts[0].shape[1:])
-    kernel = functools.partial(join_kernel, places)
+def join_kernel(starts, *refs):
+    out = refs[-1]
+    for start, part in zip(starts, refs):
+        out[start : start + part.shape[0]] = part[...]
+
+
+def joined(parts, after=(), after_specs=(), places=None):
+    starts = [sum(part.shape[0] for part in parts[:k]) for k in range(len(parts))]
+    if places:
+        starts = [place * parts[0].shape[0] for place in places]
+    shape = (sum(part.shape[0] for part in parts), *parts[0].shape[1:])
+    kernel = functools.partial(join_kernel, starts)
     specs = [VMEM] * len(parts) + list(after_specs or [VMEM] * len(after))
     return small_call(kernel, jax.ShapeDtypeStruct(shape, parts[0].dtype), specs)(*parts, *after)
 
@@ -84,8 +86,10 @@
 
 
 def all_gathered(line, after=()):
-    mine = joined(shifted(line, 1), after, (), (0, *STEP_ORDER))
-    return joined([mine, lax.ppermute(mine, "row", core_swap())])
+    their_line = lax.ppermute(line, "row", core_swap())
+    rest = joined(shifted(line, 1)[1:], (*after, their_line), (), [step - 1 for step in STEP_ORDER])
+    their_rest = lax.ppermute(rest, "row", core_swap())
+    return joined([line, rest, their_line, their_rest])
 
 
 def padded_room(slots, span):

time: 97.7 us -> 96.1 us (0.984)
  starting transfers between devices: 48.8 us -> 46.3 us
    ppermute x9, starting transfers between devices: 21 us -> 18.2 us  [image_pieces(): lax.ppermute(piece, 'col', [(i, (i + part) % parts) for i in range(parts)])]
    ppermute x3 -> x6, waiting for transfers between devices: 5.69 us -> 5.14 us  [the longest x3 5.13 us: all_gathered(): their_rest = lax.ppermute(rest, 'row', core_swap())]
  transfers between devices with their start and end apart: 30 -> 33, of which waited for: 23 -> 22; matrix products, arithmetic and copies ran while one was open for 0% -> 0% of each run, Pallas kernels for 6% -> 6%
where the time goes in v6:
time: 96.1 us; the launch traced here: 94.8 us
  starting transfers between devices  46.3 us (48%)
  waiting for transfers between devices  36.8 us (38%)
  Pallas kernels  8.67 us (9%)
  between operations  2.22 us (2%)
    ppermute x18, starting transfers between devices, shifted(): lax.ppermute(value, 'row', chip_shifts(stage, step))  27.4 us
    ppermute x18, waiting for transfers between devices, shifted(): lax.ppermute(value, 'row', chip_shifts(stage, step))  20.9 us
    ppermute x9, starting transfers between devices, image_pieces(): lax.ppermute(piece, 'col', [(i, (i + part) % parts) for i in range(parts)])  18.2 us
    ppermute x9, waiting for transfers between devices, image_pieces(): lax.ppermute(piece, 'col', [(i, (i + part) % parts) for i in range(parts)])  10.7 us
    ppermute x3, waiting for transfers between devices, all_gathered(): their_rest = lax.ppermute(rest, 'row', core_swap())  5.13 us
    pallas_call x12, Pallas kernels, local_products(): pl.pallas_call(functools.partial(products_kernel, part * owned), out_shap...  3.83 us
    pallas_call x1, Pallas kernels, sort_plan(): pl.pallas_call(functools.partial(plan_kernel, parts, owned), out_shape=[p...  2.09 us
  transfers between devices with their start and end apart: 33, of which 22 were waited for; matrix products, arithmetic and copies ran while one was open for 0% of the time, Pallas kernels for 6%

profile of v6, /device:TPU:0, one launch (start us, length us, event | category | flops | bytes accessed | tf_op | source)
XLA Modules:
  0.0 94.8 jit_solution(16202608822754852368)
XLA Ops:
  0.8 3.3 %collective-permute-start.2 = (bf16[4,32,128]{2,1,0:T(8,128)(2,1)S(1)}, bf16[4,32,128]{2,1,0:T(8,128)(2,1)S(1)}, u32[]{:S(2)}, u32[]{:S(2)}) collective-permute-start(bf16[4,32,128]{2,1,0:T(8,128)(2,1)S(1)} %shard_map.73._after.refs_0_), channel_id=1, source_target_pairs={{0,16},{4,68},{8,24},{12,76},{16,0},{20,84},{24,8},{28,92},{32,48}... | collective-permute-start | bytes 98312 | tf_op jit(solution)/shard_map/ppermute | solution.py:81
  8.1 2.1 %shard_map.74 = (s32[1,640]{1,0:T(1,128)S(4)}, s32[1,1344]{1,0:T(1,128)S(4)}, f32[1]{0:T(128)S(4)}, f32[1]{0:T(128)S(4)}) custom-call(s32[1]{0:T(128)S(6)} %copy.8.live_ref, s32[640]{0:T(1024)} %rows_hbm.1, s32[640]{0:T(1024)} %cols_hbm.1, f32[]{:T(128)S(6)} %copy.9.center, f32[]{:T(128)S(6)} %copy.10.half_width, ...), custom_call_target="tpu_custom_call" | custom-call | flops 1000 | bytes 1000 | tf_op jit(solution)/shard_map/pallas_call | solution.py:173
  10.4 3.1 %collective-permute-start.5 = (bf16[16,32,128]{2,1,0:T(8,128)(2,1)S(1)}, bf16[16,32,128]{2,1,0:T(8,128)(2,1)S(1)}, u32[]{:S(2)}, u32[]{:S(2)}) collective-permute-start(bf16[16,32,128]{2,1,0:T(8,128)(2,1)S(1)} %shard_map.75._after.refs_0_), channel_id=1, source_target_pairs={{0,64},{4,20},{8,72},{12,28},{16,80},{20,4},{24,88},{28,12},{32,96... | collective-permute-start | bytes 393224 | tf_op jit(solution)/shard_map/ppermute | solution.py:81
  15.6 1.7 %shard_map.76.refs_3_.store = bf16[832,128,128]{2,1,0:T(8,128)(2,1)S(1)} custom-call(s32[1,640]{1,0:T(1,128)S(4)} %get-tuple-element.16.place, s32[1,1344]{1,0:T(1,128)S(4)} %get-tuple-element.15.refs_4_.sizes.table, bf16[16,32,128]{2,1,0:T(8,128)(2,1)S(1)} %shard_map.75._after.refs_0_, bf16[640,128,128]{2,1,0:T(8,128)(2,1)} %blocks_hbm.1), custom_call_target="tpu_custom_call" | custom-call | flops 1000 | bytes 20971520 | tf_op jit(solution)/shard_map/pallas_call | solution.py:215
  18.5 2.4 %collective-permute-done.3.refs_0_ = bf16[16,32,128]{2,1,0:T(8,128)(2,1)S(1)} collective-permute-done((bf16[16,32,128]{2,1,0:T(8,128)(2,1)S(1)}, bf16[16,32,128]{2,1,0:T(8,128)(2,1)S(1)}, u32[]{:S(2)}, u32[]{:S(2)}) %collective-permute-start.3) | collective-permute-done | bytes 131104 | tf_op jit(solution)/shard_map/ppermute | solution.py:81
  21.0 1.7 %collective-permute-done.7.refs_3_ = bf16[48,32,128]{2,1,0:T(8,128)(2,1)S(1)} collective-permute-done((bf16[48,32,128]{2,1,0:T(8,128)(2,1)S(1)}, bf16[48,32,128]{2,1,0:T(8,128)(2,1)S(1)}, u32[]{:S(2)}, u32[]{:S(2)}) %collective-permute-start.7) | collective-permute-done | bytes 393248 | tf_op jit(solution)/shard_map/ppermute | solution.py:91
  23.5 4.7 %collective-permute-start.10 = (f32[4,32,128]{2,1,0:T(8,128)S(1)}, f32[4,32,128]{2,1,0:T(8,128)S(1)}, u32[]{:S(2)}, u32[]{:S(2)}) collective-permute-start(f32[4,32,128]{2,1,0:T(8,128)S(1)} %shard_map.81.refs_0_), channel_id=1, source_target_pairs={{0,3},{1,0},{2,1},{3,2},{4,7},{5,4},{6,5},{7,6},{8,11},{9,8},{10,9... | collective-permute-start | bytes 196616 | tf_op jit(solution)/shard_map/ppermute | solution.py:299
  28.2 2.5 %collective-permute-start.8 = (f32[4,32,128]{2,1,0:T(8,128)S(1)}, f32[4,32,128]{2,1,0:T(8,128)S(1)}, u32[]{:S(2)}, u32[]{:S(2)}) collective-permute-start(f32[4,32,128]{2,1,0:T(8,128)S(1)} %shard_map.79.refs_0_), channel_id=1, source_target_pairs={{0,2},{1,3},{2,0},{3,1},{4,6},{5,7},{6,4},{7,5},{8,10},{9,11},{10,... | collective-permute-start | bytes 196616 | tf_op jit(solution)/shard_map/ppermute | solution.py:299
  31.3 4.0 %collective-permute-done.9.refs_1_ = f32[4,32,128]{2,1,0:T(8,128)S(1)} collective-permute-done((f32[4,32,128]{2,1,0:T(8,128)S(1)}, f32[4,32,128]{2,1,0:T(8,128)S(1)}, u32[]{:S(2)}, u32[]{:S(2)}) %collective-permute-start.9) | collective-permute-done | bytes 65568 | tf_op jit(solution)/shard_map/ppermute | solution.py:299
  36.3 2.3 %collective-permute-start.12 = (bf16[4,32,128]{2,1,0:T(8,128)(2,1)S(1)}, bf16[4,32,128]{2,1,0:T(8,128)(2,1)S(1)}, u32[]{:S(2)}, u32[]{:S(2)}) collective-permute-start(bf16[4,32,128]{2,1,0:T(8,128)(2,1)S(1)} %get-tuple-element.18.refs_0_), channel_id=1, source_target_pairs={{0,24},{4,100},{8,0},{12,108},{16,8},{20,116},{24,16},{28,124},{32... | collective-permute-start | bytes 98312 | tf_op jit(solution)/shard_map/ppermute | solution.py:81
  39.2 1.6 %collective-permute-done.13.refs_3_ = bf16[4,32,128]{2,1,0:T(8,128)(2,1)S(1)} collective-permute-done((bf16[4,32,128]{2,1,0:T(8,128)(2,1)S(1)}, bf16[4,32,128]{2,1,0:T(8,128)(2,1)S(1)}, u32[]{:S(2)}, u32[]{:S(2)}) %collective-permute-start.13) | collective-permute-done | bytes 32800 | tf_op jit(solution)/shard_map/ppermute | solution.py:81
  41.4 2.3 %collective-permute-done.11.refs_1_ = bf16[4,32,128]{2,1,0:T(8,128)(2,1)S(1)} collective-permute-done((bf16[4,32,128]{2,1,0:T(8,128)(2,1)S(1)}, bf16[4,32,128]{2,1,0:T(8,128)(2,1)S(1)}, u32[]{:S(2)}, u32[]{:S(2)}) %collective-permute-start.11) | collective-permute-done | bytes 32800 | tf_op jit(solution)/shard_map/ppermute | solution.py:81
  44.0 2.5 %collective-permute-start.16 = (bf16[16,32,128]{2,1,0:T(8,128)(2,1)S(1)}, bf16[16,32,128]{2,1,0:T(8,128)(2,1)S(1)}, u32[]{:S(2)}, u32[]{:S(2)}) collective-permute-start(bf16[16,32,128]{2,1,0:T(8,128)(2,1)S(1)} %shard_map.84.refs_0_), channel_id=1, source_target_pairs={{0,64},{4,20},{8,72},{12,28},{16,80},{20,4},{24,88},{28,12},{32,96... | collective-permute-start | bytes 393224 | tf_op jit(solution)/shard_map/ppermute | solution.py:81
  48.5 2.0 %collective-permute-done.16.refs_2_ = bf16[16,32,128]{2,1,0:T(8,128)(2,1)S(1)} collective-permute-done((bf16[16,32,128]{2,1,0:T(8,128)(2,1)S(1)}, bf16[16,32,128]{2,1,0:T(8,128)(2,1)S(1)}, u32[]{:S(2)}, u32[]{:S(2)}) %collective-permute-start.16) | collective-permute-done | bytes 131104 | tf_op jit(solution)/shard_map/ppermute | solution.py:81
  50.5 1.9 %collective-permute-done.15.refs_1_ = bf16[16,32,128]{2,1,0:T(8,128)(2,1)S(1)} collective-permute-done((bf16[16,32,128]{2,1,0:T(8,128)(2,1)S(1)}, bf16[16,32,128]{2,1,0:T(8,128)(2,1)S(1)}, u32[]{:S(2)}, u32[]{:S(2)}) %collective-permute-start.15) | collective-permute-done | bytes 131104 | tf_op jit(solution)/shard_map/ppermute | solution.py:81
  53.5 1.7 %collective-permute-done.18.refs_3_ = bf16[48,32,128]{2,1,0:T(8,128)(2,1)S(1)} collective-permute-done((bf16[48,32,128]{2,1,0:T(8,128)(2,1)S(1)}, bf16[48,32,128]{2,1,0:T(8,128)(2,1)S(1)}, u32[]{:S(2)}, u32[]{:S(2)}) %collective-permute-start.18) | collective-permute-done | bytes 393248 | tf_op jit(solution)/shard_map/ppermute | solution.py:91
  55.9 2.3 %collective-permute-start.21 = (f32[4,32,128]{2,1,0:T(8,128)S(1)}, f32[4,32,128]{2,1,0:T(8,128)S(1)}, u32[]{:S(2)}, u32[]{:S(2)}) collective-permute-start(f32[4,32,128]{2,1,0:T(8,128)S(1)} %shard_map.89.refs_0_), channel_id=1, source_target_pairs={{0,3},{1,0},{2,1},{3,2},{4,7},{5,4},{6,5},{7,6},{8,11},{9,8},{10,9... | collective-permute-start | bytes 196616 | tf_op jit(solution)/shard_map/ppermute | solution.py:299
  59.2 2.5 %collective-permute-start.19 = (f32[4,32,128]{2,1,0:T(8,128)S(1)}, f32[4,32,128]{2,1,0:T(8,128)S(1)}, u32[]{:S(2)}, u32[]{:S(2)}) collective-permute-start(f32[4,32,128]{2,1,0:T(8,128)S(1)} %shard_map.87.refs_0_), channel_id=1, source_target_pairs={{0,2},{1,3},{2,0},{3,1},{4,6},{5,7},{6,4},{7,5},{8,10},{9,11},{10,... | collective-permute-start | bytes 196616 | tf_op jit(solution)/shard_map/ppermute | solution.py:299
  62.3 1.6 %collective-permute-done.20.refs_1_ = f32[4,32,128]{2,1,0:T(8,128)S(1)} collective-permute-done((f32[4,32,128]{2,1,0:T(8,128)S(1)}, f32[4,32,128]{2,1,0:T(8,128)S(1)}, u32[]{:S(2)}, u32[]{:S(2)}) %collective-permute-start.20) | collective-permute-done | bytes 65568 | tf_op jit(solution)/shard_map/ppermute | solution.py:299
  63.9 1.7 %collective-permute-done.19.refs_0_ = f32[4,32,128]{2,1,0:T(8,128)S(1)} collective-permute-done((f32[4,32,128]{2,1,0:T(8,128)S(1)}, f32[4,32,128]{2,1,0:T(8,128)S(1)}, u32[]{:S(2)}, u32[]{:S(2)}) %collective-permute-start.19) | collective-permute-done | bytes 65568 | tf_op jit(solution)/shard_map/ppermute | solution.py:299
  65.7 1.5 %collective-permute-start.24 = (bf16[4,32,128]{2,1,0:T(8,128)(2,1)S(1)}, bf16[4,32,128]{2,1,0:T(8,128)(2,1)S(1)}, u32[]{:S(2)}, u32[]{:S(2)}) collective-permute-start(bf16[4,32,128]{2,1,0:T(8,128)(2,1)S(1)} %get-tuple-element.20.refs_0_), channel_id=1, source_target_pairs={{0,16},{4,68},{8,24},{12,76},{16,0},{20,84},{24,8},{28,92},{32,48}... | collective-permute-start | bytes 98312 | tf_op jit(solution)/shard_map/ppermute | solution.py:81
  67.8 1.4 %collective-permute-start.22 = (bf16[4,32,128]{2,1,0:T(8,128)(2,1)S(1)}, bf16[4,32,128]{2,1,0:T(8,128)(2,1)S(1)}, u32[]{:S(2)}, u32[]{:S(2)}) collective-permute-start(bf16[4,32,128]{2,1,0:T(8,128)(2,1)S(1)} %get-tuple-element.20.refs_0_), channel_id=1, source_target_pairs={{0,8},{4,36},{8,16},{12,44},{16,24},{20,52},{24,0},{28,60},{32,40}... | collective-permute-start | bytes 98312 | tf_op jit(solution)/shard_map/ppermute | solution.py:81
  69.2 2.0 %collective-permute-done.24.refs_3_ = bf16[4,32,128]{2,1,0:T(8,128)(2,1)S(1)} collective-permute-done((bf16[4,32,128]{2,1,0:T(8,128)(2,1)S(1)}, bf16[4,32,128]{2,1,0:T(8,128)(2,1)S(1)}, u32[]{:S(2)}, u32[]{:S(2)}) %collective-permute-start.24) | collective-permute-done | bytes 32800 | tf_op jit(solution)/shard_map/ppermute | solution.py:81
  71.2 1.8 %collective-permute-done.22.refs_1_ = bf16[4,32,128]{2,1,0:T(8,128)(2,1)S(1)} collective-permute-done((bf16[4,32,128]{2,1,0:T(8,128)(2,1)S(1)}, bf16[4,32,128]{2,1,0:T(8,128)(2,1)S(1)}, u32[]{:S(2)}, u32[]{:S(2)}) %collective-permute-start.22) | collective-permute-done | bytes 32800 | tf_op jit(solution)/shard_map/ppermute | solution.py:81
  73.2 2.9 %collective-permute-start.27 = (bf16[16,32,128]{2,1,0:T(8,128)(2,1)S(1)}, bf16[16,32,128]{2,1,0:T(8,128)(2,1)S(1)}, u32[]{:S(2)}, u32[]{:S(2)}) collective-permute-start(bf16[16,32,128]{2,1,0:T(8,128)(2,1)S(1)} %shard_map.92.refs_0_), channel_id=1, source_target_pairs={{0,64},{4,20},{8,72},{12,28},{16,80},{20,4},{24,88},{28,12},{32,96... | collective-permute-start | bytes 393224 | tf_op jit(solution)/shard_map/ppermute | solution.py:81
  76.1 2.0 %collective-permute-start.25 = (bf16[16,32,128]{2,1,0:T(8,128)(2,1)S(1)}, bf16[16,32,128]{2,1,0:T(8,128)(2,1)S(1)}, u32[]{:S(2)}, u32[]{:S(2)}) collective-permute-start(bf16[16,32,128]{2,1,0:T(8,128)(2,1)S(1)} %shard_map.92.refs_0_), channel_id=1, source_target_pairs={{0,32},{4,12},{8,40},{12,20},{16,48},{20,28},{24,56},{28,4},{32,64... | collective-permute-start | bytes 393224 | tf_op jit(solution)/shard_map/ppermute | solution.py:81
  78.1 1.5 %collective-permute-done.27.refs_2_ = bf16[16,32,128]{2,1,0:T(8,128)(2,1)S(1)} collective-permute-done((bf16[16,32,128]{2,1,0:T(8,128)(2,1)S(1)}, bf16[16,32,128]{2,1,0:T(8,128)(2,1)S(1)}, u32[]{:S(2)}, u32[]{:S(2)}) %collective-permute-start.27) | collective-permute-done | bytes 131104 | tf_op jit(solution)/shard_map/ppermute | solution.py:81
  79.6 1.4 %collective-permute-done.26.refs_1_ = bf16[16,32,128]{2,1,0:T(8,128)(2,1)S(1)} collective-permute-done((bf16[16,32,128]{2,1,0:T(8,128)(2,1)S(1)}, bf16[16,32,128]{2,1,0:T(8,128)(2,1)S(1)}, u32[]{:S(2)}, u32[]{:S(2)}) %collective-permute-start.26) | collective-permute-done | bytes 131104 | tf_op jit(solution)/shard_map/ppermute | solution.py:81
  82.4 1.7 %collective-permute-done.29.refs_3_ = bf16[48,32,128]{2,1,0:T(8,128)(2,1)S(1)} collective-permute-done((bf16[48,32,128]{2,1,0:T(8,128)(2,1)S(1)}, bf16[48,32,128]{2,1,0:T(8,128)(2,1)S(1)}, u32[]{:S(2)}, u32[]{:S(2)}) %collective-permute-start.29) | collective-permute-done | bytes 393248 | tf_op jit(solution)/shard_map/ppermute | solution.py:91
  84.9 2.6 %collective-permute-start.32 = (f32[4,32,128]{2,1,0:T(8,128)S(1)}, f32[4,32,128]{2,1,0:T(8,128)S(1)}, u32[]{:S(2)}, u32[]{:S(2)}) collective-permute-start(f32[4,32,128]{2,1,0:T(8,128)S(1)} %shard_map.97.refs_0_), channel_id=1, source_target_pairs={{0,3},{1,0},{2,1},{3,2},{4,7},{5,4},{6,5},{7,6},{8,11},{9,8},{10,9... | collective-permute-start | bytes 196616 | tf_op jit(solution)/shard_map/ppermute | solution.py:299
  87.6 2.6 %collective-permute-start.30 = (f32[4,32,128]{2,1,0:T(8,128)S(1)}, f32[4,32,128]{2,1,0:T(8,128)S(1)}, u32[]{:S(2)}, u32[]{:S(2)}) collective-permute-start(f32[4,32,128]{2,1,0:T(8,128)S(1)} %shard_map.95.refs_0_), channel_id=1, source_target_pairs={{0,2},{1,3},{2,0},{3,1},{4,6},{5,7},{6,4},{7,5},{8,10},{9,11},{10,... | collective-permute-start | bytes 196616 | tf_op jit(solution)/shard_map/ppermute | solution.py:299
  90.8 2.7 %collective-permute-done.31.refs_1_ = f32[4,32,128]{2,1,0:T(8,128)S(1)} collective-permute-done((f32[4,32,128]{2,1,0:T(8,128)S(1)}, f32[4,32,128]{2,1,0:T(8,128)S(1)}, u32[]{:S(2)}, u32[]{:S(2)}) %collective-permute-start.31) | collective-permute-done | bytes 65568 | tf_op jit(solution)/shard_map/ppermute | solution.py:299
  (65 shorter events, 20.7 us)
Async XLA Ops:
  0.8 9.4 %collective-permute-start.2 = (bf16[4,32,128]{2,1,0:T(8,128)(2,1)S(1)}, bf16[4,32,128]{2,1,0:T(8,128)(2,1)S(1)}, u32[]{:S(2)}, u32[]{:S(2)}) collective-permute-start(bf16[4,32,128]{2,1,0:T(8,128)(2,1)S(1)} %shard_map.73._after.refs_0_), channel_id=1, source_target_pairs={{0,16},{4,68},{8,24},{12,76},{16,0},{20,84},{24,8},{28,92},{32,48}... | collective-permute-start | bytes 98312 | tf_op jit(solution)/shard_map/ppermute | solution.py:81
  4.2 6.1 %collective-permute-start.1 = (bf16[4,32,128]{2,1,0:T(8,128)(2,1)S(1)}, bf16[4,32,128]{2,1,0:T(8,128)(2,1)S(1)}, u32[]{:S(2)}, u32[]{:S(2)}) collective-permute-start(bf16[4,32,128]{2,1,0:T(8,128)(2,1)S(1)} %shard_map.73._after.refs_0_), channel_id=1, source_target_pairs={{0,24},{4,100},{8,0},{12,108},{16,8},{20,116},{24,16},{28,124},{32... | collective-permute-start | bytes 98312 | tf_op jit(solution)/shard_map/ppermute | solution.py:81
  5.2 5.1 %collective-permute-start = (bf16[4,32,128]{2,1,0:T(8,128)(2,1)S(1)}, bf16[4,32,128]{2,1,0:T(8,128)(2,1)S(1)}, u32[]{:S(2)}, u32[]{:S(2)}) collective-permute-start(bf16[4,32,128]{2,1,0:T(8,128)(2,1)S(1)} %shard_map.73._after.refs_0_), channel_id=1, source_target_pairs={{0,8},{4,36},{8,16},{12,44},{16,24},{20,52},{24,0},{28,60},{32,40}... | collective-permute-start | bytes 98312 | tf_op jit(solution)/shard_map/ppermute | solution.py:81
  10.3 7.0 %collective-permute-start.6 = (bf16[16,32,128]{2,1,0:T(8,128)(2,1)S(1)}, bf16[16,32,128]{2,1,0:T(8,128)(2,1)S(1)}, u32[]{:S(2)}, u32[]{:S(2)}) collective-permute-start(bf16[16,32,128]{2,1,0:T(8,128)(2,1)S(1)} %shard_map.75._after.refs_0_), channel_id=1, source_target_pairs={{0,4},{4,0},{8,12},{12,8},{16,20},{20,16},{24,28},{28,24},{32,36},... | collective-permute-start | bytes 393224 | tf_op jit(solution)/shard_map/ppermute | solution.py:89
  10.4 6.9 %collective-permute-start.5 = (bf16[16,32,128]{2,1,0:T(8,128)(2,1)S(1)}, bf16[16,32,128]{2,1,0:T(8,128)(2,1)S(1)}, u32[]{:S(2)}, u32[]{:S(2)}) collective-permute-start(bf16[16,32,128]{2,1,0:T(8,128)(2,1)S(1)} %shard_map.75._after.refs_0_), channel_id=1, source_target_pairs={{0,64},{4,20},{8,72},{12,28},{16,80},{20,4},{24,88},{28,12},{32,96... | collective-permute-start | bytes 393224 | tf_op jit(solution)/shard_map/ppermute | solution.py:81
  13.5 5.0 %collective-permute-start.4 = (bf16[16,32,128]{2,1,0:T(8,128)(2,1)S(1)}, bf16[16,32,128]{2,1,0:T(8,128)(2,1)S(1)}, u32[]{:S(2)}, u32[]{:S(2)}) collective-permute-start(bf16[16,32,128]{2,1,0:T(8,128)(2,1)S(1)} %shard_map.75._after.refs_0_), channel_id=1, source_target_pairs={{0,96},{4,28},{8,104},{12,4},{16,112},{20,12},{24,120},{28,20},{32... | collective-permute-start | bytes 393224 | tf_op jit(solution)/shard_map/ppermute | solution.py:81
  14.7 6.2 %collective-permute-start.3 = (bf16[16,32,128]{2,1,0:T(8,128)(2,1)S(1)}, bf16[16,32,128]{2,1,0:T(8,128)(2,1)S(1)}, u32[]{:S(2)}, u32[]{:S(2)}) collective-permute-start(bf16[16,32,128]{2,1,0:T(8,128)(2,1)S(1)} %shard_map.75._after.refs_0_), channel_id=1, source_target_pairs={{0,32},{4,12},{8,40},{12,20},{16,48},{20,28},{24,56},{28,4},{32,64... | collective-permute-start | bytes 393224 | tf_op jit(solution)/shard_map/ppermute | solution.py:81
  20.9 1.8 %collective-permute-start.7 = (bf16[48,32,128]{2,1,0:T(8,128)(2,1)S(1)}, bf16[48,32,128]{2,1,0:T(8,128)(2,1)S(1)}, u32[]{:S(2)}, u32[]{:S(2)}) collective-permute-start(bf16[48,32,128]{2,1,0:T(8,128)(2,1)S(1)} %shard_map.77.refs_1_), channel_id=1, source_target_pairs={{0,4},{4,0},{8,12},{12,8},{16,20},{20,16},{24,28},{28,24},{32,36},... | collective-permute-start | bytes 1179656 | tf_op jit(solution)/shard_map/ppermute | solution.py:91
  23.5 7.8 %collective-permute-start.10 = (f32[4,32,128]{2,1,0:T(8,128)S(1)}, f32[4,32,128]{2,1,0:T(8,128)S(1)}, u32[]{:S(2)}, u32[]{:S(2)}) collective-permute-start(f32[4,32,128]{2,1,0:T(8,128)S(1)} %shard_map.81.refs_0_), channel_id=1, source_target_pairs={{0,3},{1,0},{2,1},{3,2},{4,7},{5,4},{6,5},{7,6},{8,11},{9,8},{10,9... | collective-permute-start | bytes 196616 | tf_op jit(solution)/shard_map/ppermute | solution.py:299
  28.2 7.1 %collective-permute-start.9 = (f32[4,32,128]{2,1,0:T(8,128)S(1)}, f32[4,32,128]{2,1,0:T(8,128)S(1)}, u32[]{:S(2)}, u32[]{:S(2)}) collective-permute-start(f32[4,32,128]{2,1,0:T(8,128)S(1)} %shard_map.80.refs_0_), channel_id=1, source_target_pairs={{0,1},{1,2},{2,3},{3,0},{4,5},{5,6},{6,7},{7,4},{8,9},{9,10},{10,1... | collective-permute-start | bytes 196616 | tf_op jit(solution)/shard_map/ppermute | solution.py:299
  28.2 7.1 %collective-permute-start.8 = (f32[4,32,128]{2,1,0:T(8,128)S(1)}, f32[4,32,128]{2,1,0:T(8,128)S(1)}, u32[]{:S(2)}, u32[]{:S(2)}) collective-permute-start(f32[4,32,128]{2,1,0:T(8,128)S(1)} %shard_map.79.refs_0_), channel_id=1, source_target_pairs={{0,2},{1,3},{2,0},{3,1},{4,6},{5,7},{6,4},{7,5},{8,10},{9,11},{10,... | collective-permute-start | bytes 196616 | tf_op jit(solution)/shard_map/ppermute | solution.py:299
  35.3 5.5 %collective-permute-start.13 = (bf16[4,32,128]{2,1,0:T(8,128)(2,1)S(1)}, bf16[4,32,128]{2,1,0:T(8,128)(2,1)S(1)}, u32[]{:S(2)}, u32[]{:S(2)}) collective-permute-start(bf16[4,32,128]{2,1,0:T(8,128)(2,1)S(1)} %get-tuple-element.18.refs_0_), channel_id=1, source_target_pairs={{0,16},{4,68},{8,24},{12,76},{16,0},{20,84},{24,8},{28,92},{32,48}... | collective-permute-start | bytes 98312 | tf_op jit(solution)/shard_map/ppermute | solution.py:81
  36.3 5.1 %collective-permute-start.12 = (bf16[4,32,128]{2,1,0:T(8,128)(2,1)S(1)}, bf16[4,32,128]{2,1,0:T(8,128)(2,1)S(1)}, u32[]{:S(2)}, u32[]{:S(2)}) collective-permute-start(bf16[4,32,128]{2,1,0:T(8,128)(2,1)S(1)} %get-tuple-element.18.refs_0_), channel_id=1, source_target_pairs={{0,24},{4,100},{8,0},{12,108},{16,8},{20,116},{24,16},{28,124},{32... | collective-permute-start | bytes 98312 | tf_op jit(solution)/shard_map/ppermute | solution.py:81
  38.6 5.1 %collective-permute-start.11 = (bf16[4,32,128]{2,1,0:T(8,128)(2,1)S(1)}, bf16[4,32,128]{2,1,0:T(8,128)(2,1)S(1)}, u32[]{:S(2)}, u32[]{:S(2)}) collective-permute-start(bf16[4,32,128]{2,1,0:T(8,128)(2,1)S(1)} %get-tuple-element.18.refs_0_), channel_id=1, source_target_pairs={{0,8},{4,36},{8,16},{12,44},{16,24},{20,52},{24,0},{28,60},{32,40}... | collective-permute-start | bytes 98312 | tf_op jit(solution)/shard_map/ppermute | solution.py:81
  43.8 4.7 %collective-permute-start.17 = (bf16[16,32,128]{2,1,0:T(8,128)(2,1)S(1)}, bf16[16,32,128]{2,1,0:T(8,128)(2,1)S(1)}, u32[]{:S(2)}, u32[]{:S(2)}) collective-permute-start(bf16[16,32,128]{2,1,0:T(8,128)(2,1)S(1)} %shard_map.84.refs_0_), channel_id=1, source_target_pairs={{0,4},{4,0},{8,12},{12,8},{16,20},{20,16},{24,28},{28,24},{32,36},... | collective-permute-start | bytes 393224 | tf_op jit(solution)/shard_map/ppermute | solution.py:89
  44.0 6.5 %collective-permute-start.16 = (bf16[16,32,128]{2,1,0:T(8,128)(2,1)S(1)}, bf16[16,32,128]{2,1,0:T(8,128)(2,1)S(1)}, u32[]{:S(2)}, u32[]{:S(2)}) collective-permute-start(bf16[16,32,128]{2,1,0:T(8,128)(2,1)S(1)} %shard_map.84.refs_0_), channel_id=1, source_target_pairs={{0,64},{4,20},{8,72},{12,28},{16,80},{20,4},{24,88},{28,12},{32,96... | collective-permute-start | bytes 393224 | tf_op jit(solution)/shard_map/ppermute | solution.py:81
  46.4 5.9 %collective-permute-start.15 = (bf16[16,32,128]{2,1,0:T(8,128)(2,1)S(1)}, bf16[16,32,128]{2,1,0:T(8,128)(2,1)S(1)}, u32[]{:S(2)}, u32[]{:S(2)}) collective-permute-start(bf16[16,32,128]{2,1,0:T(8,128)(2,1)S(1)} %shard_map.84.refs_0_), channel_id=1, source_target_pairs={{0,96},{4,28},{8,104},{12,4},{16,112},{20,12},{24,120},{28,20},{32... | collective-permute-start | bytes 393224 | tf_op jit(solution)/shard_map/ppermute | solution.py:81
  47.2 6.2 %collective-permute-start.14 = (bf16[16,32,128]{2,1,0:T(8,128)(2,1)S(1)}, bf16[16,32,128]{2,1,0:T(8,128)(2,1)S(1)}, u32[]{:S(2)}, u32[]{:S(2)}) collective-permute-start(bf16[16,32,128]{2,1,0:T(8,128)(2,1)S(1)} %shard_map.84.refs_0_), channel_id=1, source_target_pairs={{0,32},{4,12},{8,40},{12,20},{16,48},{20,28},{24,56},{28,4},{32,64... | collective-permute-start | bytes 393224 | tf_op jit(solution)/shard_map/ppermute | solution.py:81
  53.4 1.8 %collective-permute-start.18 = (bf16[48,32,128]{2,1,0:T(8,128)(2,1)S(1)}, bf16[48,32,128]{2,1,0:T(8,128)(2,1)S(1)}, u32[]{:S(2)}, u32[]{:S(2)}) collective-permute-start(bf16[48,32,128]{2,1,0:T(8,128)(2,1)S(1)} %shard_map.85.refs_1_), channel_id=1, source_target_pairs={{0,4},{4,0},{8,12},{12,8},{16,20},{20,16},{24,28},{28,24},{32,36},... | collective-permute-start | bytes 1179656 | tf_op jit(solution)/shard_map/ppermute | solution.py:91
  55.9 6.3 %collective-permute-start.21 = (f32[4,32,128]{2,1,0:T(8,128)S(1)}, f32[4,32,128]{2,1,0:T(8,128)S(1)}, u32[]{:S(2)}, u32[]{:S(2)}) collective-permute-start(f32[4,32,128]{2,1,0:T(8,128)S(1)} %shard_map.89.refs_0_), channel_id=1, source_target_pairs={{0,3},{1,0},{2,1},{3,2},{4,7},{5,4},{6,5},{7,6},{8,11},{9,8},{10,9... | collective-permute-start | bytes 196616 | tf_op jit(solution)/shard_map/ppermute | solution.py:299
  58.2 5.7 %collective-permute-start.20 = (f32[4,32,128]{2,1,0:T(8,128)S(1)}, f32[4,32,128]{2,1,0:T(8,128)S(1)}, u32[]{:S(2)}, u32[]{:S(2)}) collective-permute-start(f32[4,32,128]{2,1,0:T(8,128)S(1)} %shard_map.88.refs_0_), channel_id=1, source_target_pairs={{0,1},{1,2},{2,3},{3,0},{4,5},{5,6},{6,7},{7,4},{8,9},{9,10},{10,1... | collective-permute-start | bytes 196616 | tf_op jit(solution)/shard_map/ppermute | solution.py:299
  59.2 6.4 %collective-permute-start.19 = (f32[4,32,128]{2,1,0:T(8,128)S(1)}, f32[4,32,128]{2,1,0:T(8,128)S(1)}, u32[]{:S(2)}, u32[]{:S(2)}) collective-permute-start(f32[4,32,128]{2,1,0:T(8,128)S(1)} %shard_map.87.refs_0_), channel_id=1, source_target_pairs={{0,2},{1,3},{2,0},{3,1},{4,6},{5,7},{6,4},{7,5},{8,10},{9,11},{10,... | collective-permute-start | bytes 196616 | tf_op jit(solution)/shard_map/ppermute | solution.py:299
  65.7 5.5 %collective-permute-start.24 = (bf16[4,32,128]{2,1,0:T(8,128)(2,1)S(1)}, bf16[4,32,128]{2,1,0:T(8,128)(2,1)S(1)}, u32[]{:S(2)}, u32[]{:S(2)}) collective-permute-start(bf16[4,32,128]{2,1,0:T(8,128)(2,1)S(1)} %get-tuple-element.20.refs_0_), channel_id=1, source_target_pairs={{0,16},{4,68},{8,24},{12,76},{16,0},{20,84},{24,8},{28,92},{32,48}... | collective-permute-start | bytes 98312 | tf_op jit(solution)/shard_map/ppermute | solution.py:81
  67.2 4.0 %collective-permute-start.23 = (bf16[4,32,128]{2,1,0:T(8,128)(2,1)S(1)}, bf16[4,32,128]{2,1,0:T(8,128)(2,1)S(1)}, u32[]{:S(2)}, u32[]{:S(2)}) collective-permute-start(bf16[4,32,128]{2,1,0:T(8,128)(2,1)S(1)} %get-tuple-element.20.refs_0_), channel_id=1, source_target_pairs={{0,24},{4,100},{8,0},{12,108},{16,8},{20,116},{24,16},{28,124},{32... | collective-permute-start | bytes 98312 | tf_op jit(solution)/shard_map/ppermute | solution.py:81
  67.8 5.1 %collective-permute-start.22 = (bf16[4,32,128]{2,1,0:T(8,128)(2,1)S(1)}, bf16[4,32,128]{2,1,0:T(8,128)(2,1)S(1)}, u32[]{:S(2)}, u32[]{:S(2)}) collective-permute-start(bf16[4,32,128]{2,1,0:T(8,128)(2,1)S(1)} %get-tuple-element.20.refs_0_), channel_id=1, source_target_pairs={{0,8},{4,36},{8,16},{12,44},{16,24},{20,52},{24,0},{28,60},{32,40}... | collective-permute-start | bytes 98312 | tf_op jit(solution)/shard_map/ppermute | solution.py:81
  72.9 5.2 %collective-permute-start.28 = (bf16[16,32,128]{2,1,0:T(8,128)(2,1)S(1)}, bf16[16,32,128]{2,1,0:T(8,128)(2,1)S(1)}, u32[]{:S(2)}, u32[]{:S(2)}) collective-permute-start(bf16[16,32,128]{2,1,0:T(8,128)(2,1)S(1)} %shard_map.92.refs_0_), channel_id=1, source_target_pairs={{0,4},{4,0},{8,12},{12,8},{16,20},{20,16},{24,28},{28,24},{32,36},... | collective-permute-start | bytes 393224 | tf_op jit(solution)/shard_map/ppermute | solution.py:89
  73.2 6.5 %collective-permute-start.27 = (bf16[16,32,128]{2,1,0:T(8,128)(2,1)S(1)}, bf16[16,32,128]{2,1,0:T(8,128)(2,1)S(1)}, u32[]{:S(2)}, u32[]{:S(2)}) collective-permute-start(bf16[16,32,128]{2,1,0:T(8,128)(2,1)S(1)} %shard_map.92.refs_0_), channel_id=1, source_target_pairs={{0,64},{4,20},{8,72},{12,28},{16,80},{20,4},{24,88},{28,12},{32,96... | collective-permute-start | bytes 393224 | tf_op jit(solution)/shard_map/ppermute | solution.py:81
  76.1 5.0 %collective-permute-start.26 = (bf16[16,32,128]{2,1,0:T(8,128)(2,1)S(1)}, bf16[16,32,128]{2,1,0:T(8,128)(2,1)S(1)}, u32[]{:S(2)}, u32[]{:S(2)}) collective-permute-start(bf16[16,32,128]{2,1,0:T(8,128)(2,1)S(1)} %shard_map.92.refs_0_), channel_id=1, source_target_pairs={{0,96},{4,28},{8,104},{12,4},{16,112},{20,12},{24,120},{28,20},{32... | collective-permute-start | bytes 393224 | tf_op jit(solution)/shard_map/ppermute | solution.py:81
  76.1 6.2 %collective-permute-start.25 = (bf16[16,32,128]{2,1,0:T(8,128)(2,1)S(1)}, bf16[16,32,128]{2,1,0:T(8,128)(2,1)S(1)}, u32[]{:S(2)}, u32[]{:S(2)}) collective-permute-start(bf16[16,32,128]{2,1,0:T(8,128)(2,1)S(1)} %shard_map.92.refs_0_), channel_id=1, source_target_pairs={{0,32},{4,12},{8,40},{12,20},{16,48},{20,28},{24,56},{28,4},{32,64... | collective-permute-start | bytes 393224 | tf_op jit(solution)/shard_map/ppermute | solution.py:81
  84.9 5.9 %collective-permute-start.32 = (f32[4,32,128]{2,1,0:T(8,128)S(1)}, f32[4,32,128]{2,1,0:T(8,128)S(1)}, u32[]{:S(2)}, u32[]{:S(2)}) collective-permute-start(f32[4,32,128]{2,1,0:T(8,128)S(1)} %shard_map.97.refs_0_), channel_id=1, source_target_pairs={{0,3},{1,0},{2,1},{3,2},{4,7},{5,4},{6,5},{7,6},{8,11},{9,8},{10,9... | collective-permute-start | bytes 196616 | tf_op jit(solution)/shard_map/ppermute | solution.py:299
  87.5 6.0 %collective-permute-start.31 = (f32[4,32,128]{2,1,0:T(8,128)S(1)}, f32[4,32,128]{2,1,0:T(8,128)S(1)}, u32[]{:S(2)}, u32[]{:S(2)}) collective-permute-start(f32[4,32,128]{2,1,0:T(8,128)S(1)} %shard_map.96.refs_0_), channel_id=1, source_target_pairs={{0,1},{1,2},{2,3},{3,0},{4,5},{5,6},{6,7},{7,4},{8,9},{9,10},{10,1... | collective-permute-start | bytes 196616 | tf_op jit(solution)/shard_map/ppermute | solution.py:299
  87.6 6.6 %collective-permute-start.30 = (f32[4,32,128]{2,1,0:T(8,128)S(1)}, f32[4,32,128]{2,1,0:T(8,128)S(1)}, u32[]{:S(2)}, u32[]{:S(2)}) collective-permute-start(f32[4,32,128]{2,1,0:T(8,128)S(1)} %shard_map.95.refs_0_), channel_id=1, source_target_pairs={{0,2},{1,3},{2,0},{3,1},{4,6},{5,7},{6,4},{7,5},{8,10},{9,11},{10,... | collective-permute-start | bytes 196616 | tf_op jit(solution)/shard_map/ppermute | solution.py:299
  (3 other events, 15.0 us)

commit v7 on v4

--- a/solution.py
+++ b/solution.py
@@ -116,7 +116,9 @@
     head = HEAD
     room = table_ref.shape[1] - head - SPARE
 
-    turned = lax.rem(lax.div(rows, owned) + (parts - here), parts) * owned + lax.rem(rows, owned)
+    away = lax.rem(lax.div(rows, owned) + (parts - here), parts)
+    spot = sum(jnp.where(away == part, k, 0) for k, part in enumerate((*PART_ORDER, 0)))
+    turned = spot * owned + lax.rem(rows, owned)
     ids = iota((1, slots), 1)
     alive = ids < live
     hot = jnp.where((turned == iota((span, slots), 0)) & alive, 1.0, 0.0)
@@ -222,12 +224,12 @@
     )(place, sizes, after, blocks)
 
 
-def products_kernel(first_row, table, vec, store, *refs):
-    out, sums = refs[-2:]
-    owned = out.shape[0]
+def products_kernel(first_row, count_out, table, vec, store, *refs):
+    outs, sums = refs[-1 - count_out : -1], refs[-1]
+    owned = outs[0].shape[0]
     size = store.shape[1]
     start = lax.div(table[0, first_row - 1], GROUP) if first_row else 0
-    count = lax.div(table[0, first_row + owned - 1], GROUP) - start
+    count = lax.div(table[0, first_row + count_out * owned - 1], GROUP) - start
     sums[...] = jnp.zeros_like(sums)
 
     @pl.loop(0, lax.div(count + (BATCH - 1), BATCH))
@@ -238,17 +240,18 @@
             right = store[pl.ds(group * GROUP, GROUP)].reshape(GROUP * size, size)
             sums[table[0, LANES + group]] += jnp.dot(left, right, preferred_element_type=jnp.float32)
 
-    out[...] = sums[first_row : first_row + owned]
-
-
-def local_products(part, vec, prep, after, owned, parts):
+    for k, out in enumerate(outs):
+        out[...] = sums[first_row + k * owned : first_row + (k + 1) * owned]
+
+
+def local_products(spot, count, vec, prep, after, owned, parts):
     table, store = prep
     _, vecs, size = vec.shape
     return pl.pallas_call(
-        functools.partial(products_kernel, part * owned),
-        out_shape=jax.ShapeDtypeStruct((owned, vecs, size), jnp.float32),
+        functools.partial(products_kernel, spot * owned, count),
+        out_shape=[jax.ShapeDtypeStruct((owned, vecs, size), jnp.float32)] * count,
         in_specs=[SMEM] + [VMEM] * (2 + len(after)),
-        out_specs=VMEM,
+        out_specs=[VMEM] * count,
         scratch_shapes=[pltpu.VMEM((owned * parts + 1, vecs, size), jnp.float32)],
         compiler_params=pltpu.CompilerParams(vmem_limit_bytes=4 * MIB),
         cost_estimate=pl.CostEstimate(flops=640 // 2 * vecs * size * size, bytes_accessed=MIB, transcendentals=0),
@@ -288,13 +291,13 @@
 
     def image_pieces(vec):
         pieces, last = [], ()
-        for part in (*PART_ORDER, 0):
-            piece = local_products(part, vec, prep, last, owned, parts)
-            last = (piece,)
-            if part:
-                piece = lax.ppermute(piece, "col", [(i, (i + part) % parts) for i in range(parts)])
-            pieces.append(piece)
-        return pieces
+        for spot, aways in ((0, PART_ORDER[:1]), (1, PART_ORDER[1:]), (parts - 1, ())):
+            last = local_products(spot, max(1, len(aways)), vec, prep, last[:1], owned, parts)
+            if not aways:
+                pieces.append(last[0])
+            for away, piece in zip(aways, last):
+                pieces.append(lax.ppermute(piece, "col", [(i, (i + away) % parts) for i in range(parts)]))
+        return pieces[::-1]
 
     start_bf = rounded(start_vectors)
     place, table, *scalars = sort_plan(block_rows, block_cols, live_counts, scalars, start_bf, parts, owned)

time: 97.7 us -> 94.7 us (0.969)
  starting transfers between devices: 48.8 us -> 41.9 us
  waiting for transfers between devices: 36.7 us -> 40.4 us
    ppermute x9, starting transfers between devices: 21 us -> 14.7 us  [image_pieces(): lax.ppermute(piece, 'col', [(i, (i + away) % parts) for i in range(parts)])]
    ppermute x18, waiting for transfers between devices: 21.2 us -> 23.5 us  [shifted(): lax.ppermute(value, 'row', chip_shifts(stage, step))]
    ppermute x9, waiting for transfers between devices: 9.74 us -> 11.2 us  [image_pieces(): lax.ppermute(piece, 'col', [(i, (i + away) % parts) for i in range(parts)])]
    pallas_call x12 -> x9, Pallas kernels: 4.01 us -> 3.76 us  [local_products(): pl.pallas_call(functools.partial(products_kernel, spot * owned, count), o...]
  transfers between devices with their start and end apart: 30 -> 30, of which waited for: 23 -> 26; matrix products, arithmetic and copies ran while one was open for 0% -> 0% of each run, Pallas kernels for 6% -> 8%
where the time goes in v7:
time: 94.7 us; the launch traced here: 94 us
  starting transfers between devices  41.9 us (44%)
  waiting for transfers between devices  40.4 us (43%)
  Pallas kernels  8.62 us (9%)
  between operations  2.17 us (2%)
    ppermute x18, starting transfers between devices, shifted(): lax.ppermute(value, 'row', chip_shifts(stage, step))  27 us
    ppermute x18, waiting for transfers between devices, shifted(): lax.ppermute(value, 'row', chip_shifts(stage, step))  23.5 us
    ppermute x9, starting transfers between devices, image_pieces(): lax.ppermute(piece, 'col', [(i, (i + away) % parts) for i in range(parts)])  14.7 us
    ppermute x9, waiting for transfers between devices, image_pieces(): lax.ppermute(piece, 'col', [(i, (i + away) % parts) for i in range(parts)])  11.2 us
    ppermute x3, waiting for transfers between devices, all_gathered(): return joined([mine, lax.ppermute(mine, 'row', core_swap())])  5.69 us
    pallas_call x9, Pallas kernels, local_products(): pl.pallas_call(functools.partial(products_kernel, spot * owned, count), o...  3.76 us
    pallas_call x1, Pallas kernels, sort_plan(): pl.pallas_call(functools.partial(plan_kernel, parts, owned), out_shape=[p...  2.09 us
  transfers between devices with their start and end apart: 30, of which 26 were waited for; matrix products, arithmetic and copies ran while one was open for 0% of the time, Pallas kernels for 8%

profile of v7, /device:TPU:0, one launch (start us, length us, event | category | flops | bytes accessed | tf_op | source)
XLA Modules:
  0.0 94.0 jit_solution(6975408032282725418)
XLA Ops:
  0.8 3.3 %collective-permute-start.2 = (bf16[4,32,128]{2,1,0:T(8,128)(2,1)S(1)}, bf16[4,32,128]{2,1,0:T(8,128)(2,1)S(1)}, u32[]{:S(2)}, u32[]{:S(2)}) collective-permute-start(bf16[4,32,128]{2,1,0:T(8,128)(2,1)S(1)} %shard_map.73._after.refs_0_), channel_id=1, source_target_pairs={{0,16},{4,68},{8,24},{12,76},{16,0},{20,84},{24,8},{28,92},{32,48}... | collective-permute-start | bytes 98312 | tf_op jit(solution)/shard_map/ppermute | solution.py:79
  8.1 2.1 %shard_map.74 = (s32[1,640]{1,0:T(1,128)S(4)}, s32[1,1344]{1,0:T(1,128)S(4)}, f32[1]{0:T(128)S(4)}, f32[1]{0:T(128)S(4)}) custom-call(s32[1]{0:T(128)S(6)} %copy.8.live_ref, s32[640]{0:T(1024)} %rows_hbm.1, s32[640]{0:T(1024)} %cols_hbm.1, f32[]{:T(128)S(6)} %copy.9.center, f32[]{:T(128)S(6)} %copy.10.half_width, ...), custom_call_target="tpu_custom_call" | custom-call | flops 1000 | bytes 1000 | tf_op jit(solution)/shard_map/pallas_call | solution.py:171
  10.3 3.1 %collective-permute-start.5 = (bf16[16,32,128]{2,1,0:T(8,128)(2,1)S(1)}, bf16[16,32,128]{2,1,0:T(8,128)(2,1)S(1)}, u32[]{:S(2)}, u32[]{:S(2)}) collective-permute-start(bf16[16,32,128]{2,1,0:T(8,128)(2,1)S(1)} %shard_map.75._after.refs_0_), channel_id=1, source_target_pairs={{0,64},{4,20},{8,72},{12,28},{16,80},{20,4},{24,88},{28,12},{32,96... | collective-permute-start | bytes 393224 | tf_op jit(solution)/shard_map/ppermute | solution.py:79
  15.5 1.7 %shard_map.76.refs_4_.store = bf16[832,128,128]{2,1,0:T(8,128)(2,1)S(1)} custom-call(s32[1,640]{1,0:T(1,128)S(4)} %get-tuple-element.22.place, s32[1,1344]{1,0:T(1,128)S(4)} %get-tuple-element.21.refs_4_.sizes.table, bf16[16,32,128]{2,1,0:T(8,128)(2,1)S(1)} %shard_map.75._after.refs_0_, bf16[640,128,128]{2,1,0:T(8,128)(2,1)} %blocks_hbm.1), custom_call_target="tpu_custom_call" | custom-call | flops 1000 | bytes 20971520 | tf_op jit(solution)/shard_map/pallas_call | solution.py:213
  18.4 2.4 %collective-permute-done.3.refs_1_ = bf16[16,32,128]{2,1,0:T(8,128)(2,1)S(1)} collective-permute-done((bf16[16,32,128]{2,1,0:T(8,128)(2,1)S(1)}, bf16[16,32,128]{2,1,0:T(8,128)(2,1)S(1)}, u32[]{:S(2)}, u32[]{:S(2)}) %collective-permute-start.3) | collective-permute-done | bytes 131104 | tf_op jit(solution)/shard_map/ppermute | solution.py:79
  20.9 1.9 %collective-permute-done.6.refs_1_ = bf16[64,32,128]{2,1,0:T(8,128)(2,1)S(1)} collective-permute-done((bf16[64,32,128]{2,1,0:T(8,128)(2,1)S(1)}, bf16[64,32,128]{2,1,0:T(8,128)(2,1)S(1)}, u32[]{:S(2)}, u32[]{:S(2)}) %collective-permute-start.6) | collective-permute-done | bytes 524320 | tf_op jit(solution)/shard_map/ppermute | solution.py:88
  22.9 4.6 %collective-permute-start.9 = (f32[4,32,128]{2,1,0:T(8,128)S(1)}, f32[4,32,128]{2,1,0:T(8,128)S(1)}, u32[]{:S(2)}, u32[]{:S(2)}) collective-permute-start(f32[4,32,128]{2,1,0:T(8,128)S(1)} %shard_map.79.refs_0_), channel_id=1, source_target_pairs={{0,2},{1,3},{2,0},{3,1},{4,6},{5,7},{6,4},{7,5},{8,10},{9,11},{10,... | collective-permute-start | bytes 196616 | tf_op jit(solution)/shard_map/ppermute | solution.py:299
  28.9 1.3 %collective-permute-start.8 = (f32[4,32,128]{2,1,0:T(8,128)S(1)}, f32[4,32,128]{2,1,0:T(8,128)S(1)}, u32[]{:S(2)}, u32[]{:S(2)}) collective-permute-start(f32[4,32,128]{2,1,0:T(8,128)S(1)} %get-tuple-element.23.refs_0_), channel_id=1, source_target_pairs={{0,1},{1,2},{2,3},{3,0},{4,5},{5,6},{6,7},{7,4},{8,9},{9,10},{10,1... | collective-permute-start | bytes 196616 | tf_op jit(solution)/shard_map/ppermute | solution.py:299
  30.8 1.8 %collective-permute-done.7.refs_1_ = f32[4,32,128]{2,1,0:T(8,128)S(1)} collective-permute-done((f32[4,32,128]{2,1,0:T(8,128)S(1)}, f32[4,32,128]{2,1,0:T(8,128)S(1)}, u32[]{:S(2)}, u32[]{:S(2)}) %collective-permute-start.7) | collective-permute-done | bytes 65568 | tf_op jit(solution)/shard_map/ppermute | solution.py:299
  32.6 1.7 %collective-permute-done.8.refs_2_ = f32[4,32,128]{2,1,0:T(8,128)S(1)} collective-permute-done((f32[4,32,128]{2,1,0:T(8,128)S(1)}, f32[4,32,128]{2,1,0:T(8,128)S(1)}, u32[]{:S(2)}, u32[]{:S(2)}) %collective-permute-start.8) | collective-permute-done | bytes 65568 | tf_op jit(solution)/shard_map/ppermute | solution.py:299
  35.1 3.2 %collective-permute-start.11 = (bf16[4,32,128]{2,1,0:T(8,128)(2,1)S(1)}, bf16[4,32,128]{2,1,0:T(8,128)(2,1)S(1)}, u32[]{:S(2)}, u32[]{:S(2)}) collective-permute-start(bf16[4,32,128]{2,1,0:T(8,128)(2,1)S(1)} %get-tuple-element.26.refs_0_), channel_id=1, source_target_pairs={{0,24},{4,100},{8,0},{12,108},{16,8},{20,116},{24,16},{28,124},{32... | collective-permute-start | bytes 98312 | tf_op jit(solution)/shard_map/ppermute | solution.py:79
  38.4 1.5 %collective-permute-done.12.refs_3_ = bf16[4,32,128]{2,1,0:T(8,128)(2,1)S(1)} collective-permute-done((bf16[4,32,128]{2,1,0:T(8,128)(2,1)S(1)}, bf16[4,32,128]{2,1,0:T(8,128)(2,1)S(1)}, u32[]{:S(2)}, u32[]{:S(2)}) %collective-permute-start.12) | collective-permute-done | bytes 32800 | tf_op jit(solution)/shard_map/ppermute | solution.py:79
  40.6 2.9 %collective-permute-done.10.refs_1_ = bf16[4,32,128]{2,1,0:T(8,128)(2,1)S(1)} collective-permute-done((bf16[4,32,128]{2,1,0:T(8,128)(2,1)S(1)}, bf16[4,32,128]{2,1,0:T(8,128)(2,1)S(1)}, u32[]{:S(2)}, u32[]{:S(2)}) %collective-permute-start.10) | collective-permute-done | bytes 32800 | tf_op jit(solution)/shard_map/ppermute | solution.py:79
  43.5 2.4 %collective-permute-start.15 = (bf16[16,32,128]{2,1,0:T(8,128)(2,1)S(1)}, bf16[16,32,128]{2,1,0:T(8,128)(2,1)S(1)}, u32[]{:S(2)}, u32[]{:S(2)}) collective-permute-start(bf16[16,32,128]{2,1,0:T(8,128)(2,1)S(1)} %shard_map.83.refs_0_), channel_id=1, source_target_pairs={{0,64},{4,20},{8,72},{12,28},{16,80},{20,4},{24,88},{28,12},{32,96... | collective-permute-start | bytes 393224 | tf_op jit(solution)/shard_map/ppermute | solution.py:79
  45.9 1.9 %collective-permute-start.14 = (bf16[16,32,128]{2,1,0:T(8,128)(2,1)S(1)}, bf16[16,32,128]{2,1,0:T(8,128)(2,1)S(1)}, u32[]{:S(2)}, u32[]{:S(2)}) collective-permute-start(bf16[16,32,128]{2,1,0:T(8,128)(2,1)S(1)} %shard_map.83.refs_0_), channel_id=1, source_target_pairs={{0,96},{4,28},{8,104},{12,4},{16,112},{20,12},{24,120},{28,20},{32... | collective-permute-start | bytes 393224 | tf_op jit(solution)/shard_map/ppermute | solution.py:79
  48.5 1.5 %collective-permute-done.15.refs_3_ = bf16[16,32,128]{2,1,0:T(8,128)(2,1)S(1)} collective-permute-done((bf16[16,32,128]{2,1,0:T(8,128)(2,1)S(1)}, bf16[16,32,128]{2,1,0:T(8,128)(2,1)S(1)}, u32[]{:S(2)}, u32[]{:S(2)}) %collective-permute-start.15) | collective-permute-done | bytes 131104 | tf_op jit(solution)/shard_map/ppermute | solution.py:79
  50.0 2.9 %collective-permute-done.14.refs_2_ = bf16[16,32,128]{2,1,0:T(8,128)(2,1)S(1)} collective-permute-done((bf16[16,32,128]{2,1,0:T(8,128)(2,1)S(1)}, bf16[16,32,128]{2,1,0:T(8,128)(2,1)S(1)}, u32[]{:S(2)}, u32[]{:S(2)}) %collective-permute-start.14) | collective-permute-done | bytes 131104 | tf_op jit(solution)/shard_map/ppermute | solution.py:79
  54.0 1.9 %collective-permute-done.16.refs_1_ = bf16[64,32,128]{2,1,0:T(8,128)(2,1)S(1)} collective-permute-done((bf16[64,32,128]{2,1,0:T(8,128)(2,1)S(1)}, bf16[64,32,128]{2,1,0:T(8,128)(2,1)S(1)}, u32[]{:S(2)}, u32[]{:S(2)}) %collective-permute-start.16) | collective-permute-done | bytes 524320 | tf_op jit(solution)/shard_map/ppermute | solution.py:88
  56.0 1.8 %collective-permute-start.19 = (f32[4,32,128]{2,1,0:T(8,128)S(1)}, f32[4,32,128]{2,1,0:T(8,128)S(1)}, u32[]{:S(2)}, u32[]{:S(2)}) collective-permute-start(f32[4,32,128]{2,1,0:T(8,128)S(1)} %shard_map.86.refs_0_), channel_id=1, source_target_pairs={{0,2},{1,3},{2,0},{3,1},{4,6},{5,7},{6,4},{7,5},{8,10},{9,11},{10,... | collective-permute-start | bytes 196616 | tf_op jit(solution)/shard_map/ppermute | solution.py:299
  58.4 1.8 %collective-permute-start.17 = (f32[4,32,128]{2,1,0:T(8,128)S(1)}, f32[4,32,128]{2,1,0:T(8,128)S(1)}, u32[]{:S(2)}, u32[]{:S(2)}) collective-permute-start(f32[4,32,128]{2,1,0:T(8,128)S(1)} %get-tuple-element.28), channel_id=1, source_target_pairs={{0,3},{1,0},{2,1},{3,2},{4,7},{5,4},{6,5},{7,6},{8,11},{9,8},{10,9... | collective-permute-start | bytes 196616 | tf_op jit(solution)/shard_map/ppermute | solution.py:299
  63.0 2.8 %collective-permute-done.18.refs_2_ = f32[4,32,128]{2,1,0:T(8,128)S(1)} collective-permute-done((f32[4,32,128]{2,1,0:T(8,128)S(1)}, f32[4,32,128]{2,1,0:T(8,128)S(1)}, u32[]{:S(2)}, u32[]{:S(2)}) %collective-permute-start.18) | collective-permute-done | bytes 65568 | tf_op jit(solution)/shard_map/ppermute | solution.py:299
  65.8 1.7 %collective-permute-start.22 = (bf16[4,32,128]{2,1,0:T(8,128)(2,1)S(1)}, bf16[4,32,128]{2,1,0:T(8,128)(2,1)S(1)}, u32[]{:S(2)}, u32[]{:S(2)}) collective-permute-start(bf16[4,32,128]{2,1,0:T(8,128)(2,1)S(1)} %get-tuple-element.30.refs_0_), channel_id=1, source_target_pairs={{0,16},{4,68},{8,24},{12,76},{16,0},{20,84},{24,8},{28,92},{32,48}... | collective-permute-start | bytes 98312 | tf_op jit(solution)/shard_map/ppermute | solution.py:79
  69.5 1.7 %collective-permute-done.22.refs_3_ = bf16[4,32,128]{2,1,0:T(8,128)(2,1)S(1)} collective-permute-done((bf16[4,32,128]{2,1,0:T(8,128)(2,1)S(1)}, bf16[4,32,128]{2,1,0:T(8,128)(2,1)S(1)}, u32[]{:S(2)}, u32[]{:S(2)}) %collective-permute-start.22) | collective-permute-done | bytes 32800 | tf_op jit(solution)/shard_map/ppermute | solution.py:79
  71.4 2.0 %collective-permute-done.20.refs_1_ = bf16[4,32,128]{2,1,0:T(8,128)(2,1)S(1)} collective-permute-done((bf16[4,32,128]{2,1,0:T(8,128)(2,1)S(1)}, bf16[4,32,128]{2,1,0:T(8,128)(2,1)S(1)}, u32[]{:S(2)}, u32[]{:S(2)}) %collective-permute-start.20) | collective-permute-done | bytes 32800 | tf_op jit(solution)/shard_map/ppermute | solution.py:79
  73.4 1.8 %collective-permute-start.25 = (bf16[16,32,128]{2,1,0:T(8,128)(2,1)S(1)}, bf16[16,32,128]{2,1,0:T(8,128)(2,1)S(1)}, u32[]{:S(2)}, u32[]{:S(2)}) collective-permute-start(bf16[16,32,128]{2,1,0:T(8,128)(2,1)S(1)} %shard_map.90.refs_0_), channel_id=1, source_target_pairs={{0,64},{4,20},{8,72},{12,28},{16,80},{20,4},{24,88},{28,12},{32,96... | collective-permute-start | bytes 393224 | tf_op jit(solution)/shard_map/ppermute | solution.py:79
  75.2 1.3 %collective-permute-start.24 = (bf16[16,32,128]{2,1,0:T(8,128)(2,1)S(1)}, bf16[16,32,128]{2,1,0:T(8,128)(2,1)S(1)}, u32[]{:S(2)}, u32[]{:S(2)}) collective-permute-start(bf16[16,32,128]{2,1,0:T(8,128)(2,1)S(1)} %shard_map.90.refs_0_), channel_id=1, source_target_pairs={{0,96},{4,28},{8,104},{12,4},{16,112},{20,12},{24,120},{28,20},{32... | collective-permute-start | bytes 393224 | tf_op jit(solution)/shard_map/ppermute | solution.py:79
  77.2 2.8 %collective-permute-done.25.refs_3_ = bf16[16,32,128]{2,1,0:T(8,128)(2,1)S(1)} collective-permute-done((bf16[16,32,128]{2,1,0:T(8,128)(2,1)S(1)}, bf16[16,32,128]{2,1,0:T(8,128)(2,1)S(1)}, u32[]{:S(2)}, u32[]{:S(2)}) %collective-permute-start.25) | collective-permute-done | bytes 131104 | tf_op jit(solution)/shard_map/ppermute | solution.py:79
  80.1 2.5 %collective-permute-done.23.refs_1_ = bf16[16,32,128]{2,1,0:T(8,128)(2,1)S(1)} collective-permute-done((bf16[16,32,128]{2,1,0:T(8,128)(2,1)S(1)}, bf16[16,32,128]{2,1,0:T(8,128)(2,1)S(1)}, u32[]{:S(2)}, u32[]{:S(2)}) %collective-permute-start.23) | collective-permute-done | bytes 131104 | tf_op jit(solution)/shard_map/ppermute | solution.py:79
  82.8 1.9 %collective-permute-done.26.refs_1_ = bf16[64,32,128]{2,1,0:T(8,128)(2,1)S(1)} collective-permute-done((bf16[64,32,128]{2,1,0:T(8,128)(2,1)S(1)}, bf16[64,32,128]{2,1,0:T(8,128)(2,1)S(1)}, u32[]{:S(2)}, u32[]{:S(2)}) %collective-permute-start.26) | collective-permute-done | bytes 524320 | tf_op jit(solution)/shard_map/ppermute | solution.py:88
  84.8 2.0 %collective-permute-start.29 = (f32[4,32,128]{2,1,0:T(8,128)S(1)}, f32[4,32,128]{2,1,0:T(8,128)S(1)}, u32[]{:S(2)}, u32[]{:S(2)}) collective-permute-start(f32[4,32,128]{2,1,0:T(8,128)S(1)} %shard_map.93.refs_0_), channel_id=1, source_target_pairs={{0,2},{1,3},{2,0},{3,1},{4,6},{5,7},{6,4},{7,5},{8,10},{9,11},{10,... | collective-permute-start | bytes 196616 | tf_op jit(solution)/shard_map/ppermute | solution.py:299
  87.8 1.8 %collective-permute-start.28 = (f32[4,32,128]{2,1,0:T(8,128)S(1)}, f32[4,32,128]{2,1,0:T(8,128)S(1)}, u32[]{:S(2)}, u32[]{:S(2)}) collective-permute-start(f32[4,32,128]{2,1,0:T(8,128)S(1)} %get-tuple-element.31.refs_0_), channel_id=1, source_target_pairs={{0,1},{1,2},{2,3},{3,0},{4,5},{5,6},{6,7},{7,4},{8,9},{9,10},{10,1... | collective-permute-start | bytes 196616 | tf_op jit(solution)/shard_map/ppermute | solution.py:299
  92.0 1.3 %collective-permute-done.28.refs_2_ = f32[4,32,128]{2,1,0:T(8,128)S(1)} collective-permute-done((f32[4,32,128]{2,1,0:T(8,128)S(1)}, f32[4,32,128]{2,1,0:T(8,128)S(1)}, u32[]{:S(2)}, u32[]{:S(2)}) %collective-permute-start.28) | collective-permute-done | bytes 65568 | tf_op jit(solution)/shard_map/ppermute | solution.py:299
  (56 shorter events, 22.5 us)
Async XLA Ops:
  0.0 0.8 copy-start
  0.8 9.4 %collective-permute-start.2 = (bf16[4,32,128]{2,1,0:T(8,128)(2,1)S(1)}, bf16[4,32,128]{2,1,0:T(8,128)(2,1)S(1)}, u32[]{:S(2)}, u32[]{:S(2)}) collective-permute-start(bf16[4,32,128]{2,1,0:T(8,128)(2,1)S(1)} %shard_map.73._after.refs_0_), channel_id=1, source_target_pairs={{0,16},{4,68},{8,24},{12,76},{16,0},{20,84},{24,8},{28,92},{32,48}... | collective-permute-start | bytes 98312 | tf_op jit(solution)/shard_map/ppermute | solution.py:79
  4.2 6.1 %collective-permute-start.1 = (bf16[4,32,128]{2,1,0:T(8,128)(2,1)S(1)}, bf16[4,32,128]{2,1,0:T(8,128)(2,1)S(1)}, u32[]{:S(2)}, u32[]{:S(2)}) collective-permute-start(bf16[4,32,128]{2,1,0:T(8,128)(2,1)S(1)} %shard_map.73._after.refs_0_), channel_id=1, source_target_pairs={{0,24},{4,100},{8,0},{12,108},{16,8},{20,116},{24,16},{28,124},{32... | collective-permute-start | bytes 98312 | tf_op jit(solution)/shard_map/ppermute | solution.py:79
  5.2 5.1 %collective-permute-start = (bf16[4,32,128]{2,1,0:T(8,128)(2,1)S(1)}, bf16[4,32,128]{2,1,0:T(8,128)(2,1)S(1)}, u32[]{:S(2)}, u32[]{:S(2)}) collective-permute-start(bf16[4,32,128]{2,1,0:T(8,128)(2,1)S(1)} %shard_map.73._after.refs_0_), channel_id=1, source_target_pairs={{0,8},{4,36},{8,16},{12,44},{16,24},{20,52},{24,0},{28,60},{32,40}... | collective-permute-start | bytes 98312 | tf_op jit(solution)/shard_map/ppermute | solution.py:79
  10.3 6.9 %collective-permute-start.5 = (bf16[16,32,128]{2,1,0:T(8,128)(2,1)S(1)}, bf16[16,32,128]{2,1,0:T(8,128)(2,1)S(1)}, u32[]{:S(2)}, u32[]{:S(2)}) collective-permute-start(bf16[16,32,128]{2,1,0:T(8,128)(2,1)S(1)} %shard_map.75._after.refs_0_), channel_id=1, source_target_pairs={{0,64},{4,20},{8,72},{12,28},{16,80},{20,4},{24,88},{28,12},{32,96... | collective-permute-start | bytes 393224 | tf_op jit(solution)/shard_map/ppermute | solution.py:79
  13.5 5.0 %collective-permute-start.4 = (bf16[16,32,128]{2,1,0:T(8,128)(2,1)S(1)}, bf16[16,32,128]{2,1,0:T(8,128)(2,1)S(1)}, u32[]{:S(2)}, u32[]{:S(2)}) collective-permute-start(bf16[16,32,128]{2,1,0:T(8,128)(2,1)S(1)} %shard_map.75._after.refs_0_), channel_id=1, source_target_pairs={{0,96},{4,28},{8,104},{12,4},{16,112},{20,12},{24,120},{28,20},{32... | collective-permute-start | bytes 393224 | tf_op jit(solution)/shard_map/ppermute | solution.py:79
  14.6 6.2 %collective-permute-start.3 = (bf16[16,32,128]{2,1,0:T(8,128)(2,1)S(1)}, bf16[16,32,128]{2,1,0:T(8,128)(2,1)S(1)}, u32[]{:S(2)}, u32[]{:S(2)}) collective-permute-start(bf16[16,32,128]{2,1,0:T(8,128)(2,1)S(1)} %shard_map.75._after.refs_0_), channel_id=1, source_target_pairs={{0,32},{4,12},{8,40},{12,20},{16,48},{20,28},{24,56},{28,4},{32,64... | collective-permute-start | bytes 393224 | tf_op jit(solution)/shard_map/ppermute | solution.py:79
  20.8 2.0 %collective-permute-start.6 = (bf16[64,32,128]{2,1,0:T(8,128)(2,1)S(1)}, bf16[64,32,128]{2,1,0:T(8,128)(2,1)S(1)}, u32[]{:S(2)}, u32[]{:S(2)}) collective-permute-start(bf16[64,32,128]{2,1,0:T(8,128)(2,1)S(1)} %shard_map.77.refs_0_), channel_id=1, source_target_pairs={{0,4},{4,0},{8,12},{12,8},{16,20},{20,16},{24,28},{28,24},{32,36},... | collective-permute-start | bytes 1572872 | tf_op jit(solution)/shard_map/ppermute | solution.py:88
  22.9 11.4 %copy-start.1 = (f32[4,32,128]{2,1,0:T(8,128)S(1)}, f32[4,32,128]{2,1,0:T(8,128)}, u32[]{:S(2)}) copy-start(f32[4,32,128]{2,1,0:T(8,128)} %previous.1) | copy-start | bytes 196612
  22.9 7.9 %collective-permute-start.9 = (f32[4,32,128]{2,1,0:T(8,128)S(1)}, f32[4,32,128]{2,1,0:T(8,128)S(1)}, u32[]{:S(2)}, u32[]{:S(2)}) collective-permute-start(f32[4,32,128]{2,1,0:T(8,128)S(1)} %shard_map.79.refs_0_), channel_id=1, source_target_pairs={{0,2},{1,3},{2,0},{3,1},{4,6},{5,7},{6,4},{7,5},{8,10},{9,11},{10,... | collective-permute-start | bytes 196616 | tf_op jit(solution)/shard_map/ppermute | solution.py:299
  28.1 4.5 %collective-permute-start.7 = (f32[4,32,128]{2,1,0:T(8,128)S(1)}, f32[4,32,128]{2,1,0:T(8,128)S(1)}, u32[]{:S(2)}, u32[]{:S(2)}) collective-permute-start(f32[4,32,128]{2,1,0:T(8,128)S(1)} %get-tuple-element.24), channel_id=1, source_target_pairs={{0,3},{1,0},{2,1},{3,2},{4,7},{5,4},{6,5},{7,6},{8,11},{9,8},{10,9... | collective-permute-start | bytes 196616 | tf_op jit(solution)/shard_map/ppermute | solution.py:299
  28.9 5.5 %collective-permute-start.8 = (f32[4,32,128]{2,1,0:T(8,128)S(1)}, f32[4,32,128]{2,1,0:T(8,128)S(1)}, u32[]{:S(2)}, u32[]{:S(2)}) collective-permute-start(f32[4,32,128]{2,1,0:T(8,128)S(1)} %get-tuple-element.23.refs_0_), channel_id=1, source_target_pairs={{0,1},{1,2},{2,3},{3,0},{4,5},{5,6},{6,7},{7,4},{8,9},{9,10},{10,1... | collective-permute-start | bytes 196616 | tf_op jit(solution)/shard_map/ppermute | solution.py:299
  34.4 5.5 %collective-permute-start.12 = (bf16[4,32,128]{2,1,0:T(8,128)(2,1)S(1)}, bf16[4,32,128]{2,1,0:T(8,128)(2,1)S(1)}, u32[]{:S(2)}, u32[]{:S(2)}) collective-permute-start(bf16[4,32,128]{2,1,0:T(8,128)(2,1)S(1)} %get-tuple-element.26.refs_0_), channel_id=1, source_target_pairs={{0,16},{4,68},{8,24},{12,76},{16,0},{20,84},{24,8},{28,92},{32,48}... | collective-permute-start | bytes 98312 | tf_op jit(solution)/shard_map/ppermute | solution.py:79
  35.1 5.5 %collective-permute-start.11 = (bf16[4,32,128]{2,1,0:T(8,128)(2,1)S(1)}, bf16[4,32,128]{2,1,0:T(8,128)(2,1)S(1)}, u32[]{:S(2)}, u32[]{:S(2)}) collective-permute-start(bf16[4,32,128]{2,1,0:T(8,128)(2,1)S(1)} %get-tuple-element.26.refs_0_), channel_id=1, source_target_pairs={{0,24},{4,100},{8,0},{12,108},{16,8},{20,116},{24,16},{28,124},{32... | collective-permute-start | bytes 98312 | tf_op jit(solution)/shard_map/ppermute | solution.py:79
  38.3 5.1 %collective-permute-start.10 = (bf16[4,32,128]{2,1,0:T(8,128)(2,1)S(1)}, bf16[4,32,128]{2,1,0:T(8,128)(2,1)S(1)}, u32[]{:S(2)}, u32[]{:S(2)}) collective-permute-start(bf16[4,32,128]{2,1,0:T(8,128)(2,1)S(1)} %get-tuple-element.26.refs_0_), channel_id=1, source_target_pairs={{0,8},{4,36},{8,16},{12,44},{16,24},{20,52},{24,0},{28,60},{32,40}... | collective-permute-start | bytes 98312 | tf_op jit(solution)/shard_map/ppermute | solution.py:79
  43.5 6.6 %collective-permute-start.15 = (bf16[16,32,128]{2,1,0:T(8,128)(2,1)S(1)}, bf16[16,32,128]{2,1,0:T(8,128)(2,1)S(1)}, u32[]{:S(2)}, u32[]{:S(2)}) collective-permute-start(bf16[16,32,128]{2,1,0:T(8,128)(2,1)S(1)} %shard_map.83.refs_0_), channel_id=1, source_target_pairs={{0,64},{4,20},{8,72},{12,28},{16,80},{20,4},{24,88},{28,12},{32,96... | collective-permute-start | bytes 393224 | tf_op jit(solution)/shard_map/ppermute | solution.py:79
  45.9 7.0 %collective-permute-start.14 = (bf16[16,32,128]{2,1,0:T(8,128)(2,1)S(1)}, bf16[16,32,128]{2,1,0:T(8,128)(2,1)S(1)}, u32[]{:S(2)}, u32[]{:S(2)}) collective-permute-start(bf16[16,32,128]{2,1,0:T(8,128)(2,1)S(1)} %shard_map.83.refs_0_), channel_id=1, source_target_pairs={{0,96},{4,28},{8,104},{12,4},{16,112},{20,12},{24,120},{28,20},{32... | collective-permute-start | bytes 393224 | tf_op jit(solution)/shard_map/ppermute | solution.py:79
  47.7 6.2 %collective-permute-start.13 = (bf16[16,32,128]{2,1,0:T(8,128)(2,1)S(1)}, bf16[16,32,128]{2,1,0:T(8,128)(2,1)S(1)}, u32[]{:S(2)}, u32[]{:S(2)}) collective-permute-start(bf16[16,32,128]{2,1,0:T(8,128)(2,1)S(1)} %shard_map.83.refs_0_), channel_id=1, source_target_pairs={{0,32},{4,12},{8,40},{12,20},{16,48},{20,28},{24,56},{28,4},{32,64... | collective-permute-start | bytes 393224 | tf_op jit(solution)/shard_map/ppermute | solution.py:79
  53.9 2.0 %collective-permute-start.16 = (bf16[64,32,128]{2,1,0:T(8,128)(2,1)S(1)}, bf16[64,32,128]{2,1,0:T(8,128)(2,1)S(1)}, u32[]{:S(2)}, u32[]{:S(2)}) collective-permute-start(bf16[64,32,128]{2,1,0:T(8,128)(2,1)S(1)} %shard_map.84.refs_0_), channel_id=1, source_target_pairs={{0,4},{4,0},{8,12},{12,8},{16,20},{20,16},{24,28},{28,24},{32,36},... | collective-permute-start | bytes 1572872 | tf_op jit(solution)/shard_map/ppermute | solution.py:88
  56.0 6.3 %collective-permute-start.19 = (f32[4,32,128]{2,1,0:T(8,128)S(1)}, f32[4,32,128]{2,1,0:T(8,128)S(1)}, u32[]{:S(2)}, u32[]{:S(2)}) collective-permute-start(f32[4,32,128]{2,1,0:T(8,128)S(1)} %shard_map.86.refs_0_), channel_id=1, source_target_pairs={{0,2},{1,3},{2,0},{3,1},{4,6},{5,7},{6,4},{7,5},{8,10},{9,11},{10,... | collective-permute-start | bytes 196616 | tf_op jit(solution)/shard_map/ppermute | solution.py:299
  58.4 4.5 %collective-permute-start.17 = (f32[4,32,128]{2,1,0:T(8,128)S(1)}, f32[4,32,128]{2,1,0:T(8,128)S(1)}, u32[]{:S(2)}, u32[]{:S(2)}) collective-permute-start(f32[4,32,128]{2,1,0:T(8,128)S(1)} %get-tuple-element.28), channel_id=1, source_target_pairs={{0,3},{1,0},{2,1},{3,2},{4,7},{5,4},{6,5},{7,6},{8,11},{9,8},{10,9... | collective-permute-start | bytes 196616 | tf_op jit(solution)/shard_map/ppermute | solution.py:299
  60.2 5.5 %collective-permute-start.18 = (f32[4,32,128]{2,1,0:T(8,128)S(1)}, f32[4,32,128]{2,1,0:T(8,128)S(1)}, u32[]{:S(2)}, u32[]{:S(2)}) collective-permute-start(f32[4,32,128]{2,1,0:T(8,128)S(1)} %get-tuple-element.27.refs_0_), channel_id=1, source_target_pairs={{0,1},{1,2},{2,3},{3,0},{4,5},{5,6},{6,7},{7,4},{8,9},{9,10},{10,1... | collective-permute-start | bytes 196616 | tf_op jit(solution)/shard_map/ppermute | solution.py:299
  65.8 5.5 %collective-permute-start.22 = (bf16[4,32,128]{2,1,0:T(8,128)(2,1)S(1)}, bf16[4,32,128]{2,1,0:T(8,128)(2,1)S(1)}, u32[]{:S(2)}, u32[]{:S(2)}) collective-permute-start(bf16[4,32,128]{2,1,0:T(8,128)(2,1)S(1)} %get-tuple-element.30.refs_0_), channel_id=1, source_target_pairs={{0,16},{4,68},{8,24},{12,76},{16,0},{20,84},{24,8},{28,92},{32,48}... | collective-permute-start | bytes 98312 | tf_op jit(solution)/shard_map/ppermute | solution.py:79
  67.5 3.9 %collective-permute-start.21 = (bf16[4,32,128]{2,1,0:T(8,128)(2,1)S(1)}, bf16[4,32,128]{2,1,0:T(8,128)(2,1)S(1)}, u32[]{:S(2)}, u32[]{:S(2)}) collective-permute-start(bf16[4,32,128]{2,1,0:T(8,128)(2,1)S(1)} %get-tuple-element.30.refs_0_), channel_id=1, source_target_pairs={{0,24},{4,100},{8,0},{12,108},{16,8},{20,116},{24,16},{28,124},{32... | collective-permute-start | bytes 98312 | tf_op jit(solution)/shard_map/ppermute | solution.py:79
  68.3 5.1 %collective-permute-start.20 = (bf16[4,32,128]{2,1,0:T(8,128)(2,1)S(1)}, bf16[4,32,128]{2,1,0:T(8,128)(2,1)S(1)}, u32[]{:S(2)}, u32[]{:S(2)}) collective-permute-start(bf16[4,32,128]{2,1,0:T(8,128)(2,1)S(1)} %get-tuple-element.30.refs_0_), channel_id=1, source_target_pairs={{0,8},{4,36},{8,16},{12,44},{16,24},{20,52},{24,0},{28,60},{32,40}... | collective-permute-start | bytes 98312 | tf_op jit(solution)/shard_map/ppermute | solution.py:79
  73.4 6.6 %collective-permute-start.25 = (bf16[16,32,128]{2,1,0:T(8,128)(2,1)S(1)}, bf16[16,32,128]{2,1,0:T(8,128)(2,1)S(1)}, u32[]{:S(2)}, u32[]{:S(2)}) collective-permute-start(bf16[16,32,128]{2,1,0:T(8,128)(2,1)S(1)} %shard_map.90.refs_0_), channel_id=1, source_target_pairs={{0,64},{4,20},{8,72},{12,28},{16,80},{20,4},{24,88},{28,12},{32,96... | collective-permute-start | bytes 393224 | tf_op jit(solution)/shard_map/ppermute | solution.py:79
  75.2 5.0 %collective-permute-start.24 = (bf16[16,32,128]{2,1,0:T(8,128)(2,1)S(1)}, bf16[16,32,128]{2,1,0:T(8,128)(2,1)S(1)}, u32[]{:S(2)}, u32[]{:S(2)}) collective-permute-start(bf16[16,32,128]{2,1,0:T(8,128)(2,1)S(1)} %shard_map.90.refs_0_), channel_id=1, source_target_pairs={{0,96},{4,28},{8,104},{12,4},{16,112},{20,12},{24,120},{28,20},{32... | collective-permute-start | bytes 393224 | tf_op jit(solution)/shard_map/ppermute | solution.py:79
  76.5 6.2 %collective-permute-start.23 = (bf16[16,32,128]{2,1,0:T(8,128)(2,1)S(1)}, bf16[16,32,128]{2,1,0:T(8,128)(2,1)S(1)}, u32[]{:S(2)}, u32[]{:S(2)}) collective-permute-start(bf16[16,32,128]{2,1,0:T(8,128)(2,1)S(1)} %shard_map.90.refs_0_), channel_id=1, source_target_pairs={{0,32},{4,12},{8,40},{12,20},{16,48},{20,28},{24,56},{28,4},{32,64... | collective-permute-start | bytes 393224 | tf_op jit(solution)/shard_map/ppermute | solution.py:79
  82.7 2.0 %collective-permute-start.26 = (bf16[64,32,128]{2,1,0:T(8,128)(2,1)S(1)}, bf16[64,32,128]{2,1,0:T(8,128)(2,1)S(1)}, u32[]{:S(2)}, u32[]{:S(2)}) collective-permute-start(bf16[64,32,128]{2,1,0:T(8,128)(2,1)S(1)} %shard_map.91.refs_0_), channel_id=1, source_target_pairs={{0,4},{4,0},{8,12},{12,8},{16,20},{20,16},{24,28},{28,24},{32,36},... | collective-permute-start | bytes 1572872 | tf_op jit(solution)/shard_map/ppermute | solution.py:88
  84.8 6.3 %collective-permute-start.29 = (f32[4,32,128]{2,1,0:T(8,128)S(1)}, f32[4,32,128]{2,1,0:T(8,128)S(1)}, u32[]{:S(2)}, u32[]{:S(2)}) collective-permute-start(f32[4,32,128]{2,1,0:T(8,128)S(1)} %shard_map.93.refs_0_), channel_id=1, source_target_pairs={{0,2},{1,3},{2,0},{3,1},{4,6},{5,7},{6,4},{7,5},{8,10},{9,11},{10,... | collective-permute-start | bytes 196616 | tf_op jit(solution)/shard_map/ppermute | solution.py:299
  87.5 4.5 %collective-permute-start.27 = (f32[4,32,128]{2,1,0:T(8,128)S(1)}, f32[4,32,128]{2,1,0:T(8,128)S(1)}, u32[]{:S(2)}, u32[]{:S(2)}) collective-permute-start(f32[4,32,128]{2,1,0:T(8,128)S(1)} %get-tuple-element.32), channel_id=1, source_target_pairs={{0,3},{1,0},{2,1},{3,2},{4,7},{5,4},{6,5},{7,6},{8,11},{9,8},{10,9... | collective-permute-start | bytes 196616 | tf_op jit(solution)/shard_map/ppermute | solution.py:299
  87.8 5.5 %collective-permute-start.28 = (f32[4,32,128]{2,1,0:T(8,128)S(1)}, f32[4,32,128]{2,1,0:T(8,128)S(1)}, u32[]{:S(2)}, u32[]{:S(2)}) collective-permute-start(f32[4,32,128]{2,1,0:T(8,128)S(1)} %get-tuple-element.31.refs_0_), channel_id=1, source_target_pairs={{0,1},{1,2},{2,3},{3,0},{4,5},{5,6},{6,7},{7,4},{8,9},{9,10},{10,1... | collective-permute-start | bytes 196616 | tf_op jit(solution)/shard_map/ppermute | solution.py:299
